TPU v7x, 32 devices: a whole 2x2x4 slice. The times are simulated.
32 devices in a mesh: px: 8 (over z, y), py: 4 (over x, core).
Axes of the slice: x: 2, y: 2, z: 4, core: 2. Of those that a mesh axis runs over, the one named last changes fastest.
Arguments:
- point_channel_values: bfloat16 [4096, 64, 128], P(('px', 'py')), may hold values from -6 to 6
- point_offsets: bfloat16 [4096, 3, 128], P(('px', 'py')), may hold values from -1 to 17
- point_counts: int32 [4096], P(('px', 'py')), may hold values from 1 to 128
- block_bricks: int32 [4096, 4], P(('px', 'py')), may hold values from 0 to 16383, as said below
- spectral_weights: bfloat16 [2, 32, 32, 32, 64, 128], P(None, None, 'px', 'py'), may hold values from -0.5 to 0.5
- skip_weights: bfloat16 [2, 64, 64], replicated, may hold values from -0.75 to 0.75
- skip_bias: float32 [2, 64], replicated, may hold values from -3 to 3
Outputs:
- decoded: bfloat16 [4096, 64, 128], P(('px', 'py'))
Inputs may be any that keep to these rules, and one draw needn't show every extreme that they name: `block_bricks`: the 4 bricks of a block are distinct and lie on one device. Among the 128 blocks of one device at most 8 have their bricks on any one device, and in every draw some device receives exactly 8 blocks from every device.
All inputs are finite; a program needn't handle non-finite values.
Results may differ from a plain program's by a relative error of at most 0.0075.
Values may be sent and summed in bfloat16 or wider, within the bound.
A program may use at most 256 MiB of HBM per device.

v0:
```python
import math

import jax
import jax.numpy as jnp
from jax import lax
from jax.sharding import PartitionSpec as P

MODES = 32
NX = 128
NY = 128
NZ = 128
LAYERS = 2


AMPLITUDE = 0.25
SPREAD = 4.5
DECODE_SCALE = 0.1
PRECISE = lax.Precision.HIGHEST


def wave_numbers(kept_modes):
    position = jnp.arange(kept_modes, dtype=jnp.int32)
    return jnp.where(position < kept_modes // 2, position, position - kept_modes)


def forward_matrix(length, frequency):
    places = jnp.arange(length, dtype=jnp.int32)
    products = jnp.remainder(places[:, None] * frequency[None, :], length)
    angles = 2.0 * math.pi / length * products.astype(jnp.float32)
    cosine = jnp.cos(angles) / math.sqrt(length)
    sine_part = jnp.sin(angles) / math.sqrt(length)
    from_real = jnp.stack([cosine, -sine_part], axis=-1)
    from_imag = jnp.stack([sine_part, cosine], axis=-1)
    return jnp.stack([from_real, from_imag], axis=1)


def cell_centers():
    cell_index = jnp.arange(128, dtype=jnp.int32)
    return (
        jnp.stack([cell_index // 64, cell_index // 16 % 4, cell_index % 16]).astype(jnp.float32)
        + 0.5
    )


def brick_anchor(local_ids, bricks_y, bricks_z):
    clamped_weights = jnp.maximum(local_ids, 0)
    return jnp.stack(
        [
            2 * (clamped_weights // (bricks_y * bricks_z)),
            4 * (clamped_weights // bricks_z % bricks_y),
            16 * (clamped_weights % bricks_z),
        ],
        axis=-1,
    ).astype(jnp.float32)


def block_work(features, offsets, counts, local_ids, bricks_y, bricks_z):
    total_items, channels, points = features.shape
    group_size = math.gcd(total_items, 16)
    centers = cell_centers()

    def one_group(items):
        feature_share, offset_part, count_part, id_part = items
        validity = (jnp.arange(points, dtype=jnp.int32)[None, :] < count_part[:, None]).astype(
            jnp.float32
        )
        anchors = brick_anchor(id_part, bricks_y, bricks_z)
        relative_position = anchors - anchors[:, :1, :]
        placed = offset_part.astype(jnp.float32)[:, None, :, :] - relative_position[:, :, :, None]
        apart = placed[..., None] - centers[None, None, :, None, :]
        distance = jnp.sum(apart * apart, axis=2)
        kernel_weight_value = (
            AMPLITUDE * jnp.exp(-distance / SPREAD) * validity[:, None, :, None]
        ).astype(jnp.bfloat16)
        brick_tile_grid = jnp.einsum(
            "dqw,dewn->deqn", feature_share, kernel_weight_value, preferred_element_type=jnp.float32
        ).astype(jnp.bfloat16)
        return (kernel_weight_value, brick_tile_grid)

    grouped = tuple(
        (
            member.reshape((total_items // group_size, group_size) + member.shape[1:])
            for member in (features, offsets, counts, local_ids)
        )
    )
    kernel_weight_value, brick_tile_grid = lax.map(one_group, grouped)
    return (
        kernel_weight_value.reshape((total_items,) + kernel_weight_value.shape[2:]),
        brick_tile_grid.reshape((total_items,) + brick_tile_grid.shape[2:]),
    )


def decode_points(brick_values, kernel_weight_value):
    summed = jnp.einsum(
        "nhcx,nhpx->ncp", brick_values, kernel_weight_value, preferred_element_type=jnp.float32
    )
    return (DECODE_SCALE * summed).astype(jnp.bfloat16)


def accumulate(brick_tile_grid, local_ids, bricks_device):
    flat_ids = local_ids.reshape(-1)
    selector = (flat_ids[:, None] == jnp.arange(bricks_device, dtype=jnp.int32)[None, :]).astype(
        jnp.bfloat16
    )
    flat_tiles = brick_tile_grid.reshape((flat_ids.shape[0],) + brick_tile_grid.shape[2:])
    return jnp.einsum("rb,rcx->bcx", selector, flat_tiles, preferred_element_type=jnp.float32)


def to_grid(bricks, bricks_along_first, bricks_y, bricks_z):
    channels = bricks.shape[1]
    shaped = bricks.reshape(bricks_along_first, bricks_y, bricks_z, channels, 2, 4, 16)
    return shaped.transpose(3, 0, 4, 1, 5, 2, 6).reshape(
        channels, 2 * bricks_along_first, 4 * bricks_y, 16 * bricks_z
    )


def to_bricks(grid, bricks_along_first, bricks_y, bricks_z):
    channels = grid.shape[0]
    shaped = grid.reshape(channels, bricks_along_first, 2, bricks_y, 4, bricks_z, 16)
    return shaped.transpose(1, 3, 5, 0, 2, 4, 6).reshape(
        bricks_along_first * bricks_y * bricks_z, channels, 128
    )


def spectral(grid, weights, tables):
    table_third, forward_second, forward_first, back_second, back_first, back_third = tables
    channels, cells_x = (grid.shape[0], grid.shape[1])
    third_modes = jnp.einsum(
        "cxyz,zq->cxyq", grid.astype(jnp.float32), table_third, precision=PRECISE
    ).astype(jnp.bfloat16)
    columns = lax.all_to_all(third_modes, "py", split_axis=3, concat_axis=2, tiled=True)
    third_local = columns.shape[3] // 2
    second_modes = jnp.einsum(
        "cxyzp,ypkq->cxzkq",
        columns.reshape(channels, cells_x, columns.shape[2], third_local, 2).astype(jnp.float32),
        forward_second,
        precision=PRECISE,
    ).astype(jnp.bfloat16)
    row_lines = lax.all_to_all(second_modes, "px", split_axis=3, concat_axis=1, tiled=True)
    first_modes = jnp.einsum(
        "cxzkp,xpmq->mkzcq", row_lines.astype(jnp.float32), forward_first, precision=PRECISE
    ).astype(jnp.bfloat16)
    product = jnp.einsum(
        "mkzcp,mkzcr->mkzpr", first_modes, weights, preferred_element_type=jnp.float32
    )
    product = product.reshape(product.shape[:4] + (2, channels))
    mixed_real = product[:, :, :, 0, 0] - product[:, :, :, 1, 1]
    mixed_imag = product[:, :, :, 0, 1] + product[:, :, :, 1, 0]
    mixed = jnp.stack([mixed_real, mixed_imag], axis=-1)
    first_back = jnp.einsum("mkzcp,mpxq->cxzkq", mixed, back_first, precision=PRECISE).astype(
        jnp.bfloat16
    )
    row_back = lax.all_to_all(first_back, "px", split_axis=1, concat_axis=3, tiled=True)
    second_back = jnp.einsum(
        "cxzkp,kpyq->cxyzq", row_back.astype(jnp.float32), back_second, precision=PRECISE
    )
    second_back = second_back.reshape(channels, cells_x, second_back.shape[2], -1).astype(
        jnp.bfloat16
    )
    column_back = lax.all_to_all(second_back, "py", split_axis=2, concat_axis=3, tiled=True)
    return jnp.einsum(
        "cxyq,qz->cxyz", column_back.astype(jnp.float32), back_third, precision=PRECISE
    )


def slot_plan(block_bricks, bricks_device, slot_total, capacity):
    owners = block_bricks[:, 0] // bricks_device
    order_index = jnp.arange(owners.shape[0], dtype=jnp.int32)
    earlier = (owners[None, :] == owners[:, None]) & (order_index[None, :] < order_index[:, None])
    ranking = jnp.sum(earlier.astype(jnp.int32), axis=1)
    slot_index = owners * capacity + ranking
    matching = slot_index[None, :] == jnp.arange(slot_total, dtype=jnp.int32)[:, None]
    present = jnp.any(matching, axis=1)
    sources = jnp.sum(jnp.where(matching, order_index[None, :], 0), axis=1)
    return (slot_index, present, sources)


def pack_slots(values, present, sources, filler):
    picked = jnp.take(values, sources, axis=0)
    masking = present.reshape((-1,) + (1,) * (values.ndim - 1))
    return jnp.where(masking, picked, jnp.asarray(filler, values.dtype))


def route_back(values):
    return lax.all_to_all(values, ("px", "py"), split_axis=0, concat_axis=0, tiled=True)


def per_device(
    point_channel_values,
    point_offsets,
    point_counts,
    block_bricks,
    spectral_weights,
    skip_weights,
    skip_bias,
):
    mesh_rows = lax.axis_size("px")
    mesh_columns = lax.axis_size("py")
    device_total = mesh_rows * mesh_columns
    capacity = max(2, 2 * point_channel_values.shape[0] // device_total)
    bricks_along_first = NX // mesh_rows // 2
    bricks_y = NY // mesh_columns // 4
    bricks_z = NZ // 16
    bricks_device = bricks_along_first * bricks_y * bricks_z
    slot_total = device_total * capacity
    local_ids = block_bricks % bricks_device
    slot_index, present, sources = slot_plan(block_bricks, bricks_device, slot_total, capacity)
    packed_ids = pack_slots(local_ids, present, sources, -1)
    packed_features = pack_slots(point_channel_values, present, sources, 0)
    packed_offsets = pack_slots(point_offsets, present, sources, 0)
    packed_counts = pack_slots(point_counts, present, sources, 0)
    got_features, got_offsets, got_counts, got_ids = (
        lax.all_to_all(packed_features, ("px", "py"), split_axis=0, concat_axis=0, tiled=True),
        lax.all_to_all(packed_offsets, ("px", "py"), split_axis=0, concat_axis=0, tiled=True),
        lax.all_to_all(packed_counts, ("px", "py"), split_axis=0, concat_axis=0, tiled=True),
        lax.all_to_all(packed_ids, ("px", "py"), split_axis=0, concat_axis=0, tiled=True),
    )
    got_weight, got_tiles = block_work(
        got_features, got_offsets, got_counts, got_ids, bricks_y, bricks_z
    )
    encoded = accumulate(got_tiles, got_ids, bricks_device).astype(jnp.bfloat16)
    grid = to_grid(encoded, bricks_along_first, bricks_y, bricks_z)
    third_matrix = forward_matrix(NZ, jnp.arange(MODES, dtype=jnp.int32))[:, 0]
    weighting = jnp.where(jnp.arange(MODES) == 0, 1.0, 2.0).astype(jnp.float32)
    forward_second = forward_matrix(NY, wave_numbers(MODES))
    forward_first = forward_matrix(NX, wave_numbers(MODES))
    tables = (
        third_matrix.reshape(NZ, 2 * MODES),
        forward_second,
        forward_first,
        forward_second.transpose(2, 3, 0, 1),
        forward_first.transpose(2, 3, 0, 1),
        (third_matrix * weighting[None, :, None]).reshape(NZ, 2 * MODES).T,
    )
    for depth_index in range(LAYERS):
        spectral_part = spectral(grid, spectral_weights[depth_index], tables)
        skipped = jnp.einsum(
            "io,ixyz->oxyz", skip_weights[depth_index], grid, preferred_element_type=jnp.float32
        )
        grid = jax.nn.gelu(
            spectral_part + skipped + skip_bias[depth_index][:, None, None, None], approximate=False
        ).astype(jnp.bfloat16)
    final_bricks = to_bricks(grid, bricks_along_first, bricks_y, bricks_z)
    wanted = jnp.take(final_bricks, jnp.maximum(got_ids, 0), axis=0)
    reply = decode_points(wanted, got_weight)
    returned = route_back(reply)
    return jnp.take(returned, slot_index, axis=0)


def solution(mesh):
    return jax.shard_map(
        per_device,
        mesh=mesh,
        in_specs=(
            P(("px", "py"), None, None),
            P(("px", "py"), None, None),
            P(("px", "py")),
            P(("px", "py"), None),
            P(None, None, "px", "py", None, None),
            P(),
            P(),
        ),
        out_specs=P(("px", "py"), None, None),
        check_vma=False,
    )
```

profile of v0, /device:TPU:0, one launch (start us, length us, event | category | flops | bytes accessed | tf_op | source)
XLA Modules:
  0.0 1413.6 jit_solution(9622906543560222130)
XLA Ops:
  5.5 7.3 all-to-all-start.2
  19.9 4.5 all-to-all-start
  34.5 4.4 select_select_fusion
  38.9 6.2 all-to-all-done.1
  50.8 91.7 %all-to-all-done.3 = bf16[256,64,128]{2,1,0:T(8,128)(2,1)} async-done(((bf16[256,64,128]{2,1,0:T(8,128)(2,1)}), bf16[256,64,128]{2,1,0:T(8,128)(2,1)}, u32[]{:S(2)}, u32[]{:S(2)}) %all-to-all-start.3) | async-done | bytes 4194336 | tf_op jit(solution)/shard_map/all_to_all | solution.py:213
  142.5 154.9 %while.15 = (s32[]{:T(128)}, bf16[16,16,4,128,128]{4,3,2,1,0:T(8,128)(2,1)}, bf16[16,16,4,64,128]{4,3,2,1,0:T(8,128)(2,1)}, bf16[16,16,3,128]{3,2,1,0:T(4,128)(2...) while((s32[]{:T(128)}, ...), condition=%wide.region_5.6_spmd, body=%wide.region_3.5_spmd.sunk | while | flops 151557504 | bytes 16284649 | solution.py:86
  171.8 4.1 multiply_reduce_fusion.2
  297.4 30.0 %fusion.59 = bf16[512,64,128]{2,0,1:T(8,128)(2,1)} fusion(bf16[1024,64,128]{2,1,0:T(8,128)(2,1)} %bitcast.395, s32[1024]{0:T(1024)S(1)} %eq.74), kind=kOutput, calls=%fused_computation.116 | convolution fusion | flops 8594653184 | bytes 25169920 | tf_op jit(solution)/shard_map/rb,rcx->bcx/dot_general | solution.py:106
  327.4 17.6 %copy.421 = bf16[512,64,128]{1,2,0:T(8,128)(2,1)} copy(bf16[512,64,128]{2,0,1:T(8,128)(2,1)} %fusion.59) | data formatting | bytes 16777216 | tf_op jit(solution)/shard_map/convert_element_type | solution.py:221
  345.1 15.1 %copy.422 = bf16[64,8,2,8,4,8,16]{0,6,5,4,3,2,1:T(8,128)(2,1)} copy(bf16[64,8,2,8,4,8,16]{0,6,4,2,5,3,1:T(8,128)(2,1)} %bitcast.354) | data formatting | bytes 16777216 | tf_op jit(solution)/shard_map/transpose | solution.py:112
  360.2 18.9 %copy.424 = bf16[64,16,32,128]{3,2,1,0:T(8,128)(2,1)} copy(bf16[64,16,32,128]{0,3,2,1:T(8,128)(2,1)} %bitcast.350) | data formatting | bytes 16777216 | tf_op jit(solution)/shard_map/reshape | solution.py:112
  379.1 11.1 convolution_convert_fusion.1
  390.1 16.4 %copy.425 = bf16[64,16,32,64]{0,2,1,3:T(8,128)(2,1)} copy(bf16[64,16,32,64]{3,2,1,0:T(8,128)(2,1)} %convolution_convert_fusion.1) | data formatting | bytes 8388608 | tf_op jit(solution)/shard_map/convert_element_type | solution.py:130
  406.5 9.5 reshape.1014
  416.0 5.3 all-to-all-start.4
  421.5 48.0 %all-to-all-done.4 = bf16[4,2,262144]{2,1,0:T(2,128)(2,1)} async-done(((bf16[4,2,262144]{2,1,0:T(2,128)(2,1)}), bf16[4,2,262144]{2,1,0:T(2,128)(2,1)}, u32[]{:S(2)}, u32[]{:S(2)}) %all-to-all-start.4) | async-done | bytes 4194336 | tf_op jit(solution)/shard_map/all_to_all | solution.py:131
  469.5 9.3 reshape.1015
  478.8 9.3 copy.427
  488.1 10.1 copy.484
  498.1 10.3 bitcast_convert_fusion.4
  508.5 7.7 copy.429
  517.9 29.0 %all_to_all.165 = bf16[8,2,32768]{2,1,0:T(2,128)(2,1)} all-to-all(bf16[8,2,32768]{2,1,0:T(2,128)(2,1)S(1)} %reshape.1016), channel_id=1, replica_groups=mesh['px'=8,'py'=4] {'px'}, dimensions={0} | all-to-all | bytes 2097152 | tf_op jit(solution)/shard_map/all_to_all | solution.py:139
  556.8 8.1 fusion.32
  577.2 28.8 %all_to_all.166 = bf16[8,2,32768]{2,1,0:T(2,128)(2,1)S(1)} all-to-all(bf16[8,2,32768]{2,1,0:T(2,128)(2,1)S(1)} %reshape.1018), channel_id=1, replica_groups=mesh['px'=8,'py'=4] {'px'}, dimensions={0} | all-to-all | bytes 2097152 | tf_op jit(solution)/shard_map/all_to_all | solution.py:153
  615.2 4.6 copy.443
  619.8 16.5 %copy.444 = bf16[64,16,128,16]{0,3,1,2:T(8,128)(2,1)} copy(bf16[64,16,128,16]{2,1,3,0:T(8,128)(2,1)} %bitcast.368) | data formatting | bytes 8388608 | tf_op jit(solution)/shard_map/convert_element_type | solution.py:157
  636.4 9.6 reshape.1020
  645.9 5.0 all-to-all-start.7
  651.0 12.8 fusion.106
  663.8 35.3 %all-to-all-done.7 = bf16[4,2,262144]{2,1,0:T(2,128)(2,1)} async-done(((bf16[4,2,262144]{2,1,0:T(2,128)(2,1)}), bf16[4,2,262144]{2,1,0:T(2,128)(2,1)}, u32[]{:S(2)}, u32[]{:S(2)}) %all-to-all-start.7) | async-done | bytes 4194336 | tf_op jit(solution)/shard_map/all_to_all | solution.py:160
  699.1 9.3 reshape.1021
  708.4 9.1 copy.446
  717.5 13.1 copy.448
  730.6 28.6 %fusion.54 = (u16[64,32,128]{2,1,0:T(8,128)(2,1)S(1)}, f32[64,16,32,128]{3,2,1,0:T(8,128)}) fusion(f32[64]{0:T(128)S(1)} %get-tuple-element.225, f32[16,32,128,64]{2,3,1,0:T(8,128)} %fusion.106, bf16[64,16,32,64]{3,2,1,0:T(8,128)(2,1)} %copy.448, f32[128,64,1,1]{0,1,3,2:T(8,128)S(1)} %bitcast.388), kind=kOutput, calls=%fused_computation.104 | convolution fusion | flops 3258712064 | bytes 38306048 | tf_op jit(solution)/shard_map/cxyq,qz->cxyz/dot_general | solution.py:161
  759.2 38.2 %fusion.24 = bf16[64,16,32,128]{3,2,1,0:T(8,128)(2,1)S(1)} fusion(f32[64,16,32,128]{3,2,1,0:T(8,128)} %get-tuple-element.230, u16[64,32,128]{2,1,0:T(8,128)(2,1)S(1)} %get-tuple-element.229), kind=kLoop, calls=%fused_computation.54 | loop fusion | flops 285212672 | bytes 25690112 | tf_op jit(solution)/shard_map/convert_element_type | solution.py:242
  800.7 8.6 convolution_convert_fusion
  809.3 16.4 %copy.452 = bf16[64,16,32,64]{0,2,1,3:T(8,128)(2,1)} copy(bf16[64,16,32,64]{3,2,1,0:T(8,128)(2,1)} %convolution_convert_fusion) | data formatting | bytes 8388608 | tf_op jit(solution)/shard_map/convert_element_type | solution.py:130
  825.7 9.5 reshape.1022
  835.2 54.2 %all_to_all.167 = bf16[4,2,262144]{2,1,0:T(2,128)(2,1)} all-to-all(bf16[4,2,262144]{2,1,0:T(2,128)(2,1)} %reshape.1022), channel_id=1, replica_groups=mesh['px'=8,'py'=4] {'py'}, dimensions={0} | all-to-all | bytes 8388608 | tf_op jit(solution)/shard_map/all_to_all | solution.py:131
  889.4 9.3 reshape.1023
  898.7 9.3 copy.454
  907.9 10.1 copy.496
  918.0 10.4 bitcast_convert_fusion.2
  928.4 7.7 copy.456
  937.7 29.1 %all_to_all.168 = bf16[8,2,32768]{2,1,0:T(2,128)(2,1)} all-to-all(bf16[8,2,32768]{2,1,0:T(2,128)(2,1)S(1)} %reshape.1024), channel_id=1, replica_groups=mesh['px'=8,'py'=4] {'px'}, dimensions={0} | all-to-all | bytes 2097152 | tf_op jit(solution)/shard_map/all_to_all | solution.py:139
  976.7 8.1 fusion.29
  996.9 28.7 %all_to_all.169 = bf16[8,2,32768]{2,1,0:T(2,128)(2,1)S(1)} all-to-all(bf16[8,2,32768]{2,1,0:T(2,128)(2,1)S(1)} %reshape.1026), channel_id=1, replica_groups=mesh['px'=8,'py'=4] {'px'}, dimensions={0} | all-to-all | bytes 2097152 | tf_op jit(solution)/shard_map/all_to_all | solution.py:153
  1034.8 4.6 copy.470
  1039.4 16.5 %copy.471 = bf16[64,16,128,16]{0,3,1,2:T(8,128)(2,1)} copy(bf16[64,16,128,16]{2,1,3,0:T(8,128)(2,1)} %bitcast.369) | data formatting | bytes 8388608 | tf_op jit(solution)/shard_map/convert_element_type | solution.py:157
  1055.9 9.5 reshape.1028
  1065.5 5.3 all-to-all-start.11
  1072.5 15.5 %fusion.56 = f32[16,32,128,64]{2,3,1,0:T(8,128)} fusion(bf16[64,16,32,128]{3,2,1,0:T(8,128)(2,1)} %copy-done.2, bf16[2,64,64]{2,1,0:T(8,128)(2,1)S(1)} %copy-done.7), kind=kOutput, calls=%fused_computation.111 | convolution fusion | flops 536870912 | bytes 25182208 | tf_op jit(solution)/shard_map/io,ixyz->oxyz/dot_general | solution.py:237
  1088.0 30.9 %all-to-all-done.11 = bf16[4,2,262144]{2,1,0:T(2,128)(2,1)} async-done(((bf16[4,2,262144]{2,1,0:T(2,128)(2,1)}), bf16[4,2,262144]{2,1,0:T(2,128)(2,1)}, u32[]{:S(2)}, u32[]{:S(2)}) %all-to-all-start.11) | async-done | bytes 4194336 | tf_op jit(solution)/shard_map/all_to_all | solution.py:160
  1118.9 9.3 reshape.1029
  1128.2 9.1 copy.473
  1137.3 13.1 copy.474
  1150.4 45.7 %fusion.27 = bf16[64,16,32,128]{3,2,1,0:T(8,128)(2,1)} fusion(f32[16,32,128,64]{2,3,1,0:T(8,128)} %fusion.56, bf16[64,16,32,64]{3,2,1,0:T(8,128)(2,1)} %copy.474, f32[128,64,1,1]{0,1,3,2:T(8,128)S(1)} %bitcast.389, f32[64]{0:T(128)S(1)} %get-tuple-element.224), kind=kOutput, calls=%fused_computation.57 | convolution fusion | flops 3502243840 | bytes 29393152 | tf_op jit(solution)/shard_map/cxyq,qz->cxyz/dot_general | solution.py:161
  1196.1 17.7 %copy.478 = bf16[64,16,32,128]{0,3,2,1:T(8,128)(2,1)} copy(bf16[64,16,32,128]{3,2,1,0:T(8,128)(2,1)} %fusion.27) | data formatting | bytes 16777216 | tf_op jit(solution)/shard_map/convert_element_type | solution.py:242
  1213.8 15.3 %copy.479 = bf16[8,8,8,64,2,4,16]{3,6,5,4,2,1,0:T(8,128)(2,1)} copy(bf16[8,8,8,64,2,4,16]{3,6,2,5,1,4,0:T(8,128)(2,1)} %bitcast.355) | data formatting | bytes 16777216 | tf_op jit(solution)/shard_map/transpose | solution.py:120
  1229.1 26.6 %gather_fusion.4 = bf16[1024,64,128]{1,2,0:T(8,128)(2,1)} fusion(bf16[512,64,128]{1,2,0:T(8,128)(2,1)} %bitcast.353, s32[1024]{0:T(1024)S(1)} %copy-done.3), kind=kCustom, calls=%fused_computation.4 | custom fusion | bytes 33558528 | tf_op jit(solution)/shard_map/jit(_take)/gather | solution.py:244
  1255.7 30.5 %copy.481 = bf16[256,4,64,128]{3,2,1,0:T(8,128)(2,1)} copy(bf16[256,4,64,128]{2,3,1,0:T(8,128)(2,1)} %bitcast.352) | data formatting | bytes 33554432 | tf_op jit(solution)/shard_map/jit(_take)/gather | solution.py:244
  1286.2 22.2 %fusion.55 = bf16[256,64,128]{2,1,0:T(8,128)(2,1)} fusion(bf16[256,4,128,128]{3,2,1,0:T(8,128)(2,1)} %bitcast.394, bf16[256,4,64,128]{3,2,1,0:T(8,128)(2,1)} %copy.481, pred[256,4]{1,0:T(8,128)(4,1)S(1)} %bitcast.390), kind=kOutput, calls=%fused_computation.106 | convolution fusion | flops 2160066560 | bytes 54526976 | tf_op jit(solution)/shard_map/nhcx,nhpx->ncp/dot_general | solution.py:94
  1312.7 93.2 %all-to-all-done.12 = bf16[256,64,128]{2,1,0:T(8,128)(2,1)} async-done(((bf16[256,64,128]{2,1,0:T(8,128)(2,1)}), bf16[256,64,128]{2,1,0:T(8,128)(2,1)}, u32[]{:S(2)}, u32[]{:S(2)}) %all-to-all-start.12) | async-done | bytes 4194336 | tf_op jit(solution)/shard_map/all_to_all | solution.py:185
  1405.9 4.3 gather_fusion.5
  (339 shorter events, 256.3 us)
Async XLA Ops:
  0.0 24.6 %copy-start = (bf16[128,64,128]{2,1,0:T(8,128)(2,1)S(1)}, bf16[128,64,128]{2,1,0:T(8,128)(2,1)}, u32[]{:S(2)}) copy-start(bf16[128,64,128]{2,1,0:T(8,128)(2,1)} %param.9) | copy-start | bytes 6291460
  1.7 0.8 copy-start.9
  5.5 14.4 %all-to-all-start.2 = ((s32[32,8,1]{1,2,0:T(1,128)}), s32[32,8,1]{1,2,0:T(1,128)S(1)}, u32[]{:S(2)}, u32[]{:S(2)}) async-start(s32[32,8,1]{1,2,0:T(1,128)} %bitcast.34), calls=%async_computation.2 | async-start | bytes 32768 | tf_op jit(solution)/shard_map/all_to_all | solution.py:215
  19.9 12.0 all-to-all-start
  31.9 110.6 %copy-start.4 = (s32[32,8,4]{1,2,0:T(4,128)}, s32[32,8,4]{1,2,0:T(4,128)S(1)}, u32[]{:S(2)}) copy-start(s32[32,8,4]{1,2,0:T(4,128)S(1)} %all-to-all-done) | copy-start | bytes 12292
  31.9 13.2 all-to-all-start.1
  45.0 97.5 %all-to-all-start.3 = ((bf16[256,64,128]{2,1,0:T(8,128)(2,1)}), bf16[256,64,128]{2,1,0:T(8,128)(2,1)}, u32[]{:S(2)}, u32[]{:S(2)}) async-start(bf16[256,64,128]{2,1,0:T(8,128)(2,1)} %select_select_fusion), calls=%async_computation.3 | async-start | bytes 8388608 | tf_op jit(solution)/shard_map/all_to_all | solution.py:213
  416.0 53.4 %all-to-all-start.4 = ((bf16[4,2,262144]{2,1,0:T(2,128)(2,1)}), bf16[4,2,262144]{2,1,0:T(2,128)(2,1)}, u32[]{:S(2)}, u32[]{:S(2)}) async-start(bf16[4,2,262144]{2,1,0:T(2,128)(2,1)} %reshape.1014), calls=%async_computation.4 | async-start | bytes 8388608 | tf_op jit(solution)/shard_map/all_to_all | solution.py:131
  619.8 31.1 %copy-start.8 = (f32[2,64]{1,0:T(2,128)S(1)}, f32[2,64]{1,0:T(2,128)}, u32[]{:S(2)}) copy-start(f32[2,64]{1,0:T(2,128)} %param.15) | copy-start | bytes 1540
  619.8 31.2 %copy-start.7 = (bf16[2,64,64]{2,1,0:T(8,128)(2,1)S(1)}, bf16[2,64,64]{2,1,0:T(8,128)(2,1)}, u32[]{:S(2)}) copy-start(bf16[2,64,64]{2,1,0:T(8,128)(2,1)} %param.14) | copy-start | bytes 49156
  645.9 53.2 %all-to-all-start.7 = ((bf16[4,2,262144]{2,1,0:T(2,128)(2,1)}), bf16[4,2,262144]{2,1,0:T(2,128)(2,1)}, u32[]{:S(2)}, u32[]{:S(2)}) async-start(bf16[4,2,262144]{2,1,0:T(2,128)(2,1)} %reshape.1020), calls=%async_computation.7 | async-start | bytes 8388608 | tf_op jit(solution)/shard_map/all_to_all | solution.py:160
  797.4 3.2 copy-start.2
  1039.4 31.3 %copy-start.5 = (s32[32,8,4]{1,2,0:T(4,128)S(1)}, s32[32,8,4]{1,2,0:T(4,128)}, u32[]{:S(2)}) copy-start(s32[32,8,4]{1,2,0:T(4,128)} %copy-done.4) | copy-start | bytes 12292
  1065.5 53.4 %all-to-all-start.11 = ((bf16[4,2,262144]{2,1,0:T(2,128)(2,1)}), bf16[4,2,262144]{2,1,0:T(2,128)(2,1)}, u32[]{:S(2)}, u32[]{:S(2)}) async-start(bf16[4,2,262144]{2,1,0:T(2,128)(2,1)} %reshape.1028), calls=%async_computation.11 | async-start | bytes 8388608 | tf_op jit(solution)/shard_map/all_to_all | solution.py:160
  1213.8 15.3 %copy-start.3 = (s32[1024]{0:T(1024)S(1)}, s32[1024]{0:T(1024)}, u32[]{:S(2)}) copy-start(s32[1024]{0:T(1024)} %broadcast_clamp_fusion) | copy-start | bytes 12292
  1255.7 30.5 %copy-start.6 = (pred[32,8,4]{2,1,0:T(8,128)(4,1)S(1)}, pred[32,8,4]{2,1,0:T(8,128)(4,1)}, u32[]{:S(2)}) copy-start(pred[32,8,4]{2,1,0:T(8,128)(4,1)} %copy.505) | copy-start | bytes 3076
  1286.2 25.8 %copy-start.10 = (s32[128]{0:T(128)S(1)}, s32[128]{0:T(128)}, u32[]{:S(2)}) copy-start(s32[128]{0:T(128)} %copy-done.9) | copy-start | bytes 1540
  1286.2 127.2 %copy-start.1 = (bf16[128,64,128]{2,1,0:T(8,128)(2,1)S(1)}, bf16[128,64,128]{2,1,0:T(8,128)(2,1)}, u32[]{:S(2)}) copy-start(bf16[128,64,128]{2,1,0:T(8,128)(2,1)} %param.9) | copy-start | bytes 6291460
  1308.4 97.5 %all-to-all-start.12 = ((bf16[256,64,128]{2,1,0:T(8,128)(2,1)}), bf16[256,64,128]{2,1,0:T(8,128)(2,1)}, u32[]{:S(2)}, u32[]{:S(2)}) async-start(bf16[256,64,128]{2,1,0:T(8,128)(2,1)} %fusion.55), calls=%async_computation.12 | async-start | bytes 8388608 | tf_op jit(solution)/shard_map/all_to_all | solution.py:185
where the time goes:
time: 1430 us; the launch traced here: 1410 us
  local copies, waits for them, and re-layouts  462 us (32%)
  waiting for transfers between devices  310 us (22%)
  matrix products  273 us (19%)
  blocking collectives  170 us (12%)
  other arithmetic  160 us (11%)
  starting transfers between devices  37.1 us (3%)
    unnamed x39, local copies, waits for them, and re-layouts  97.6 us
    all_to_all x1, waiting for transfers between devices, route_back(): lax.all_to_all(values, ('px', 'py'), split_axis=0, concat_axis=0, tiled=T...  93.2 us
    all_to_all x1, waiting for transfers between devices, per_device(): lax.all_to_all(packed_features, ('px', 'py'), split_axis=0, concat_axis=0...  91.7 us
    dot_general x2, matrix products, spectral(): jnp.einsum('cxyq,qz->cxyz', column_back.astype(jnp.float32), back_third,...  74.4 us
    all_to_all x2, waiting for transfers between devices, spectral(): lax.all_to_all(second_back, 'py', split_axis=2, concat_axis=3, tiled=True)  66.3 us
    reduce_sum x16, other arithmetic, one_group(): distance = jnp.sum(apart * apart, axis=2)  65.9 us
    all_to_all x2, blocking collectives, spectral(): lax.all_to_all(second_modes, 'px', split_axis=3, concat_axis=1, tiled=True)  58.1 us
    all_to_all x2, blocking collectives, spectral(): lax.all_to_all(first_back, 'px', split_axis=1, concat_axis=3, tiled=True)  57.6 us
  transfers between devices with their start and end apart: 8, of which 8 were waited for; matrix products, arithmetic and copies ran while one was open for 3% of the time, Pallas kernels for 0%

commit v1 on v0

v1 whole, which is shorter than its diff:
```python
import functools
import math

import jax
import jax.numpy as jnp
from jax import lax
from jax.experimental import pallas as pl
from jax.experimental.pallas import tpu as pltpu
from jax.sharding import PartitionSpec as P

MODES = 32
NX = 128
NY = 128
NZ = 128
LAYERS = 2

AMPLITUDE = 0.25
SPREAD = 4.5
DECODE_SCALE = 0.1
VMEM_LIMIT = 60 * 1024 * 1024
F32 = jnp.float32
BF16 = jnp.bfloat16


def wave_numbers(kept_modes):
    position = jnp.arange(kept_modes, dtype=jnp.int32)
    return jnp.where(position < kept_modes // 2, position, position - kept_modes)


def forward_matrix(length, frequency):
    places = jnp.arange(length, dtype=jnp.int32)
    products = jnp.remainder(places[:, None] * frequency[None, :], length)
    angles = 2.0 * math.pi / length * products.astype(F32)
    cosine = jnp.cos(angles) / math.sqrt(length)
    sine_part = jnp.sin(angles) / math.sqrt(length)
    from_real = jnp.stack([cosine, -sine_part], axis=-1)
    from_imag = jnp.stack([sine_part, cosine], axis=-1)
    return jnp.stack([from_real, from_imag], axis=1)


def unit_angles(products, length):
    return 2.0 * math.pi / length * jnp.remainder(products, length).astype(F32)


def block_kernel(info_ref, slot, offsets, points):
    base = slot * 13
    count = info_ref[base + 12]
    lanes = lax.broadcasted_iota(jnp.int32, (1, points), 1)
    amplitude = jnp.where(lanes < count, AMPLITUDE, 0.0).astype(F32)

    def part(dim, brick, cells, scale):
        shift = ((info_ref[base + 3 * brick + dim] - info_ref[base + dim]) * scale).astype(F32)
        center = lax.broadcasted_iota(jnp.int32, (cells, points), 0).astype(F32) + 0.5
        apart = (offsets[dim : dim + 1, :] - shift) - center
        return jnp.exp(apart * apart * (-1.0 / SPREAD))

    rows = []
    for brick in range(4):
        along_x = part(0, brick, 2, 2) * amplitude
        along_y = part(1, brick, 4, 4)
        along_z = part(2, brick, 16, 16)
        for cy in range(4):
            plane = along_z * along_y[cy : cy + 1, :]
            rows.append(
                jnp.concatenate(
                    [plane * along_x[0:1, :], plane * along_x[1:2, :]], axis=1
                ).astype(BF16)
            )
    return jnp.concatenate(rows, axis=0)


def brick_place(info_ref, slot, brick, cy, depth):
    base = slot * 13 + 3 * brick
    row = (info_ref[base + 1] * 4 + cy) * depth + info_ref[base + 2] * 16
    return (
        pl.ds(pl.multiple_of(row, 16), 16),
        pl.ds(pl.multiple_of(info_ref[base] * 128, 128), 128),
    )


def encode_body(group, depth, steps, info_ref, feature_ref, offset_ref, out_ref, total_ref):
    step = pl.program_id(0)
    channels, points = feature_ref.shape[1:]

    @pl.when(step == 0)
    def _():
        total_ref[...] = jnp.zeros_like(total_ref)

    def one(member, carry):
        slot = step * group + member

        @pl.when(info_ref[slot * 13 + 12] > 0)
        def _():
            values = block_kernel(info_ref, slot, offset_ref[member].astype(F32), points)
            feature = feature_ref[member]
            empty = jnp.zeros_like(feature)
            pair = jnp.concatenate(
                [
                    jnp.concatenate([feature, empty], axis=1),
                    jnp.concatenate([empty, feature], axis=1),
                ],
                axis=0,
            )
            tiles = lax.dot_general(
                values, pair, (((1,), (1,)), ((), ())), preferred_element_type=F32
            )
            tiles = tiles.astype(BF16).astype(F32)
            for brick in range(4):
                for cy in range(4):
                    place = brick_place(info_ref, slot, brick, cy, depth)
                    start = brick * 64 + cy * 16
                    total_ref[place] = total_ref[place] + tiles[start : start + 16, :]

        return carry

    lax.fori_loop(0, group, one, 0)

    @pl.when(step == steps - 1)
    def _():
        out_ref[...] = total_ref[...].astype(BF16)


def encode(info, features, offsets, rows, depth, lanes):
    slots, channels, points = features.shape
    group = math.gcd(slots, 32)
    steps = slots // group
    return pl.pallas_call(
        functools.partial(encode_body, group, depth, steps),
        grid_spec=pltpu.PrefetchScalarGridSpec(
            num_scalar_prefetch=1,
            grid=(steps,),
            in_specs=[
                pl.BlockSpec((group, channels, points), lambda i, info: (i, 0, 0)),
                pl.BlockSpec((group, offsets.shape[1], points), lambda i, info: (i, 0, 0)),
            ],
            out_specs=pl.BlockSpec((rows, lanes), lambda i, info: (0, 0)),
            scratch_shapes=[pltpu.VMEM((rows, lanes), F32)],
        ),
        out_shape=jax.ShapeDtypeStruct((rows, lanes), BF16),
        compiler_params=pltpu.CompilerParams(vmem_limit_bytes=VMEM_LIMIT),
        name="encode",
    )(info, features, offsets)


def decode_body(group, depth, info_ref, grid_ref, offset_ref, out_ref):
    step = pl.program_id(0)
    channels, points = out_ref.shape[1:]

    def one(member, carry):
        slot = step * group + member

        @pl.when(info_ref[slot * 13 + 12] > 0)
        def _():
            values = block_kernel(info_ref, slot, offset_ref[member].astype(F32), points)
            cells = jnp.concatenate(
                [
                    grid_ref[brick_place(info_ref, slot, brick, cy, depth)]
                    for brick in range(4)
                    for cy in range(4)
                ],
                axis=0,
            )
            both = lax.dot_general(
                cells, values, (((0,), (0,)), ((), ())), preferred_element_type=F32
            )
            summed = both[:channels, :points] + both[channels:, points:]
            out_ref[member] = (DECODE_SCALE * summed).astype(BF16)

        @pl.when(info_ref[slot * 13 + 12] <= 0)
        def _():
            out_ref[member] = jnp.zeros((channels, points), BF16)

        return carry

    lax.fori_loop(0, group, one, 0)


def decode(info, grid, offsets, channels, depth):
    slots, rows3, points = offsets.shape
    group = math.gcd(slots, 32)
    return pl.pallas_call(
        functools.partial(decode_body, group, depth),
        grid_spec=pltpu.PrefetchScalarGridSpec(
            num_scalar_prefetch=1,
            grid=(slots // group,),
            in_specs=[
                pl.BlockSpec(grid.shape, lambda i, info: (0, 0)),
                pl.BlockSpec((group, rows3, points), lambda i, info: (i, 0, 0)),
            ],
            out_specs=pl.BlockSpec((group, channels, points), lambda i, info: (i, 0, 0)),
        ),
        out_shape=jax.ShapeDtypeStruct((slots, channels, points), BF16),
        compiler_params=pltpu.CompilerParams(vmem_limit_bytes=VMEM_LIMIT),
        name="decode",
    )(info, grid, offsets)


def forward_table_body(depth, u_ref, v_ref, cos_ref, sin_ref, out_ref):
    for place in range(out_ref.shape[1] // depth):
        out_ref[:, place * depth : (place + 1) * depth] = (
            u_ref[:, place : place + 1] * cos_ref[...] + v_ref[:, place : place + 1] * sin_ref[...]
        ).astype(BF16)


def forward_table(u, v, cosine, sine):
    modes, cells_y = u.shape
    depth = cosine.shape[1]
    block = math.gcd(modes, 256)
    narrow = pl.BlockSpec((block, cells_y), lambda i: (i, 0))
    wide = pl.BlockSpec((block, depth), lambda i: (i, 0))
    return pl.pallas_call(
        functools.partial(forward_table_body, depth),
        grid=(modes // block,),
        in_specs=[narrow, narrow, wide, wide],
        out_specs=pl.BlockSpec((block, cells_y * depth), lambda i: (i, 0)),
        out_shape=jax.ShapeDtypeStruct((modes, cells_y * depth), BF16),
        compiler_params=pltpu.CompilerParams(vmem_limit_bytes=VMEM_LIMIT),
        name="forward_table",
    )(u, v, cosine, sine)


def back_table_body(depth, u_ref, v_ref, cos_ref, sin_ref, out_ref):
    for place in range(u_ref.shape[0]):
        out_ref[place * depth : (place + 1) * depth, :] = (
            u_ref[place : place + 1, :] * cos_ref[...] + v_ref[place : place + 1, :] * sin_ref[...]
        ).astype(BF16)


def back_table(u, v, cosine, sine):
    cells_y, modes = u.shape
    depth = cosine.shape[0]
    group = math.gcd(cells_y, 8)
    narrow = pl.BlockSpec((group, modes), lambda i: (i, 0))
    wide = pl.BlockSpec((depth, modes), lambda i: (0, 0))
    return pl.pallas_call(
        functools.partial(back_table_body, depth),
        grid=(cells_y // group,),
        in_specs=[narrow, narrow, wide, wide],
        out_specs=pl.BlockSpec((group * depth, modes), lambda i: (i, 0)),
        out_shape=jax.ShapeDtypeStruct((cells_y * depth, modes), BF16),
        compiler_params=pltpu.CompilerParams(vmem_limit_bytes=VMEM_LIMIT),
        name="back_table",
    )(u, v, cosine, sine)


def layer_body(table_ref, modes_ref, grid_ref, skip_ref, bias_ref, out_ref):
    width = skip_ref.shape[0]
    for start in range(0, out_ref.shape[1], width):
        lanes = slice(start, start + width)
        spectral = jnp.dot(table_ref[...], modes_ref[:, lanes], preferred_element_type=F32)
        skipped = jnp.dot(grid_ref[:, lanes], skip_ref[...], preferred_element_type=F32)
        value = spectral + skipped + bias_ref[...]
        out_ref[:, lanes] = (
            0.5 * value * (1.0 + lax.erf(value * math.sqrt(0.5)))
        ).astype(BF16)


def layer_back(table, modes, grid, skip, bias):
    rows, lanes = grid.shape
    depth = modes.shape[0]
    block = math.gcd(rows, 256)
    channels = skip.shape[0]
    copies = math.gcd(lanes // channels, 4)
    width = copies * channels
    wide_skip = jnp.kron(jnp.eye(copies, dtype=BF16), skip)
    wide_bias = jnp.tile(bias, copies).reshape(1, width)
    return pl.pallas_call(
        layer_body,
        grid=(rows // block,),
        in_specs=[
            pl.BlockSpec((block, depth), lambda i: (i, 0)),
            pl.BlockSpec((depth, lanes), lambda i: (0, 0)),
            pl.BlockSpec((block, lanes), lambda i: (i, 0)),
            pl.BlockSpec((width, width), lambda i: (0, 0)),
            pl.BlockSpec((1, width), lambda i: (0, 0)),
        ],
        out_specs=pl.BlockSpec((block, lanes), lambda i: (i, 0)),
        out_shape=jax.ShapeDtypeStruct((rows, lanes), BF16),
        compiler_params=pltpu.CompilerParams(vmem_limit_bytes=VMEM_LIMIT),
        name="layer_back",
    )(table, modes, grid, wide_skip, wide_bias)


def swap(values, distance, size):
    return lax.ppermute(values, "py", [(i, i ^ distance) for i in range(size)])


def spectral_modes(grid, weights, forward, first_forward, first_back_table, size):
    rows_px = lax.axis_size("px")
    channels = weights.shape[3]
    ky_dev, kz_dev = weights.shape[1], weights.shape[2]
    lanes = grid.shape[1]
    x_dev = lanes // channels
    held = jnp.dot(forward, grid, preferred_element_type=F32).astype(BF16)
    held = held.reshape(size, -1, lanes)
    distance = 1
    while distance < size:
        halves = held.reshape(held.shape[0] // 2, 2, -1, lanes)
        came = swap(halves[:, 1], distance, size)
        held = (halves[:, 0].astype(F32) + came.astype(F32)).astype(BF16)
        distance *= 2
    own = held.reshape(rows_px, -1, lanes)
    lines = lax.all_to_all(own, "px", split_axis=0, concat_axis=0, tiled=True)
    lines = lines.reshape(rows_px, ky_dev, kz_dev, 2, x_dev, channels)
    first_modes = jnp.einsum(
        "skzpxc,sxpmq->mkzqc", lines, first_forward, preferred_element_type=F32
    ).astype(BF16)
    product = jnp.einsum(
        "mkzpc,mkzcr->mkzpr", first_modes, weights, preferred_element_type=F32
    )
    mixed = jnp.stack(
        [
            product[..., 0, :channels] - product[..., 1, channels:],
            product[..., 0, channels:] + product[..., 1, :channels],
        ],
        axis=3,
    ).astype(BF16)
    first_back = jnp.einsum(
        "mkzpc,mpsxq->skzqxc", mixed, first_back_table, preferred_element_type=F32
    ).astype(BF16)
    first_back = first_back.reshape(rows_px, -1, lanes)
    back = lax.all_to_all(first_back, "px", split_axis=0, concat_axis=0, tiled=True)
    held = back.reshape(1, -1, lanes)
    distance = size // 2
    while distance >= 1:
        came = swap(held, distance, size)
        held = jnp.stack([held, came], axis=1).reshape(-1, held.shape[1], lanes)
        distance //= 2
    return held.reshape(-1, lanes)


def slot_plan(block_bricks, bricks_device, slot_total, capacity):
    owners = block_bricks[:, 0] // bricks_device
    order_index = jnp.arange(owners.shape[0], dtype=jnp.int32)
    earlier = (owners[None, :] == owners[:, None]) & (order_index[None, :] < order_index[:, None])
    ranking = jnp.sum(earlier.astype(jnp.int32), axis=1)
    slot_index = owners * capacity + ranking
    matching = slot_index[None, :] == jnp.arange(slot_total, dtype=jnp.int32)[:, None]
    present = jnp.any(matching, axis=1)
    sources = jnp.sum(jnp.where(matching, order_index[None, :], 0), axis=1)
    return (slot_index, present, sources)


def pack_slots(values, present, sources, filler):
    picked = jnp.take(values, sources, axis=0)
    masking = present.reshape((-1,) + (1,) * (values.ndim - 1))
    return jnp.where(masking, picked, jnp.asarray(filler, values.dtype))


def route_back(values):
    return lax.all_to_all(values, ("px", "py"), split_axis=0, concat_axis=0, tiled=True)


def per_device(
    point_channel_values,
    point_offsets,
    point_counts,
    block_bricks,
    spectral_weights,
    skip_weights,
    skip_bias,
):
    mesh_rows = lax.axis_size("px")
    mesh_columns = lax.axis_size("py")
    device_total = mesh_rows * mesh_columns
    capacity = max(2, 2 * point_channel_values.shape[0] // device_total)
    channels, points = point_channel_values.shape[1:]
    x_dev, y_dev = NX // mesh_rows, NY // mesh_columns
    bricks_y = y_dev // 4
    bricks_z = NZ // 16
    bricks_device = x_dev // 2 * bricks_y * bricks_z
    slot_total = device_total * capacity
    local_ids = block_bricks % bricks_device
    slot_index, present, sources = slot_plan(block_bricks, bricks_device, slot_total, capacity)
    coordinates = jnp.stack(
        [local_ids // (bricks_y * bricks_z), local_ids // bricks_z % bricks_y, local_ids % bricks_z],
        axis=-1,
    ).reshape(local_ids.shape[0], -1)
    facts = jnp.concatenate([coordinates, point_counts[:, None]], axis=1).astype(BF16)
    facts = jnp.pad(facts, ((0, 0), (0, points - facts.shape[1])))
    notes = jnp.concatenate([point_offsets, facts[:, None, :]], axis=1)
    packed_notes = pack_slots(notes, present, sources, 0)
    packed_features = pack_slots(point_channel_values, present, sources, 0)
    got_notes = route_back(packed_notes)
    got_features = route_back(packed_features)
    info = got_notes[:, 3, :13].astype(jnp.int32).reshape(-1)

    kz_dev = MODES // mesh_columns
    me_x, me_y = lax.axis_index("px"), lax.axis_index("py")
    index = jnp.arange(2 * MODES * MODES, dtype=jnp.int32)
    part = index % 2
    kz = index // 2 % kz_dev + kz_dev * jnp.bitwise_xor(index // (2 * kz_dev * MODES), me_y)
    ky_at = index // (2 * kz_dev) % MODES
    ky = jnp.where(ky_at < MODES // 2, ky_at, ky_at - MODES)
    angle_y = unit_angles(
        ky[:, None] * (me_y * y_dev + jnp.arange(y_dev, dtype=jnp.int32))[None, :], NY
    )
    angle_z = unit_angles(kz[:, None] * jnp.arange(NZ, dtype=jnp.int32)[None, :], NZ)
    real_row = (part == 0)[:, None]
    norm = 1.0 / math.sqrt(NY * NZ)
    cos_y, sin_y = jnp.cos(angle_y) * norm, jnp.sin(angle_y) * norm
    table_u = jnp.where(real_row, cos_y, -sin_y)
    table_v = jnp.where(real_row, -sin_y, -cos_y)
    cos_z, sin_z = jnp.cos(angle_z), jnp.sin(angle_z)
    forward = forward_table(table_u, table_v, cos_z, sin_z)
    fold = jnp.where(kz == 0, 1.0, 2.0).astype(F32)[:, None]
    back = back_table(table_u.T, table_v.T, (cos_z * fold).T, (sin_z * fold).T)
    first_matrix = forward_matrix(NX, wave_numbers(MODES))
    first_forward = first_matrix.reshape(mesh_rows, x_dev, 2, MODES, 2).astype(BF16)
    first_back = (
        first_matrix.transpose(2, 3, 0, 1).reshape(MODES, 2, mesh_rows, x_dev, 2).astype(BF16)
    )
    grid = encode(info, got_features, got_notes, y_dev * NZ, NZ, x_dev * channels)
    for depth_index in range(LAYERS):
        modes = spectral_modes(
            grid, spectral_weights[depth_index], forward, first_forward, first_back, mesh_columns
        )
        grid = layer_back(
            back, modes, grid, skip_weights[depth_index], skip_bias[depth_index]
        )
    reply = decode(info, grid, got_notes, channels, NZ)
    returned = route_back(reply)
    return jnp.take(returned, slot_index, axis=0)


def solution(mesh):
    return jax.shard_map(
        per_device,
        mesh=mesh,
        in_specs=(
            P(("px", "py"), None, None),
            P(("px", "py"), None, None),
            P(("px", "py")),
            P(("px", "py"), None),
            P(None, None, "px", "py", None, None),
            P(),
            P(),
        ),
        out_specs=P(("px", "py"), None, None),
        check_vma=False,
    )
```

time: 1430 us -> 770 us (0.54)
  local copies, waits for them, and re-layouts: 462 us -> 28.4 us
  matrix products: 273 us -> 64.9 us
  Pallas kernels: 0 us -> 168 us
  other arithmetic: 160 us -> 57.4 us
  blocking collectives: 170 us -> 88.3 us
  starting transfers between devices: 37.1 us -> 70.1 us
  waiting for transfers between devices: 310 us -> 288 us
    dot_general x34 -> x8, matrix products: 273 us -> 64.9 us  [the longest x2 45.3 us: spectral_modes(): held = jnp.dot(forward, grid, preferred_element_type=F32).astype(BF16)]
    all_to_all x7 -> x1, waiting for transfers between devices: 217 us -> 24.8 us  [spectral_modes(): lines = lax.all_to_all(own, 'px', split_axis=0, concat_axis=0, tiled=True)]
    pallas_call x0 -> x6, Pallas kernels: none -> 168 us  [the longest x2 56.1 us: layer_back(): pl.pallas_call(layer_body, grid=(rows // block,), in_specs=[pl.BlockSpec(...]
    convert_element_type x12 -> x3, local copies, waits for them, and re-layouts: 132 us -> 4.3 us  [the longest x2 3.5 us: spectral_modes(): first_back = jnp.einsum('mkzpc,mpsxq->skzqxc', mixed, first_back_table, p...]
    ppermute x0 -> x8, waiting for transfers between devices: none -> 107 us  [swap(): return lax.ppermute(values, 'py', [(i, i ^ distance) for i in range(size)])]
    unnamed x39 -> x31, local copies, waits for them, and re-layouts: 97.6 us -> 1.06 us
    all_to_all x5 -> x3, blocking collectives: 170 us -> 88.3 us  [the longest x2 58.3 us: spectral_modes(): lax.all_to_all(first_back, 'px', split_axis=0, concat_axis=0, tiled=True)]
    all_to_all x16 -> x2, local copies, waits for them, and re-layouts: 79.6 us -> 1.16 us  [spectral_modes(): lines = lax.all_to_all(own, 'px', split_axis=0, concat_axis=0, tiled=True)]
  transfers between devices with their start and end apart: 8 -> 12, of which waited for: 8 -> 11; matrix products, arithmetic and copies ran while one was open for 3% -> 4% of each run, Pallas kernels for 0% -> 4%
where the time goes in v1:
time: 770 us; the launch traced here: 765 us
  waiting for transfers between devices  288 us (37%)
  Pallas kernels  168 us (22%)
  blocking collectives  88.3 us (11%)
  starting transfers between devices  70.1 us (9%)
  matrix products  64.9 us (8%)
  other arithmetic  57.4 us (7%)
  local copies, waits for them, and re-layouts  28.4 us (4%)
    all_to_all x3, waiting for transfers between devices, route_back(): lax.all_to_all(values, ('px', 'py'), split_axis=0, concat_axis=0, tiled=T...  155 us
    ppermute x8, waiting for transfers between devices, swap(): return lax.ppermute(values, 'py', [(i, i ^ distance) for i in range(size)])  107 us
    all_to_all x2, blocking collectives, spectral_modes(): lax.all_to_all(first_back, 'px', split_axis=0, concat_axis=0, tiled=True)  58.3 us
    pallas_call x2, Pallas kernels, layer_back(): pl.pallas_call(layer_body, grid=(rows // block,), in_specs=[pl.BlockSpec(...  56.1 us
    dot_general x2, matrix products, spectral_modes(): held = jnp.dot(forward, grid, preferred_element_type=F32).astype(BF16)  45.3 us
    pallas_call x1, Pallas kernels, encode(): pl.pallas_call(functools.partial(encode_body, group, depth, steps), grid_...  41.4 us
    pallas_call x1, Pallas kernels, decode(): pl.pallas_call(functools.partial(decode_body, group, depth), grid_spec=pl...  40.5 us
    all_to_all x3, starting transfers between devices, route_back(): lax.all_to_all(values, ('px', 'py'), split_axis=0, concat_axis=0, tiled=T...  39.5 us
  transfers between devices with their start and end apart: 12, of which 11 were waited for; matrix products, arithmetic and copies ran while one was open for 4% of the time, Pallas kernels for 4%

profile of v1, /device:TPU:0, one launch (start us, length us, event | category | flops | bytes accessed | tf_op | source)
XLA Modules:
  0.0 765.0 jit_solution(17109523055781257032)
XLA Ops:
  0.0 0.8 fusion.105
  2.7 0.7 fusion.95
  4.3 1.0 copy.70
  5.4 1.0 gather_fusion
  6.4 2.1 select_select_fusion.1
  8.5 7.3 all-to-all-start
  15.8 3.1 gather_fusion.1
  18.9 4.4 select_select_fusion
  23.4 3.0 all-to-all-done.offset_ref
  26.4 3.8 all-to-all-start.1
  30.2 5.9 fusion.46
  36.1 6.3 negate_select_fusion.5
  42.4 20.8 %forward_table.1 = bf16[2048,4096]{1,0:T(8,128)(2,1)} custom-call(f32[2048,32]{1,0:T(8,128)} %get-tuple-element.22.u_ref, f32[2048,32]{1,0:T(8,128)} %get-tuple-element.21.v_ref, f32[2048,128]{1,0:T(8,128)} %get-tuple-element.28.cos_ref, f32[2048,128]{1,0:T(8,128)} %get-tuple-element.27.sin_ref), custom_call_target="tpu_custom_call" | custom-call | tf_op jit(solution)/shard_map/forward_table/pallas_call | solution.py:211
  63.7 0.8 reshape.451.info_ref
  64.5 59.5 %all-to-all-done.1.feature_ref = bf16[256,64,128]{2,1,0:T(8,128)(2,1)} async-done(((bf16[256,64,128]{2,1,0:T(8,128)(2,1)}), bf16[256,64,128]{2,1,0:T(8,128)(2,1)}, u32[]{:S(2)}, u32[]{:S(2)}) %all-to-all-start.1) | async-done | bytes 4194336 | tf_op jit(solution)/shard_map/all_to_all | solution.py:351
  124.0 41.4 %encode.1.grid_ref = bf16[4096,1024]{1,0:T(8,128)(2,1)} custom-call(s32[3328]{0:T(1024)} %reshape.451.info_ref, bf16[256,64,128]{2,1,0:T(8,128)(2,1)} %all-to-all-done.1.feature_ref, bf16[256,4,128]{2,1,0:T(4,128)(2,1)} %copy-done.2), custom_call_target="tpu_custom_call" | custom-call | tf_op jit(solution)/shard_map/encode/pallas_call | solution.py:127
  165.4 22.7 %convolution_convert_fusion.1 = bf16[2048,1024]{1,0:T(8,128)(2,1)S(1)} fusion(bf16[2048,4096]{1,0:T(8,128)(2,1)} %forward_table.1, bf16[4096,1024]{1,0:T(8,128)(2,1)} %encode.1.grid_ref), kind=kOutput, calls=%fused_computation.19 | convolution fusion | flops 17181966336 | bytes 29360128 | tf_op jit(solution)/shard_map/dot_general | solution.py:294
  188.4 4.1 collective-permute-done
  192.5 1.0 fusion.8
  193.6 25.2 %collective-permute-done.1 = bf16[1,512,1024]{2,1,0:T(8,128)(2,1)S(1)} collective-permute-done((bf16[1,512,1024]{2,1,0:T(8,128)(2,1)S(1)}, bf16[1,512,1024]{2,1,0:T(8,128)(2,1)S(1)}, u32[]{:S(2)}, u32[]{:S(2)}) %collective-permute-start.1) | collective-permute-done | bytes 1048608 | tf_op jit(solution)/shard_map/ppermute | solution.py:285
  218.8 1.4 fusion.11
  220.2 28.1 %all-to-all-start.2 = ((bf16[8,64,1024]{2,1,0:T(8,128)(2,1)}), bf16[8,64,1024]{2,1,0:T(8,128)(2,1)S(1)}, u32[]{:S(2)}, u32[]{:S(2)}) async-start(bf16[8,64,1024]{2,1,0:T(8,128)(2,1)} %bitcast.27), calls=%async_computation.2 | async-start | bytes 2097152 | tf_op jit(solution)/shard_map/all_to_all | solution.py:303
  249.0 24.8 %all-to-all-done.2 = bf16[8,64,1024]{2,1,0:T(8,128)(2,1)S(1)} async-done(((bf16[8,64,1024]{2,1,0:T(8,128)(2,1)}), bf16[8,64,1024]{2,1,0:T(8,128)(2,1)S(1)}, u32[]{:S(2)}, u32[]{:S(2)}) %all-to-all-start.2) | async-done | bytes 1048608 | tf_op jit(solution)/shard_map/all_to_all | solution.py:303
  274.4 1.3 reshape.481
  276.3 8.1 %fusion.2 = f32[32,4,8,2,128]{4,3,2,1,0:T(2,128)S(1)} fusion(bf16[2,32,4,8,64,128]{5,4,3,2,1,0:T(8,128)(2,1)} %param.11, bf16[32,4,8,2,64]{4,0,2,1,3:T(8,128)(2,1)S(1)} %fusion.21), kind=kOutput, calls=%fused_computation.5 | convolution fusion | flops 33554432 | bytes 18087936 | tf_op jit(solution)/shard_map/mkzpc,mkzcr->mkzpr/dot_general | solution.py:308
  284.4 2.3 fusion.41
  286.7 1.4 maximum_bitcast_fusion
  288.1 0.8 fusion.12
  288.9 1.8 copy.78
  290.6 3.2 reshape.442
  293.9 29.6 %all_to_all.35 = bf16[8,64,1024]{2,1,0:T(8,128)(2,1)S(1)} all-to-all(bf16[8,64,1024]{2,1,0:T(8,128)(2,1)S(1)} %reshape.442), channel_id=1, replica_groups=mesh['px'=8,'py'=4] {'px'}, dimensions={0} | all-to-all | bytes 2097152 | tf_op jit(solution)/shard_map/all_to_all | solution.py:322
  324.0 23.1 %collective-permute-done.2 = bf16[1,512,1024]{2,1,0:T(8,128)(2,1)S(1)} collective-permute-done((bf16[1,512,1024]{2,1,0:T(8,128)(2,1)S(1)}, bf16[1,512,1024]{2,1,0:T(8,128)(2,1)S(1)}, u32[]{:S(2)}, u32[]{:S(2)}) %collective-permute-start.2) | collective-permute-done | bytes 1048608 | tf_op jit(solution)/shard_map/ppermute | solution.py:285
  347.1 1.6 fusion.17
  350.2 0.9 mul.388.skip_ref
  351.1 2.0 negate_select_fusion.7
  353.1 5.1 sine_multiply_fusion
  358.2 8.9 %back_table.1.table_ref = bf16[4096,2048]{1,0:T(8,128)(2,1)} custom-call(f32[32,2048]{1,0:T(8,128)} %get-tuple-element.24.u_ref, f32[32,2048]{1,0:T(8,128)} %get-tuple-element.23.v_ref, f32[128,2048]{1,0:T(8,128)} %get-tuple-element.20.cos_ref, f32[128,2048]{1,0:T(8,128)} %get-tuple-element.19.sin_ref), custom_call_target="tpu_custom_call" | custom-call | tf_op jit(solution)/shard_map/back_table/pallas_call | solution.py:235
  367.1 4.0 pad_maximum_fusion
  371.1 28.0 %layer_back.2.grid_ref = bf16[4096,1024]{1,0:T(8,128)(2,1)} custom-call(bf16[4096,2048]{1,0:T(8,128)(2,1)} %back_table.1.table_ref, bf16[2048,1024]{1,0:T(8,128)(2,1)} %bitcast.179, bf16[4096,1024]{1,0:T(8,128)(2,1)} %encode.1.grid_ref, bf16[256,256]{1,0:T(8,128)(2,1)} %mul.388.skip_ref, f32[1,256]{1,0:T(1,128)} %reshape_tile.6.bias_ref), custom_call_target="tpu_custom_call" | custom-call | tf_op jit(solution)/shard_map/layer_back/pallas_call | solution.py:267
  399.1 22.7 %convolution_convert_fusion = bf16[2048,1024]{1,0:T(8,128)(2,1)S(1)} fusion(bf16[2048,4096]{1,0:T(8,128)(2,1)} %forward_table.1, bf16[4096,1024]{1,0:T(8,128)(2,1)} %layer_back.2.grid_ref), kind=kOutput, calls=%fused_computation.18 | convolution fusion | flops 17181966336 | bytes 29360128 | tf_op jit(solution)/shard_map/dot_general | solution.py:294
  422.5 3.8 collective-permute-done.4
  426.3 1.0 fusion.9
  428.0 24.9 %collective-permute-done.5 = bf16[1,512,1024]{2,1,0:T(8,128)(2,1)S(1)} collective-permute-done((bf16[1,512,1024]{2,1,0:T(8,128)(2,1)S(1)}, bf16[1,512,1024]{2,1,0:T(8,128)(2,1)S(1)}, u32[]{:S(2)}, u32[]{:S(2)}) %collective-permute-start.5) | collective-permute-done | bytes 1048608 | tf_op jit(solution)/shard_map/ppermute | solution.py:285
  453.3 30.0 %all_to_all.36 = bf16[8,64,1024]{2,1,0:T(8,128)(2,1)S(1)} all-to-all(bf16[8,64,1024]{2,1,0:T(8,128)(2,1)S(1)} %bitcast.184), channel_id=1, replica_groups=mesh['px'=8,'py'=4] {'px'}, dimensions={0} | all-to-all | bytes 2097152 | tf_op jit(solution)/shard_map/all_to_all | solution.py:303
  483.9 1.3 reshape.486
  485.2 1.3 fusion.20
  486.6 8.1 %fusion = f32[32,4,8,2,128]{4,3,2,1,0:T(2,128)S(1)} fusion(bf16[2,32,4,8,64,128]{5,4,3,2,1,0:T(8,128)(2,1)} %param.11, bf16[32,4,8,2,64]{4,0,2,1,3:T(8,128)(2,1)S(1)} %fusion.20), kind=kOutput, calls=%fused_computation.3 | convolution fusion | flops 33554432 | bytes 18087936 | tf_op jit(solution)/shard_map/mkzpc,mkzcr->mkzpr/dot_general | solution.py:308
  494.7 2.3 fusion.39
  497.0 1.4 maximum_bitcast_fusion.1
  498.4 0.8 fusion.13
  499.2 1.8 copy.85
  500.9 3.2 reshape.448
  504.2 28.8 %all_to_all.37 = bf16[8,64,1024]{2,1,0:T(8,128)(2,1)S(1)} all-to-all(bf16[8,64,1024]{2,1,0:T(8,128)(2,1)S(1)} %reshape.448), channel_id=1, replica_groups=mesh['px'=8,'py'=4] {'px'}, dimensions={0} | all-to-all | bytes 2097152 | tf_op jit(solution)/shard_map/all_to_all | solution.py:322
  533.5 23.2 %collective-permute-done.6 = bf16[1,512,1024]{2,1,0:T(8,128)(2,1)S(1)} collective-permute-done((bf16[1,512,1024]{2,1,0:T(8,128)(2,1)S(1)}, bf16[1,512,1024]{2,1,0:T(8,128)(2,1)S(1)}, u32[]{:S(2)}, u32[]{:S(2)}) %collective-permute-start.6) | collective-permute-done | bytes 1048608 | tf_op jit(solution)/shard_map/ppermute | solution.py:285
  556.7 1.6 fusion.15
  558.9 0.9 mul.392.skip_ref
  559.8 3.0 collective-permute-done.7
  562.8 3.9 pad_maximum_fusion.1
  566.7 28.0 %layer_back.3.grid_ref = bf16[4096,1024]{1,0:T(8,128)(2,1)} custom-call(bf16[4096,2048]{1,0:T(8,128)(2,1)} %back_table.1.table_ref, bf16[2048,1024]{1,0:T(8,128)(2,1)} %bitcast.178, bf16[4096,1024]{1,0:T(8,128)(2,1)} %layer_back.2.grid_ref, bf16[256,256]{1,0:T(8,128)(2,1)} %mul.392.skip_ref, f32[1,256]{1,0:T(1,128)} %reshape_tile.7.bias_ref), custom_call_target="tpu_custom_call" | custom-call | tf_op jit(solution)/shard_map/layer_back/pallas_call | solution.py:267
  594.8 40.5 %decode.1 = bf16[256,64,128]{2,1,0:T(8,128)(2,1)} custom-call(s32[3328]{0:T(1024)} %reshape.451.info_ref, bf16[4096,1024]{1,0:T(8,128)(2,1)} %layer_back.3.grid_ref, bf16[256,4,128]{2,1,0:T(4,128)(2,1)} %copy-done.2), custom_call_target="tpu_custom_call" | custom-call | tf_op jit(solution)/shard_map/decode/pallas_call | solution.py:181
  635.2 28.4 %all-to-all-start.6 = ((bf16[256,64,128]{2,1,0:T(8,128)(2,1)}), bf16[256,64,128]{2,1,0:T(8,128)(2,1)}, u32[]{:S(2)}, u32[]{:S(2)}) async-start(bf16[256,64,128]{2,1,0:T(8,128)(2,1)} %decode.1), calls=%async_computation.6 | async-start | bytes 8388608 | tf_op jit(solution)/shard_map/all_to_all | solution.py:351
  664.4 93.0 %all-to-all-done.6 = bf16[256,64,128]{2,1,0:T(8,128)(2,1)} async-done(((bf16[256,64,128]{2,1,0:T(8,128)(2,1)}), bf16[256,64,128]{2,1,0:T(8,128)(2,1)}, u32[]{:S(2)}, u32[]{:S(2)}) %all-to-all-start.6) | async-done | bytes 4194336 | tf_op jit(solution)/shard_map/all_to_all | solution.py:351
  757.3 4.3 gather_fusion.2
  761.7 3.2 broadcast_select_fusion
  (86 shorter events, 11.9 us)
Async XLA Ops:
  0.0 15.8 %copy-start = (bf16[128,64,128]{2,1,0:T(8,128)(2,1)S(1)}, bf16[128,64,128]{2,1,0:T(8,128)(2,1)}, u32[]{:S(2)}) copy-start(bf16[128,64,128]{2,1,0:T(8,128)(2,1)} %param.7) | copy-start | bytes 6291460
  1.7 0.8 copy-start.13
  8.5 17.9 %all-to-all-start = ((bf16[256,4,128]{2,1,0:T(4,128)(2,1)}), bf16[256,4,128]{2,1,0:T(4,128)(2,1)S(1)}, u32[]{:S(2)}, u32[]{:S(2)}) async-start(bf16[256,4,128]{2,1,0:T(4,128)(2,1)} %select_select_fusion.1), calls=%async_computation | async-start | bytes 524288 | tf_op jit(solution)/shard_map/all_to_all | solution.py:351
  26.4 36.8 %copy-start.2 = (bf16[256,4,128]{2,1,0:T(4,128)(2,1)}, bf16[256,4,128]{2,1,0:T(4,128)(2,1)S(1)}, u32[]{:S(2)}) copy-start(bf16[256,4,128]{2,1,0:T(4,128)(2,1)S(1)} %all-to-all-done.offset_ref) | copy-start | bytes 786436
  26.4 97.6 %all-to-all-start.1 = ((bf16[256,64,128]{2,1,0:T(8,128)(2,1)}), bf16[256,64,128]{2,1,0:T(8,128)(2,1)}, u32[]{:S(2)}, u32[]{:S(2)}) async-start(bf16[256,64,128]{2,1,0:T(8,128)(2,1)} %select_select_fusion), calls=%async_computation.1 | async-start | bytes 8388608 | tf_op jit(solution)/shard_map/all_to_all | solution.py:351
  30.2 33.0 %copy-start.10 = (s32[32]{0:T(128)}, s32[32]{0:T(128)S(1)}, u32[]{:S(2)}) copy-start(s32[32]{0:T(128)S(1)} %iota_add_fusion) | copy-start | bytes 388
  30.2 33.0 %copy-start.7 = (pred[2048]{0:T(1024)(128)(4,1)}, pred[2048]{0:T(1024)(128)(4,1)S(1)}, u32[]{:S(2)}) copy-start(pred[2048]{0:T(1024)(128)(4,1)S(1)} %fusion.72) | copy-start | bytes 6148
  188.3 4.2 collective-permute-start
  193.6 25.3 %collective-permute-start.1 = (bf16[1,512,1024]{2,1,0:T(8,128)(2,1)S(1)}, bf16[1,512,1024]{2,1,0:T(8,128)(2,1)S(1)}, u32[]{:S(2)}, u32[]{:S(2)}) collective-permute-start(bf16[1,512,1024]{2,1,0:T(8,128)(2,1)S(1)} %slice_bitcast_fusion.6), channel_id=1, source_target_pairs={{0,2},{1,3},{2,0},{3,1},{4,6},{5,7},{6,4},{7,5},{8,10},{9,11},{10,... | collective-permute-start | bytes 3145736 | tf_op jit(solution)/shard_map/ppermute | solution.py:285
  220.2 53.6 %all-to-all-start.2 = ((bf16[8,64,1024]{2,1,0:T(8,128)(2,1)}), bf16[8,64,1024]{2,1,0:T(8,128)(2,1)S(1)}, u32[]{:S(2)}, u32[]{:S(2)}) async-start(bf16[8,64,1024]{2,1,0:T(8,128)(2,1)} %bitcast.27), calls=%async_computation.2 | async-start | bytes 2097152 | tf_op jit(solution)/shard_map/all_to_all | solution.py:303
  249.0 35.4 %copy-start.3 = (bf16[8,16,1,32,1]{3,1,0,2,4:T(8,128)(2,1)}, bf16[8,16,1,32,1]{3,1,0,2,4:T(8,128)(2,1)S(1)}, u32[]{:S(2)}) copy-start(bf16[8,16,1,32,1]{3,1,0,2,4:T(8,128)(2,1)S(1)} %get-tuple-element.29) | copy-start | bytes 24580
  249.0 35.4 %copy-start.4 = (bf16[8,16,1,32,1]{3,1,0,2,4:T(8,128)(2,1)}, bf16[8,16,1,32,1]{3,1,0,2,4:T(8,128)(2,1)S(1)}, u32[]{:S(2)}) copy-start(bf16[8,16,1,32,1]{3,1,0,2,4:T(8,128)(2,1)S(1)} %get-tuple-element.30) | copy-start | bytes 24580
  249.0 35.4 %copy-start.5 = (bf16[8,16,1,32,1]{3,1,0,2,4:T(8,128)(2,1)}, bf16[8,16,1,32,1]{3,1,0,2,4:T(8,128)(2,1)S(1)}, u32[]{:S(2)}) copy-start(bf16[8,16,1,32,1]{3,1,0,2,4:T(8,128)(2,1)S(1)} %get-tuple-element.31) | copy-start | bytes 24580
  293.9 54.8 %copy-start.12 = (f32[2,64]{1,0:T(2,128)S(1)}, f32[2,64]{1,0:T(2,128)}, u32[]{:S(2)}) copy-start(f32[2,64]{1,0:T(2,128)} %param.13) | copy-start | bytes 1540
  293.9 56.1 %copy-start.6 = (bf16[2,64,64]{2,1,0:T(8,128)(2,1)S(1)}, bf16[2,64,64]{2,1,0:T(8,128)(2,1)}, u32[]{:S(2)}) copy-start(bf16[2,64,64]{2,1,0:T(8,128)(2,1)} %param.12) | copy-start | bytes 49156
  323.5 27.7 %copy-start.8 = (pred[2048]{0:T(1024)(128)(4,1)S(1)}, pred[2048]{0:T(1024)(128)(4,1)}, u32[]{:S(2)}) copy-start(pred[2048]{0:T(1024)(128)(4,1)} %copy-done.7) | copy-start | bytes 6148
  323.5 27.7 %copy-start.11 = (s32[32]{0:T(128)S(1)}, s32[32]{0:T(128)}, u32[]{:S(2)}) copy-start(s32[32]{0:T(128)} %copy-done.10) | copy-start | bytes 388
  323.5 23.6 %collective-permute-start.2 = (bf16[1,512,1024]{2,1,0:T(8,128)(2,1)S(1)}, bf16[1,512,1024]{2,1,0:T(8,128)(2,1)S(1)}, u32[]{:S(2)}, u32[]{:S(2)}) collective-permute-start(bf16[1,512,1024]{2,1,0:T(8,128)(2,1)S(1)} %bitcast.185), channel_id=1, source_target_pairs={{0,2},{1,3},{2,0},{3,1},{4,6},{5,7},{6,4},{7,5},{8,10},{9,11},{10,... | collective-permute-start | bytes 3145736 | tf_op jit(solution)/shard_map/ppermute | solution.py:285
  348.7 18.4 %collective-permute-start.3 = (bf16[2,512,1024]{2,1,0:T(8,128)(2,1)}, bf16[2,512,1024]{2,1,0:T(8,128)(2,1)}, u32[]{:S(2)}, u32[]{:S(2)}) collective-permute-start(bf16[2,512,1024]{2,1,0:T(8,128)(2,1)} %get-tuple-element.12), channel_id=1, source_target_pairs={{0,1},{1,0},{2,3},{3,2},{4,5},{5,4},{6,7},{7,6},{8,9},{9,8},{10,11... | collective-permute-start | bytes 6291464 | tf_op jit(solution)/shard_map/ppermute | solution.py:285
  422.0 4.4 collective-permute-start.4
  427.4 25.5 %collective-permute-start.5 = (bf16[1,512,1024]{2,1,0:T(8,128)(2,1)S(1)}, bf16[1,512,1024]{2,1,0:T(8,128)(2,1)S(1)}, u32[]{:S(2)}, u32[]{:S(2)}) collective-permute-start(bf16[1,512,1024]{2,1,0:T(8,128)(2,1)S(1)} %slice_bitcast_fusion.4), channel_id=1, source_target_pairs={{0,2},{1,3},{2,0},{3,1},{4,6},{5,7},{6,4},{7,5},{8,10},{9,11},{10,... | collective-permute-start | bytes 3145736 | tf_op jit(solution)/shard_map/ppermute | solution.py:285
  504.2 54.1 %copy-start.9 = (f32[64]{0:T(128)S(1)}, f32[64]{0:T(128)}, u32[]{:S(2)}) copy-start(f32[64]{0:T(128)} %get-tuple-element.34) | copy-start | bytes 772
  532.9 23.8 %collective-permute-start.6 = (bf16[1,512,1024]{2,1,0:T(8,128)(2,1)S(1)}, bf16[1,512,1024]{2,1,0:T(8,128)(2,1)S(1)}, u32[]{:S(2)}, u32[]{:S(2)}) collective-permute-start(bf16[1,512,1024]{2,1,0:T(8,128)(2,1)S(1)} %bitcast.187), channel_id=1, source_target_pairs={{0,2},{1,3},{2,0},{3,1},{4,6},{5,7},{6,4},{7,5},{8,10},{9,11},{10,... | collective-permute-start | bytes 3145736 | tf_op jit(solution)/shard_map/ppermute | solution.py:285
  558.3 4.5 collective-permute-start.7
  635.2 28.4 %copy-start.14 = (s32[128]{0:T(128)S(1)}, s32[128]{0:T(128)}, u32[]{:S(2)}) copy-start(s32[128]{0:T(128)} %copy-done.13) | copy-start | bytes 1540
  635.2 122.1 %all-to-all-start.6 = ((bf16[256,64,128]{2,1,0:T(8,128)(2,1)}), bf16[256,64,128]{2,1,0:T(8,128)(2,1)}, u32[]{:S(2)}, u32[]{:S(2)}) async-start(bf16[256,64,128]{2,1,0:T(8,128)(2,1)} %decode.1), calls=%async_computation.6 | async-start | bytes 8388608 | tf_op jit(solution)/shard_map/all_to_all | solution.py:351
  664.3 100.5 %copy-start.1 = (bf16[128,64,128]{2,1,0:T(8,128)(2,1)S(1)}, bf16[128,64,128]{2,1,0:T(8,128)(2,1)}, u32[]{:S(2)}) copy-start(bf16[128,64,128]{2,1,0:T(8,128)(2,1)} %param.7) | copy-start | bytes 6291460

commit v2 on v1

--- a/solution.py
+++ b/solution.py
@@ -17,6 +17,8 @@
 AMPLITUDE = 0.25
 SPREAD = 4.5
 DECODE_SCALE = 0.1
+CHUNKS = 2
+WAYS = 4
 VMEM_LIMIT = 60 * 1024 * 1024
 F32 = jnp.float32
 BF16 = jnp.bfloat16
@@ -78,20 +80,21 @@
     )
 
 
-def encode_body(group, depth, steps, info_ref, feature_ref, offset_ref, out_ref, total_ref):
+def encode_body(group, depth, steps, info_ref, feature_ref, offset_ref, *refs):
+    out_refs, total_ref = refs[:-1], refs[-1]
     step = pl.program_id(0)
-    channels, points = feature_ref.shape[1:]
 
     @pl.when(step == 0)
     def _():
         total_ref[...] = jnp.zeros_like(total_ref)
 
-    def one(member, carry):
-        slot = step * group + member
-
-        @pl.when(info_ref[slot * 13 + 12] > 0)
-        def _():
-            values = block_kernel(info_ref, slot, offset_ref[member].astype(F32), points)
+    def some(turn, carry):
+        tiles = []
+        for way in range(WAYS):
+            member = turn * WAYS + way
+            values = block_kernel(
+                info_ref, step * group + member, offset_ref[member].astype(F32), offset_ref.shape[2]
+            )
             feature = feature_ref[member]
             empty = jnp.zeros_like(feature)
             pair = jnp.concatenate(
@@ -101,29 +104,44 @@
                 ],
                 axis=0,
             )
-            tiles = lax.dot_general(
-                values, pair, (((1,), (1,)), ((), ())), preferred_element_type=F32
-            )
-            tiles = tiles.astype(BF16).astype(F32)
-            for brick in range(4):
-                for cy in range(4):
-                    place = brick_place(info_ref, slot, brick, cy, depth)
-                    start = brick * 64 + cy * 16
-                    total_ref[place] = total_ref[place] + tiles[start : start + 16, :]
+            tiles.append(
+                lax.dot_general(values, pair, (((1,), (1,)), ((), ())), preferred_element_type=F32)
+            )
+        for way in range(WAYS):
+            slot = step * group + turn * WAYS + way
+            rounded = tiles[way].astype(BF16).astype(F32)
+            places = [
+                brick_place(info_ref, slot, brick, cy, depth)
+                for brick in range(4)
+                for cy in range(4)
+            ]
+            sums = [
+                total_ref[place] + rounded[16 * at : 16 * at + 16, :]
+                for at, place in enumerate(places)
+            ]
+            used = info_ref[slot * 13 + 12] > 0
+
+            @pl.when(used)
+            def _():
+                for place, value in zip(places, sums):
+                    total_ref[place] = value
 
         return carry
 
-    lax.fori_loop(0, group, one, 0)
+    lax.fori_loop(0, group // WAYS, some, 0)
 
     @pl.when(step == steps - 1)
     def _():
-        out_ref[...] = total_ref[...].astype(BF16)
+        for at, out_ref in enumerate(out_refs):
+            width = out_ref.shape[1]
+            out_ref[...] = total_ref[:, at * width : (at + 1) * width].astype(BF16)
 
 
 def encode(info, features, offsets, rows, depth, lanes):
     slots, channels, points = features.shape
     group = math.gcd(slots, 32)
     steps = slots // group
+    width = lanes // CHUNKS
     return pl.pallas_call(
         functools.partial(encode_body, group, depth, steps),
         grid_spec=pltpu.PrefetchScalarGridSpec(
@@ -133,28 +151,35 @@
                 pl.BlockSpec((group, channels, points), lambda i, info: (i, 0, 0)),
                 pl.BlockSpec((group, offsets.shape[1], points), lambda i, info: (i, 0, 0)),
             ],
-            out_specs=pl.BlockSpec((rows, lanes), lambda i, info: (0, 0)),
+            out_specs=[pl.BlockSpec((rows, width), lambda i, info: (0, 0))] * CHUNKS,
             scratch_shapes=[pltpu.VMEM((rows, lanes), F32)],
         ),
-        out_shape=jax.ShapeDtypeStruct((rows, lanes), BF16),
+        out_shape=[jax.ShapeDtypeStruct((rows, width), BF16)] * CHUNKS,
         compiler_params=pltpu.CompilerParams(vmem_limit_bytes=VMEM_LIMIT),
         name="encode",
     )(info, features, offsets)
 
 
-def decode_body(group, depth, info_ref, grid_ref, offset_ref, out_ref):
+def decode_body(group, depth, info_ref, *refs):
+    grid_refs, offset_ref, out_ref, held_ref = refs[:CHUNKS], refs[-3], refs[-2], refs[-1]
     step = pl.program_id(0)
     channels, points = out_ref.shape[1:]
 
-    def one(member, carry):
-        slot = step * group + member
-
-        @pl.when(info_ref[slot * 13 + 12] > 0)
-        def _():
+    @pl.when(step == 0)
+    def _():
+        for at, grid_ref in enumerate(grid_refs):
+            width = grid_ref.shape[1]
+            held_ref[:, at * width : (at + 1) * width] = grid_ref[...]
+
+    def some(turn, carry):
+        results = []
+        for way in range(WAYS):
+            member = turn * WAYS + way
+            slot = step * group + member
             values = block_kernel(info_ref, slot, offset_ref[member].astype(F32), points)
             cells = jnp.concatenate(
                 [
-                    grid_ref[brick_place(info_ref, slot, brick, cy, depth)]
+                    held_ref[brick_place(info_ref, slot, brick, cy, depth)]
                     for brick in range(4)
                     for cy in range(4)
                 ],
@@ -164,35 +189,32 @@
                 cells, values, (((0,), (0,)), ((), ())), preferred_element_type=F32
             )
             summed = both[:channels, :points] + both[channels:, points:]
-            out_ref[member] = (DECODE_SCALE * summed).astype(BF16)
-
-        @pl.when(info_ref[slot * 13 + 12] <= 0)
-        def _():
-            out_ref[member] = jnp.zeros((channels, points), BF16)
-
+            results.append((DECODE_SCALE * summed).astype(BF16))
+        for way in range(WAYS):
+            out_ref[turn * WAYS + way] = results[way]
         return carry
 
-    lax.fori_loop(0, group, one, 0)
-
-
-def decode(info, grid, offsets, channels, depth):
+    lax.fori_loop(0, group // WAYS, some, 0)
+
+
+def decode(info, grids, offsets, channels, depth):
     slots, rows3, points = offsets.shape
     group = math.gcd(slots, 32)
+    rows, width = grids[0].shape
     return pl.pallas_call(
         functools.partial(decode_body, group, depth),
         grid_spec=pltpu.PrefetchScalarGridSpec(
             num_scalar_prefetch=1,
             grid=(slots // group,),
-            in_specs=[
-                pl.BlockSpec(grid.shape, lambda i, info: (0, 0)),
-                pl.BlockSpec((group, rows3, points), lambda i, info: (i, 0, 0)),
-            ],
+            in_specs=[pl.BlockSpec((rows, width), lambda i, info: (0, 0))] * CHUNKS
+            + [pl.BlockSpec((group, rows3, points), lambda i, info: (i, 0, 0))],
             out_specs=pl.BlockSpec((group, channels, points), lambda i, info: (i, 0, 0)),
+            scratch_shapes=[pltpu.VMEM((rows, width * CHUNKS), BF16)],
         ),
         out_shape=jax.ShapeDtypeStruct((slots, channels, points), BF16),
         compiler_params=pltpu.CompilerParams(vmem_limit_bytes=VMEM_LIMIT),
         name="decode",
-    )(info, grid, offsets)
+    )(info, *grids, offsets)
 
 
 def forward_table_body(depth, u_ref, v_ref, cos_ref, sin_ref, out_ref):
@@ -255,15 +277,18 @@
         ).astype(BF16)
 
 
-def layer_back(table, modes, grid, skip, bias):
+def skip_tables(skip, bias, width):
+    copies = width // skip.shape[0]
+    same = jnp.eye(copies, dtype=bool)[:, None, :, None]
+    wide = jnp.where(same, skip[None, :, None, :], jnp.zeros((), skip.dtype))
+    return wide.reshape(width, width), jnp.tile(bias, copies).reshape(1, width)
+
+
+def layer_back(table, modes, grid, wide_skip, wide_bias):
     rows, lanes = grid.shape
     depth = modes.shape[0]
-    block = math.gcd(rows, 256)
-    channels = skip.shape[0]
-    copies = math.gcd(lanes // channels, 4)
-    width = copies * channels
-    wide_skip = jnp.kron(jnp.eye(copies, dtype=BF16), skip)
-    wide_bias = jnp.tile(bias, copies).reshape(1, width)
+    block = math.gcd(rows, 512)
+    width = wide_skip.shape[0]
     return pl.pallas_call(
         layer_body,
         grid=(rows // block,),
@@ -276,7 +301,12 @@
         ],
         out_specs=pl.BlockSpec((block, lanes), lambda i: (i, 0)),
         out_shape=jax.ShapeDtypeStruct((rows, lanes), BF16),
-        compiler_params=pltpu.CompilerParams(vmem_limit_bytes=VMEM_LIMIT),
+        compiler_params=pltpu.CompilerParams(vmem_limit_bytes=40 * 1024 * 1024),
+        cost_estimate=pl.CostEstimate(
+            flops=2 * rows * lanes * (depth + width),
+            bytes_accessed=2 * rows * (depth + 2 * lanes),
+            transcendentals=rows * lanes,
+        ),
         name="layer_back",
     )(table, modes, grid, wide_skip, wide_bias)
 
@@ -285,12 +315,8 @@
     return lax.ppermute(values, "py", [(i, i ^ distance) for i in range(size)])
 
 
-def spectral_modes(grid, weights, forward, first_forward, first_back_table, size):
-    rows_px = lax.axis_size("px")
-    channels = weights.shape[3]
-    ky_dev, kz_dev = weights.shape[1], weights.shape[2]
+def reduced_modes(grid, forward, size):
     lanes = grid.shape[1]
-    x_dev = lanes // channels
     held = jnp.dot(forward, grid, preferred_element_type=F32).astype(BF16)
     held = held.reshape(size, -1, lanes)
     distance = 1
@@ -299,14 +325,40 @@
         came = swap(halves[:, 1], distance, size)
         held = (halves[:, 0].astype(F32) + came.astype(F32)).astype(BF16)
         distance *= 2
-    own = held.reshape(rows_px, -1, lanes)
-    lines = lax.all_to_all(own, "px", split_axis=0, concat_axis=0, tiled=True)
-    lines = lines.reshape(rows_px, ky_dev, kz_dev, 2, x_dev, channels)
-    first_modes = jnp.einsum(
-        "skzpxc,sxpmq->mkzqc", lines, first_forward, preferred_element_type=F32
-    ).astype(BF16)
+    return held
+
+
+def gathered_modes(held, size):
+    distance = size // 2
+    while distance >= 1:
+        came = swap(held, distance, size)
+        held = jnp.stack([held, came], axis=1).reshape(-1, held.shape[1], held.shape[2])
+        distance //= 2
+    return held.reshape(-1, held.shape[2])
+
+
+def exchange_x(values):
+    return lax.all_to_all(values, "px", split_axis=0, concat_axis=0, tiled=True)
+
+
+def spectral_modes(grids, weights, forward, first_forward, first_back_table, size):
+    rows_px = lax.axis_size("px")
+    channels = weights.shape[3]
+    ky_dev, kz_dev = weights.shape[1], weights.shape[2]
+    lanes = grids[0].shape[1]
+    x_chunk = lanes // channels
+    first_modes = 0.0
+    for at, grid in enumerate(grids):
+        own = reduced_modes(grid, forward, size).reshape(rows_px, -1, lanes)
+        lines = exchange_x(own).reshape(rows_px, ky_dev, kz_dev, 2, x_chunk, channels)
+        first_modes += jnp.einsum(
+            "skzpxc,sxpmq->mkzqc",
+            lines,
+            first_forward[:, at * x_chunk : (at + 1) * x_chunk],
+            preferred_element_type=F32,
+        )
     product = jnp.einsum(
-        "mkzpc,mkzcr->mkzpr", first_modes, weights, preferred_element_type=F32
+        "mkzpc,mkzcr->mkzpr", first_modes.astype(BF16), weights, preferred_element_type=F32
     )
     mixed = jnp.stack(
         [
@@ -315,18 +367,17 @@
         ],
         axis=3,
     ).astype(BF16)
-    first_back = jnp.einsum(
-        "mkzpc,mpsxq->skzqxc", mixed, first_back_table, preferred_element_type=F32
-    ).astype(BF16)
-    first_back = first_back.reshape(rows_px, -1, lanes)
-    back = lax.all_to_all(first_back, "px", split_axis=0, concat_axis=0, tiled=True)
-    held = back.reshape(1, -1, lanes)
-    distance = size // 2
-    while distance >= 1:
-        came = swap(held, distance, size)
-        held = jnp.stack([held, came], axis=1).reshape(-1, held.shape[1], lanes)
-        distance //= 2
-    return held.reshape(-1, lanes)
+    modes = []
+    for at in range(len(grids)):
+        first_back = jnp.einsum(
+            "mkzpc,mpsxq->skzqxc",
+            mixed,
+            first_back_table[:, :, :, at * x_chunk : (at + 1) * x_chunk],
+            preferred_element_type=F32,
+        ).astype(BF16)
+        back = exchange_x(first_back.reshape(rows_px, -1, lanes))
+        modes.append(gathered_modes(back.reshape(1, -1, lanes), size))
+    return modes
 
 
 def slot_plan(block_bricks, bricks_device, slot_total, capacity):
@@ -410,15 +461,21 @@
     first_back = (
         first_matrix.transpose(2, 3, 0, 1).reshape(MODES, 2, mesh_rows, x_dev, 2).astype(BF16)
     )
-    grid = encode(info, got_features, got_notes, y_dev * NZ, NZ, x_dev * channels)
+    lanes = x_dev * channels
+    width = math.gcd(lanes // CHUNKS, 4 * channels)
+    skips = [skip_tables(skip_weights[at], skip_bias[at], width) for at in range(LAYERS)]
+    got_features, forward, back, first_forward, first_back, skips = lax.optimization_barrier(
+        (got_features, forward, back, first_forward, first_back, skips)
+    )
+    grids = encode(info, got_features, got_notes, y_dev * NZ, NZ, lanes)
     for depth_index in range(LAYERS):
         modes = spectral_modes(
-            grid, spectral_weights[depth_index], forward, first_forward, first_back, mesh_columns
+            grids, spectral_weights[depth_index], forward, first_forward, first_back, mesh_columns
         )
-        grid = layer_back(
-            back, modes, grid, skip_weights[depth_index], skip_bias[depth_index]
-        )
-    reply = decode(info, grid, got_notes, channels, NZ)
+        grids = [
+            layer_back(back, mode, grid, *skips[depth_index]) for mode, grid in zip(modes, grids)
+        ]
+    reply = decode(info, grids, got_notes, channels, NZ)
     returned = route_back(reply)
     return jnp.take(returned, slot_index, axis=0)
 

time: 770 us -> 665 us (0.86)
  blocking collectives: 88.3 us -> 17.3 us
  waiting for transfers between devices: 288 us -> 269 us
  Pallas kernels: 168 us -> 157 us
  starting transfers between devices: 70.1 us -> 59.9 us
  matrix products: 64.9 us -> 73.6 us
    all_to_all x3 -> x1, blocking collectives: 88.3 us -> 17.3 us  [exchange_x(): return lax.all_to_all(values, 'px', split_axis=0, concat_axis=0, tiled=True)]
    ppermute x8 -> x16, waiting for transfers between devices: 107 us -> 77.4 us  [swap(): return lax.ppermute(values, 'py', [(i, i ^ distance) for i in range(size)])]
    all_to_all x1 -> x7, waiting for transfers between devices: 24.8 us -> 54.1 us  [exchange_x(): return lax.all_to_all(values, 'px', split_axis=0, concat_axis=0, tiled=True)]
    all_to_all x3, starting transfers between devices: 39.5 us -> 15.4 us  [route_back(): lax.all_to_all(values, ('px', 'py'), split_axis=0, concat_axis=0, tiled=T...]
    all_to_all x3, waiting for transfers between devices: 155 us -> 138 us  [route_back(): lax.all_to_all(values, ('px', 'py'), split_axis=0, concat_axis=0, tiled=T...]
    ppermute x8 -> x16, starting transfers between devices: 2.47 us -> 12 us  [swap(): return lax.ppermute(values, 'py', [(i, i ^ distance) for i in range(size)])]
    unnamed x31 -> x33, local copies, waits for them, and re-layouts: 1.06 us -> 9.9 us
    dot_general x8 -> x14, matrix products: 64.9 us -> 73.6 us  [the longest x4 54.1 us: reduced_modes(): held = jnp.dot(forward, grid, preferred_element_type=F32).astype(BF16)]
  transfers between devices with their start and end apart: 12 -> 26, of which waited for: 11 -> 20; matrix products, arithmetic and copies ran while one was open for 4% -> 13% of each run, Pallas kernels for 4% -> 9%
where the time goes in v2:
time: 665 us; the launch traced here: 660 us
  waiting for transfers between devices  269 us (40%)
  Pallas kernels  157 us (24%)
  matrix products  73.6 us (11%)
  starting transfers between devices  59.9 us (9%)
  other arithmetic  52.5 us (8%)
  local copies, waits for them, and re-layouts  29.3 us (4%)
  blocking collectives  17.3 us (3%)
    all_to_all x3, waiting for transfers between devices, route_back(): lax.all_to_all(values, ('px', 'py'), split_axis=0, concat_axis=0, tiled=T...  138 us
    ppermute x16, waiting for transfers between devices, swap(): return lax.ppermute(values, 'py', [(i, i ^ distance) for i in range(size)])  77.4 us
    pallas_call x4, Pallas kernels, layer_back(): pl.pallas_call(layer_body, grid=(rows // block,), in_specs=[pl.BlockSpec(...  55.5 us
    dot_general x4, matrix products, reduced_modes(): held = jnp.dot(forward, grid, preferred_element_type=F32).astype(BF16)  54.1 us
    all_to_all x7, waiting for transfers between devices, exchange_x(): return lax.all_to_all(values, 'px', split_axis=0, concat_axis=0, tiled=True)  54.1 us
    pallas_call x1, Pallas kernels, encode(): pl.pallas_call(functools.partial(encode_body, group, depth, steps), grid_...  38.3 us
    pallas_call x1, Pallas kernels, decode(): pl.pallas_call(functools.partial(decode_body, group, depth), grid_spec=pl...  33.3 us
    all_to_all x7, starting transfers between devices, exchange_x(): return lax.all_to_all(values, 'px', split_axis=0, concat_axis=0, tiled=True)  32.5 us
  transfers between devices with their start and end apart: 26, of which 20 were waited for; matrix products, arithmetic and copies ran while one was open for 13% of the time, Pallas kernels for 9%

profile of v2, /device:TPU:0, one launch (start us, length us, event | category | flops | bytes accessed | tf_op | source)
XLA Modules:
  0.0 659.9 jit_solution(8704571016340625823)
XLA Ops:
  6.4 2.1 select_select_fusion.1
  8.5 7.3 %all-to-all-start = ((bf16[256,4,128]{2,1,0:T(4,128)(2,1)}), bf16[256,4,128]{2,1,0:T(4,128)(2,1)S(1)}, u32[]{:S(2)}, u32[]{:S(2)}) async-start(bf16[256,4,128]{2,1,0:T(4,128)(2,1)} %select_select_fusion.1), calls=%async_computation | async-start | bytes 524288 | tf_op jit(solution)/shard_map/all_to_all | solution.py:402
  15.8 3.1 gather_fusion.1
  18.9 4.4 select_select_fusion
  23.3 3.1 all-to-all-done.offset_ref.refs_2_
  26.4 3.7 all-to-all-start.1
  31.5 2.0 negate_select_fusion.7
  33.5 5.1 sine_multiply_fusion
  38.5 8.9 %back_table.1.table_ref = bf16[4096,2048]{1,0:T(8,128)(2,1)} custom-call(f32[32,2048]{1,0:T(8,128)} %get-tuple-element.48.u_ref, f32[32,2048]{1,0:T(8,128)} %get-tuple-element.47.v_ref, f32[128,2048]{1,0:T(8,128)} %get-tuple-element.46.cos_ref, f32[128,2048]{1,0:T(8,128)} %get-tuple-element.45.sin_ref), custom_call_target="tpu_custom_call" | custom-call | tf_op jit(solution)/shard_map/back_table/pallas_call | solution.py:257
  47.4 5.8 fusion.58
  53.2 6.3 negate_select_fusion.5
  59.5 20.8 %forward_table.1 = bf16[2048,4096]{1,0:T(8,128)(2,1)} custom-call(f32[2048,32]{1,0:T(8,128)} %get-tuple-element.50.u_ref, f32[2048,32]{1,0:T(8,128)} %get-tuple-element.49.v_ref, f32[2048,128]{1,0:T(8,128)} %get-tuple-element.54.cos_ref, f32[2048,128]{1,0:T(8,128)} %get-tuple-element.53.sin_ref), custom_call_target="tpu_custom_call" | custom-call | tf_op jit(solution)/shard_map/forward_table/pallas_call | solution.py:233
  82.1 42.0 %all-to-all-done.1.feature_ref = bf16[256,64,128]{2,1,0:T(8,128)(2,1)} async-done(((bf16[256,64,128]{2,1,0:T(8,128)(2,1)}), bf16[256,64,128]{2,1,0:T(8,128)(2,1)}, u32[]{:S(2)}, u32[]{:S(2)}) %all-to-all-start.1) | async-done | bytes 4194336 | tf_op jit(solution)/shard_map/all_to_all | solution.py:402
  124.0 38.3 %encode.1 = (bf16[4096,512]{1,0:T(8,128)(2,1)}, bf16[4096,512]{1,0:T(8,128)(2,1)}) custom-call(s32[3328]{0:T(1024)} %reshape.529.info_ref, bf16[256,64,128]{2,1,0:T(8,128)(2,1)} %all-to-all-done.1.feature_ref, bf16[256,4,128]{2,1,0:T(4,128)(2,1)} %copy-done.11), custom_call_target="tpu_custom_call" | custom-call | tf_op jit(solution)/shard_map/encode/pallas_call | solution.py:145
  162.3 13.9 %convolution_convert_fusion.2 = bf16[2048,512]{1,0:T(8,128)(2,1)S(1)} fusion(bf16[2048,4096]{1,0:T(8,128)(2,1)} %forward_table.1, bf16[4096,512]{1,0:T(8,128)(2,1)} %get-tuple-element.22.grid_ref), kind=kOutput, calls=%fused_computation.12 | convolution fusion | flops 8590983168 | bytes 23068672 | tf_op jit(solution)/shard_map/dot_general | solution.py:320
  176.4 12.4 %convolution_convert_fusion.3 = bf16[2048,512]{1,0:T(8,128)(2,1)S(1)} fusion(bf16[2048,4096]{1,0:T(8,128)(2,1)} %forward_table.1, bf16[4096,512]{1,0:T(8,128)(2,1)S(1)} %copy-done.4), kind=kOutput, calls=%fused_computation.13 | convolution fusion | flops 8590983168 | bytes 23068672 | tf_op jit(solution)/shard_map/dot_general | solution.py:320
  192.0 11.7 %collective-permute-done.3 = bf16[1,512,512]{2,1,0:T(8,128)(2,1)S(1)} collective-permute-done((bf16[1,512,512]{2,1,0:T(8,128)(2,1)S(1)}, bf16[1,512,512]{2,1,0:T(8,128)(2,1)S(1)}, u32[]{:S(2)}, u32[]{:S(2)}) %collective-permute-start.3) | collective-permute-done | bytes 524320 | tf_op jit(solution)/shard_map/ppermute | solution.py:315
  204.6 3.8 all-to-all-start.3
  208.5 1.7 collective-permute-start.1
  210.2 11.5 %collective-permute-done.1 = bf16[1,512,512]{2,1,0:T(8,128)(2,1)S(1)} collective-permute-done((bf16[1,512,512]{2,1,0:T(8,128)(2,1)S(1)}, bf16[1,512,512]{2,1,0:T(8,128)(2,1)S(1)}, u32[]{:S(2)}, u32[]{:S(2)}) %collective-permute-start.1) | collective-permute-done | bytes 524320 | tf_op jit(solution)/shard_map/ppermute | solution.py:315
  222.7 6.1 all-to-all-start.2
  229.6 12.0 %all-to-all-done.2 = bf16[8,64,512]{2,1,0:T(8,128)(2,1)S(1)} async-done(((bf16[8,64,512]{2,1,0:T(8,128)(2,1)}), bf16[8,64,512]{2,1,0:T(8,128)(2,1)S(1)}, u32[]{:S(2)}, u32[]{:S(2)}) %all-to-all-start.2) | async-done | bytes 524320 | tf_op jit(solution)/shard_map/all_to_all | solution.py:341
  243.2 8.0 %fusion.2 = f32[32,4,8,2,128]{4,3,2,1,0:T(2,128)S(1)} fusion(bf16[2,32,4,8,64,128]{5,4,3,2,1,0:T(8,128)(2,1)} %param.11, bf16[32,4,8,2,64]{4,0,2,1,3:T(8,128)(2,1)S(1)} %fusion.19), kind=kOutput, calls=%fused_computation.5 | convolution fusion | flops 33554432 | bytes 18087936 | tf_op jit(solution)/shard_map/mkzpc,mkzcr->mkzpr/dot_general | solution.py:360
  251.2 2.3 fusion.55
  253.6 1.4 maximum_bitcast_fusion
  256.3 17.3 %all_to_all.55 = bf16[8,64,512]{2,1,0:T(8,128)(2,1)} all-to-all(bf16[8,64,512]{2,1,0:T(8,128)(2,1)S(1)} %reshape.517), channel_id=1, replica_groups=mesh['px'=8,'py'=4] {'px'}, dimensions={0} | all-to-all | bytes 1048576 | tf_op jit(solution)/shard_map/all_to_all | solution.py:341
  275.0 1.4 reshape.511
  276.4 3.8 all-to-all-start.4
  280.2 6.0 collective-permute-done.8
  287.7 6.4 all-to-all-done.4
  295.3 10.9 %collective-permute-done.4 = bf16[1,512,512]{2,1,0:T(8,128)(2,1)S(1)} collective-permute-done((bf16[1,512,512]{2,1,0:T(8,128)(2,1)S(1)}, bf16[1,512,512]{2,1,0:T(8,128)(2,1)S(1)}, u32[]{:S(2)}, u32[]{:S(2)}) %collective-permute-start.4) | collective-permute-done | bytes 524320 | tf_op jit(solution)/shard_map/ppermute | solution.py:315
  306.5 1.6 pad_maximum_fusion.1
  308.9 13.8 %layer_back.5.grid_ref = bf16[4096,512]{1,0:T(8,128)(2,1)S(1)} custom-call(bf16[4096,2048]{1,0:T(8,128)(2,1)} %back_table.1.table_ref, bf16[2048,512]{1,0:T(8,128)(2,1)S(1)} %bitcast.302, bf16[4096,512]{1,0:T(8,128)(2,1)S(1)} %copy-done.6, bf16[256,256]{1,0:T(8,128)(2,1)S(1)} %select_n.323.skip_ref, f32[1,256]{1,0:T(1,128)S(1)} %reshape_tile.6.bias_ref), custom_call_target="tpu_custom_call" | custom-call | flops 9663676416 | bytes 25165824 | tf_op jit(solution)/shard_map/layer_back/pallas_call | solution.py:292
  322.8 13.9 %convolution_convert_fusion = bf16[2048,512]{1,0:T(8,128)(2,1)S(1)} fusion(bf16[2048,4096]{1,0:T(8,128)(2,1)} %forward_table.1, bf16[4096,512]{1,0:T(8,128)(2,1)S(1)} %layer_back.5.grid_ref), kind=kOutput, calls=%fused_computation.10 | convolution fusion | flops 8590983168 | bytes 23068672 | tf_op jit(solution)/shard_map/dot_general | solution.py:320
  337.5 2.0 copy-done.5
  339.5 13.8 %layer_back.4.grid_ref = bf16[4096,512]{1,0:T(8,128)(2,1)S(1)} custom-call(bf16[4096,2048]{1,0:T(8,128)(2,1)} %back_table.1.table_ref, bf16[2048,512]{1,0:T(8,128)(2,1)S(1)} %bitcast.301, bf16[4096,512]{1,0:T(8,128)(2,1)S(1)} %copy-done.5, bf16[256,256]{1,0:T(8,128)(2,1)S(1)} %select_n.323.skip_ref, f32[1,256]{1,0:T(1,128)S(1)} %reshape_tile.6.bias_ref), custom_call_target="tpu_custom_call" | custom-call | flops 9663676416 | bytes 25165824 | tf_op jit(solution)/shard_map/layer_back/pallas_call | solution.py:292
  353.4 13.9 %convolution_convert_fusion.1 = bf16[2048,512]{1,0:T(8,128)(2,1)S(1)} fusion(bf16[2048,4096]{1,0:T(8,128)(2,1)} %forward_table.1, bf16[4096,512]{1,0:T(8,128)(2,1)S(1)} %layer_back.4.grid_ref), kind=kOutput, calls=%fused_computation.11 | convolution fusion | flops 8590983168 | bytes 23068672 | tf_op jit(solution)/shard_map/dot_general | solution.py:320
  367.8 1.4 collective-permute-start.11
  370.4 11.8 %collective-permute-done.11 = bf16[1,512,512]{2,1,0:T(8,128)(2,1)S(1)} collective-permute-done((bf16[1,512,512]{2,1,0:T(8,128)(2,1)S(1)}, bf16[1,512,512]{2,1,0:T(8,128)(2,1)S(1)}, u32[]{:S(2)}, u32[]{:S(2)}) %collective-permute-start.11) | collective-permute-done | bytes 524320 | tf_op jit(solution)/shard_map/ppermute | solution.py:315
  383.1 4.7 all-to-all-start.7
  387.9 1.4 collective-permute-start.7
  389.3 11.9 %collective-permute-done.7 = bf16[1,512,512]{2,1,0:T(8,128)(2,1)S(1)} collective-permute-done((bf16[1,512,512]{2,1,0:T(8,128)(2,1)S(1)}, bf16[1,512,512]{2,1,0:T(8,128)(2,1)S(1)}, u32[]{:S(2)}, u32[]{:S(2)}) %collective-permute-start.7) | collective-permute-done | bytes 524320 | tf_op jit(solution)/shard_map/ppermute | solution.py:315
  402.2 5.9 all-to-all-start.5
  408.9 12.0 %all-to-all-done.5 = bf16[8,64,512]{2,1,0:T(8,128)(2,1)S(1)} async-done(((bf16[8,64,512]{2,1,0:T(8,128)(2,1)}), bf16[8,64,512]{2,1,0:T(8,128)(2,1)S(1)}, u32[]{:S(2)}, u32[]{:S(2)}) %all-to-all-start.5) | async-done | bytes 524320 | tf_op jit(solution)/shard_map/all_to_all | solution.py:341
  422.4 8.1 %fusion = f32[32,4,8,2,128]{4,3,2,1,0:T(2,128)S(1)} fusion(bf16[2,32,4,8,64,128]{5,4,3,2,1,0:T(8,128)(2,1)} %param.11, bf16[32,4,8,2,64]{4,0,2,1,3:T(8,128)(2,1)S(1)} %fusion.18), kind=kOutput, calls=%fused_computation.3 | convolution fusion | flops 33554432 | bytes 18087936 | tf_op jit(solution)/shard_map/mkzpc,mkzcr->mkzpr/dot_general | solution.py:360
  430.5 2.3 fusion.53
  434.9 1.4 reshape.526
  436.3 4.1 all-to-all-start.9
  441.2 1.4 reshape.523
  442.6 11.3 %all-to-all-done.9 = bf16[8,64,512]{2,1,0:T(8,128)(2,1)} async-done(((bf16[8,64,512]{2,1,0:T(8,128)(2,1)}), bf16[8,64,512]{2,1,0:T(8,128)(2,1)}, u32[]{:S(2)}, u32[]{:S(2)}) %all-to-all-start.9) | async-done | bytes 524320 | tf_op jit(solution)/shard_map/all_to_all | solution.py:341
  453.9 4.0 all-to-all-start.8
  459.2 12.3 %all-to-all-done.8 = bf16[8,64,512]{2,1,0:T(8,128)(2,1)S(1)} async-done(((bf16[8,64,512]{2,1,0:T(8,128)(2,1)}), bf16[8,64,512]{2,1,0:T(8,128)(2,1)S(1)}, u32[]{:S(2)}, u32[]{:S(2)}) %all-to-all-start.8) | async-done | bytes 524320 | tf_op jit(solution)/shard_map/all_to_all | solution.py:341
  474.1 9.6 %collective-permute-done.12 = bf16[1,512,512]{2,1,0:T(8,128)(2,1)S(1)} collective-permute-done((bf16[1,512,512]{2,1,0:T(8,128)(2,1)S(1)}, bf16[1,512,512]{2,1,0:T(8,128)(2,1)S(1)}, u32[]{:S(2)}, u32[]{:S(2)}) %collective-permute-start.12) | collective-permute-done | bytes 524320 | tf_op jit(solution)/shard_map/ppermute | solution.py:315
  484.2 2.4 collective-permute-done.13
  486.8 2.0 copy-done.8
  488.8 14.0 %layer_back.7.refs_1_ = bf16[4096,512]{1,0:T(8,128)(2,1)S(1)} custom-call(bf16[4096,2048]{1,0:T(8,128)(2,1)} %back_table.1.table_ref, bf16[2048,512]{1,0:T(8,128)(2,1)S(1)} %bitcast.299, bf16[4096,512]{1,0:T(8,128)(2,1)S(1)} %copy-done.8, bf16[256,256]{1,0:T(8,128)(2,1)S(1)} %select_n.325.skip_ref, f32[1,256]{1,0:T(1,128)S(1)} %reshape_tile.7.bias_ref), custom_call_target="tpu_custom_call" | custom-call | flops 9663676416 | bytes 25165824 | tf_op jit(solution)/shard_map/layer_back/pallas_call | solution.py:292
  502.8 2.0 copy-done.2
  504.8 13.8 %layer_back.6.refs_0_ = bf16[4096,512]{1,0:T(8,128)(2,1)S(1)} custom-call(bf16[4096,2048]{1,0:T(8,128)(2,1)} %back_table.1.table_ref, bf16[2048,512]{1,0:T(8,128)(2,1)S(1)} %bitcast.300, bf16[4096,512]{1,0:T(8,128)(2,1)S(1)} %copy-done.10, bf16[256,256]{1,0:T(8,128)(2,1)S(1)} %select_n.325.skip_ref, f32[1,256]{1,0:T(1,128)S(1)} %reshape_tile.7.bias_ref), custom_call_target="tpu_custom_call" | custom-call | flops 9663676416 | bytes 25165824 | tf_op jit(solution)/shard_map/layer_back/pallas_call | solution.py:292
  518.7 2.0 copy-done.3
  520.7 33.3 %decode.1 = bf16[256,64,128]{2,1,0:T(8,128)(2,1)} custom-call(s32[3328]{0:T(1024)} %reshape.529.info_ref, bf16[4096,512]{1,0:T(8,128)(2,1)} %copy-done.3, bf16[4096,512]{1,0:T(8,128)(2,1)} %copy-done.2, bf16[256,4,128]{2,1,0:T(4,128)(2,1)} %copy-done.11), custom_call_target="tpu_custom_call" | custom-call | tf_op jit(solution)/shard_map/decode/pallas_call | solution.py:204
  553.9 4.4 all-to-all-start.10
  559.0 93.0 %all-to-all-done.10 = bf16[256,64,128]{2,1,0:T(8,128)(2,1)} async-done(((bf16[256,64,128]{2,1,0:T(8,128)(2,1)}), bf16[256,64,128]{2,1,0:T(8,128)(2,1)}, u32[]{:S(2)}, u32[]{:S(2)}) %all-to-all-start.10) | async-done | bytes 4194336 | tf_op jit(solution)/shard_map/all_to_all | solution.py:402
  652.0 4.3 gather_fusion.2
  656.3 3.3 broadcast_select_fusion
  (143 shorter events, 38.3 us)
Async XLA Ops:
  0.0 15.8 %copy-start = (bf16[128,64,128]{2,1,0:T(8,128)(2,1)S(1)}, bf16[128,64,128]{2,1,0:T(8,128)(2,1)}, u32[]{:S(2)}) copy-start(bf16[128,64,128]{2,1,0:T(8,128)(2,1)} %param.7) | copy-start | bytes 6291460
  1.7 0.8 copy-start.14
  8.5 17.9 %all-to-all-start = ((bf16[256,4,128]{2,1,0:T(4,128)(2,1)}), bf16[256,4,128]{2,1,0:T(4,128)(2,1)S(1)}, u32[]{:S(2)}, u32[]{:S(2)}) async-start(bf16[256,4,128]{2,1,0:T(4,128)(2,1)} %select_select_fusion.1), calls=%async_computation | async-start | bytes 524288 | tf_op jit(solution)/shard_map/all_to_all | solution.py:402
  23.3 7.2 %copy-start.12 = (bf16[2,64,64]{2,1,0:T(8,128)(2,1)S(1)}, bf16[2,64,64]{2,1,0:T(8,128)(2,1)}, u32[]{:S(2)}) copy-start(bf16[2,64,64]{2,1,0:T(8,128)(2,1)} %param.12) | copy-start | bytes 49156
  23.3 7.9 %copy-start.13 = (f32[2,64]{1,0:T(2,128)S(1)}, f32[2,64]{1,0:T(2,128)}, u32[]{:S(2)}) copy-start(f32[2,64]{1,0:T(2,128)} %param.13) | copy-start | bytes 1540
  26.4 54.4 %copy-start.11 = (bf16[256,4,128]{2,1,0:T(4,128)(2,1)}, bf16[256,4,128]{2,1,0:T(4,128)(2,1)S(1)}, u32[]{:S(2)}) copy-start(bf16[256,4,128]{2,1,0:T(4,128)(2,1)S(1)} %all-to-all-done.offset_ref.refs_2_) | copy-start | bytes 786436
  26.4 97.6 %all-to-all-start.1 = ((bf16[256,64,128]{2,1,0:T(8,128)(2,1)}), bf16[256,64,128]{2,1,0:T(8,128)(2,1)}, u32[]{:S(2)}, u32[]{:S(2)}) async-start(bf16[256,64,128]{2,1,0:T(8,128)(2,1)} %select_select_fusion), calls=%async_computation.1 | async-start | bytes 8388608 | tf_op jit(solution)/shard_map/all_to_all | solution.py:402
  162.3 14.1 %copy-start.4 = (bf16[4096,512]{1,0:T(8,128)(2,1)S(1)}, bf16[4096,512]{1,0:T(8,128)(2,1)}, u32[]{:S(2)}) copy-start(bf16[4096,512]{1,0:T(8,128)(2,1)} %get-tuple-element.21.grid_ref) | copy-start | bytes 12582916
  176.3 13.1 %collective-permute-start.2 = (bf16[2,512,512]{2,1,0:T(8,128)(2,1)S(1)}, bf16[2,512,512]{2,1,0:T(8,128)(2,1)S(1)}, u32[]{:S(2)}, u32[]{:S(2)}) collective-permute-start(bf16[2,512,512]{2,1,0:T(8,128)(2,1)S(1)} %slice_bitcast_fusion.4), channel_id=1, source_target_pairs={{0,1},{1,0},{2,3},{3,2},{4,5},{5,4},{6,7},{7,6},{8,9},{9,8},{10,11... | collective-permute-start | bytes 3145736 | tf_op jit(solution)/shard_map/ppermute | solution.py:315
  188.9 2.8 collective-permute-start
  189.8 13.9 %collective-permute-start.3 = (bf16[1,512,512]{2,1,0:T(8,128)(2,1)S(1)}, bf16[1,512,512]{2,1,0:T(8,128)(2,1)S(1)}, u32[]{:S(2)}, u32[]{:S(2)}) collective-permute-start(bf16[1,512,512]{2,1,0:T(8,128)(2,1)S(1)} %slice_bitcast_fusion.12), channel_id=1, source_target_pairs={{0,2},{1,3},{2,0},{3,1},{4,6},{5,7},{6,4},{7,5},{8,10},{9,11},{10,... | collective-permute-start | bytes 1572872 | tf_op jit(solution)/shard_map/ppermute | solution.py:315
  204.6 18.1 %all-to-all-start.3 = ((bf16[8,64,512]{2,1,0:T(8,128)(2,1)}), bf16[8,64,512]{2,1,0:T(8,128)(2,1)S(1)}, u32[]{:S(2)}, u32[]{:S(2)}) async-start(bf16[8,64,512]{2,1,0:T(8,128)(2,1)} %bitcast.42), calls=%async_computation.3 | async-start | bytes 1048576 | tf_op jit(solution)/shard_map/all_to_all | solution.py:341
  208.5 13.2 %collective-permute-start.1 = (bf16[1,512,512]{2,1,0:T(8,128)(2,1)S(1)}, bf16[1,512,512]{2,1,0:T(8,128)(2,1)S(1)}, u32[]{:S(2)}, u32[]{:S(2)}) collective-permute-start(bf16[1,512,512]{2,1,0:T(8,128)(2,1)S(1)} %slice_bitcast_fusion.14), channel_id=1, source_target_pairs={{0,2},{1,3},{2,0},{3,1},{4,6},{5,7},{6,4},{7,5},{8,10},{9,11},{10,... | collective-permute-start | bytes 1572872 | tf_op jit(solution)/shard_map/ppermute | solution.py:315
  222.7 18.9 %all-to-all-start.2 = ((bf16[8,64,512]{2,1,0:T(8,128)(2,1)}), bf16[8,64,512]{2,1,0:T(8,128)(2,1)S(1)}, u32[]{:S(2)}, u32[]{:S(2)}) async-start(bf16[8,64,512]{2,1,0:T(8,128)(2,1)} %bitcast.31), calls=%async_computation.2 | async-start | bytes 1048576 | tf_op jit(solution)/shard_map/all_to_all | solution.py:341
  273.6 12.7 %collective-permute-start.8 = (bf16[1,512,512]{2,1,0:T(8,128)(2,1)}, bf16[1,512,512]{2,1,0:T(8,128)(2,1)}, u32[]{:S(2)}, u32[]{:S(2)}) collective-permute-start(bf16[1,512,512]{2,1,0:T(8,128)(2,1)} %bitcast.76), channel_id=1, source_target_pairs={{0,2},{1,3},{2,0},{3,1},{4,6},{5,7},{6,4},{7,5},{8,10},{9,11},{10,... | collective-permute-start | bytes 1572872 | tf_op jit(solution)/shard_map/ppermute | solution.py:315
  276.4 17.6 %all-to-all-start.4 = ((bf16[8,64,512]{2,1,0:T(8,128)(2,1)}), bf16[8,64,512]{2,1,0:T(8,128)(2,1)S(1)}, u32[]{:S(2)}, u32[]{:S(2)}) async-start(bf16[8,64,512]{2,1,0:T(8,128)(2,1)} %reshape.511), calls=%async_computation.4 | async-start | bytes 1048576 | tf_op jit(solution)/shard_map/all_to_all | solution.py:341
  287.6 18.9 %collective-permute-start.9 = (bf16[2,512,512]{2,1,0:T(8,128)(2,1)S(1)}, bf16[2,512,512]{2,1,0:T(8,128)(2,1)}, u32[]{:S(2)}, u32[]{:S(2)}) collective-permute-start(bf16[2,512,512]{2,1,0:T(8,128)(2,1)S(1)} %get-tuple-element.38), channel_id=1, source_target_pairs={{0,1},{1,0},{2,3},{3,2},{4,5},{5,4},{6,7},{7,6},{8,9},{9,8},{10,11... | collective-permute-start | bytes 3145736 | tf_op jit(solution)/shard_map/ppermute | solution.py:315
  294.0 12.2 %collective-permute-start.4 = (bf16[1,512,512]{2,1,0:T(8,128)(2,1)S(1)}, bf16[1,512,512]{2,1,0:T(8,128)(2,1)S(1)}, u32[]{:S(2)}, u32[]{:S(2)}) collective-permute-start(bf16[1,512,512]{2,1,0:T(8,128)(2,1)S(1)} %bitcast.313), channel_id=1, source_target_pairs={{0,2},{1,3},{2,0},{3,1},{4,6},{5,7},{6,4},{7,5},{8,10},{9,11},{10,... | collective-permute-start | bytes 1572872 | tf_op jit(solution)/shard_map/ppermute | solution.py:315
  306.4 31.0 %collective-permute-start.5 = (bf16[2,512,512]{2,1,0:T(8,128)(2,1)S(1)}, bf16[2,512,512]{2,1,0:T(8,128)(2,1)S(1)}, u32[]{:S(2)}, u32[]{:S(2)}) collective-permute-start(bf16[2,512,512]{2,1,0:T(8,128)(2,1)S(1)} %get-tuple-element.40), channel_id=1, source_target_pairs={{0,1},{1,0},{2,3},{3,2},{4,5},{5,4},{6,7},{7,6},{8,9},{9,8},{10,11... | collective-permute-start | bytes 3145736 | tf_op jit(solution)/shard_map/ppermute | solution.py:315
  306.4 2.5 copy-start.6
  322.8 13.9 %copy-start.7 = (bf16[4096,512]{1,0:T(8,128)(2,1)}, bf16[4096,512]{1,0:T(8,128)(2,1)S(1)}, u32[]{:S(2)}) copy-start(bf16[4096,512]{1,0:T(8,128)(2,1)S(1)} %layer_back.5.grid_ref) | copy-start | bytes 12582916
  336.8 30.7 %collective-permute-start.10 = (bf16[2,512,512]{2,1,0:T(8,128)(2,1)S(1)}, bf16[2,512,512]{2,1,0:T(8,128)(2,1)S(1)}, u32[]{:S(2)}, u32[]{:S(2)}) collective-permute-start(bf16[2,512,512]{2,1,0:T(8,128)(2,1)S(1)} %slice_bitcast_fusion), channel_id=1, source_target_pairs={{0,1},{1,0},{2,3},{3,2},{4,5},{5,4},{6,7},{7,6},{8,9},{9,8},{10,11... | collective-permute-start | bytes 3145736 | tf_op jit(solution)/shard_map/ppermute | solution.py:315
  337.3 2.2 copy-start.5
  353.4 13.9 %copy-start.9 = (bf16[4096,512]{1,0:T(8,128)(2,1)}, bf16[4096,512]{1,0:T(8,128)(2,1)S(1)}, u32[]{:S(2)}) copy-start(bf16[4096,512]{1,0:T(8,128)(2,1)S(1)} %layer_back.4.grid_ref) | copy-start | bytes 12582916
  367.4 2.7 collective-permute-start.6
  367.8 14.4 %collective-permute-start.11 = (bf16[1,512,512]{2,1,0:T(8,128)(2,1)S(1)}, bf16[1,512,512]{2,1,0:T(8,128)(2,1)S(1)}, u32[]{:S(2)}, u32[]{:S(2)}) collective-permute-start(bf16[1,512,512]{2,1,0:T(8,128)(2,1)S(1)} %slice_bitcast_fusion.8), channel_id=1, source_target_pairs={{0,2},{1,3},{2,0},{3,1},{4,6},{5,7},{6,4},{7,5},{8,10},{9,11},{10,... | collective-permute-start | bytes 1572872 | tf_op jit(solution)/shard_map/ppermute | solution.py:315
  383.1 19.0 %all-to-all-start.7 = ((bf16[8,64,512]{2,1,0:T(8,128)(2,1)}), bf16[8,64,512]{2,1,0:T(8,128)(2,1)S(1)}, u32[]{:S(2)}, u32[]{:S(2)}) async-start(bf16[8,64,512]{2,1,0:T(8,128)(2,1)} %bitcast.89), calls=%async_computation.7 | async-start | bytes 1048576 | tf_op jit(solution)/shard_map/all_to_all | solution.py:341
  387.9 13.2 %collective-permute-start.7 = (bf16[1,512,512]{2,1,0:T(8,128)(2,1)S(1)}, bf16[1,512,512]{2,1,0:T(8,128)(2,1)S(1)}, u32[]{:S(2)}, u32[]{:S(2)}) collective-permute-start(bf16[1,512,512]{2,1,0:T(8,128)(2,1)S(1)} %slice_bitcast_fusion.10), channel_id=1, source_target_pairs={{0,2},{1,3},{2,0},{3,1},{4,6},{5,7},{6,4},{7,5},{8,10},{9,11},{10,... | collective-permute-start | bytes 1572872 | tf_op jit(solution)/shard_map/ppermute | solution.py:315
  402.2 18.7 %all-to-all-start.5 = ((bf16[8,64,512]{2,1,0:T(8,128)(2,1)}), bf16[8,64,512]{2,1,0:T(8,128)(2,1)S(1)}, u32[]{:S(2)}, u32[]{:S(2)}) async-start(bf16[8,64,512]{2,1,0:T(8,128)(2,1)} %bitcast.65), calls=%async_computation.5 | async-start | bytes 1048576 | tf_op jit(solution)/shard_map/all_to_all | solution.py:341
  436.3 17.5 %all-to-all-start.9 = ((bf16[8,64,512]{2,1,0:T(8,128)(2,1)}), bf16[8,64,512]{2,1,0:T(8,128)(2,1)}, u32[]{:S(2)}, u32[]{:S(2)}) async-start(bf16[8,64,512]{2,1,0:T(8,128)(2,1)} %reshape.526), calls=%async_computation.9 | async-start | bytes 1048576 | tf_op jit(solution)/shard_map/all_to_all | solution.py:341
  453.9 17.7 %all-to-all-start.8 = ((bf16[8,64,512]{2,1,0:T(8,128)(2,1)}), bf16[8,64,512]{2,1,0:T(8,128)(2,1)S(1)}, u32[]{:S(2)}, u32[]{:S(2)}) async-start(bf16[8,64,512]{2,1,0:T(8,128)(2,1)} %reshape.523), calls=%async_computation.8 | async-start | bytes 1048576 | tf_op jit(solution)/shard_map/all_to_all | solution.py:341
  457.8 15.0 %collective-permute-start.14 = (bf16[1,512,512]{2,1,0:T(8,128)(2,1)}, bf16[1,512,512]{2,1,0:T(8,128)(2,1)S(1)}, u32[]{:S(2)}, u32[]{:S(2)}) collective-permute-start(bf16[1,512,512]{2,1,0:T(8,128)(2,1)} %bitcast.112), channel_id=1, source_target_pairs={{0,2},{1,3},{2,0},{3,1},{4,6},{5,7},{6,4},{7,5},{8,10},{9,11},{10,... | collective-permute-start | bytes 1572872 | tf_op jit(solution)/shard_map/ppermute | solution.py:315
  471.5 12.2 %collective-permute-start.12 = (bf16[1,512,512]{2,1,0:T(8,128)(2,1)S(1)}, bf16[1,512,512]{2,1,0:T(8,128)(2,1)S(1)}, u32[]{:S(2)}, u32[]{:S(2)}) collective-permute-start(bf16[1,512,512]{2,1,0:T(8,128)(2,1)S(1)} %bitcast.311), channel_id=1, source_target_pairs={{0,2},{1,3},{2,0},{3,1},{4,6},{5,7},{6,4},{7,5},{8,10},{9,11},{10,... | collective-permute-start | bytes 1572872 | tf_op jit(solution)/shard_map/ppermute | solution.py:315
  474.0 9.9 %collective-permute-start.15 = (bf16[2,512,512]{2,1,0:T(8,128)(2,1)S(1)}, bf16[2,512,512]{2,1,0:T(8,128)(2,1)S(1)}, u32[]{:S(2)}, u32[]{:S(2)}) collective-permute-start(bf16[2,512,512]{2,1,0:T(8,128)(2,1)S(1)} %get-tuple-element.32), channel_id=1, source_target_pairs={{0,1},{1,0},{2,3},{3,2},{4,5},{5,4},{6,7},{7,6},{8,9},{9,8},{10,11... | collective-permute-start | bytes 3145736 | tf_op jit(solution)/shard_map/ppermute | solution.py:315
  483.9 2.7 collective-permute-start.13
  486.6 2.2 copy-start.8
  488.8 16.0 %copy-start.10 = (bf16[4096,512]{1,0:T(8,128)(2,1)S(1)}, bf16[4096,512]{1,0:T(8,128)(2,1)}, u32[]{:S(2)}) copy-start(bf16[4096,512]{1,0:T(8,128)(2,1)} %copy-done.9) | copy-start | bytes 12582916
  502.8 2.0 copy-start.2
  518.7 2.0 copy-start.3
  553.9 4.4 copy-start.15
  553.9 98.1 %all-to-all-start.10 = ((bf16[256,64,128]{2,1,0:T(8,128)(2,1)}), bf16[256,64,128]{2,1,0:T(8,128)(2,1)}, u32[]{:S(2)}, u32[]{:S(2)}) async-start(bf16[256,64,128]{2,1,0:T(8,128)(2,1)} %decode.1), calls=%async_computation.10 | async-start | bytes 8388608 | tf_op jit(solution)/shard_map/all_to_all | solution.py:402
  656.3 3.3 copy-start.1

commit v3 on v2

--- a/solution.py
+++ b/solution.py
@@ -119,12 +119,8 @@
                 total_ref[place] + rounded[16 * at : 16 * at + 16, :]
                 for at, place in enumerate(places)
             ]
-            used = info_ref[slot * 13 + 12] > 0
-
-            @pl.when(used)
-            def _():
-                for place, value in zip(places, sums):
-                    total_ref[place] = value
+            for place, value in zip(places, sums):
+                total_ref[place] = value
 
         return carry
 
@@ -217,64 +213,83 @@
     )(info, *grids, offsets)
 
 
-def forward_table_body(depth, u_ref, v_ref, cos_ref, sin_ref, out_ref):
-    for place in range(out_ref.shape[1] // depth):
-        out_ref[:, place * depth : (place + 1) * depth] = (
-            u_ref[:, place : place + 1] * cos_ref[...] + v_ref[:, place : place + 1] * sin_ref[...]
+def forward_body(groups, third_ref, second_ref, grid_ref, out_ref, held_ref):
+    depth = third_ref.shape[1]
+    span = third_ref.shape[0] // groups
+    cells_y = grid_ref.shape[0] // depth
+    count_in, count_out = second_ref.shape[1], second_ref.shape[0]
+
+    def some(turn, carry):
+        for way in range(WAYS):
+            y = turn * WAYS + way
+            line = grid_ref[pl.ds(pl.multiple_of(y * depth, depth), depth), :]
+            modes = jnp.dot(third_ref[...], line, preferred_element_type=F32)
+            for at in range(groups):
+                row = pl.multiple_of(at * count_in + y * span, span)
+                held_ref[pl.ds(row, span), :] = modes[at * span : (at + 1) * span, :]
+        return carry
+
+    lax.fori_loop(0, cells_y // WAYS, some, 0)
+    for at in range(groups):
+        third = held_ref[at * count_in : (at + 1) * count_in, :].astype(BF16)
+        out_ref[at * count_out : (at + 1) * count_out, :] = jnp.dot(
+            second_ref[...], third, preferred_element_type=F32
         ).astype(BF16)
 
 
-def forward_table(u, v, cosine, sine):
-    modes, cells_y = u.shape
-    depth = cosine.shape[1]
-    block = math.gcd(modes, 256)
-    narrow = pl.BlockSpec((block, cells_y), lambda i: (i, 0))
-    wide = pl.BlockSpec((block, depth), lambda i: (i, 0))
+def forward_modes(third, second, grid, groups):
+    rows, lanes = grid.shape
+    count_out, count_in = second.shape
+    width = math.gcd(lanes, 256)
     return pl.pallas_call(
-        functools.partial(forward_table_body, depth),
-        grid=(modes // block,),
-        in_specs=[narrow, narrow, wide, wide],
-        out_specs=pl.BlockSpec((block, cells_y * depth), lambda i: (i, 0)),
-        out_shape=jax.ShapeDtypeStruct((modes, cells_y * depth), BF16),
-        compiler_params=pltpu.CompilerParams(vmem_limit_bytes=VMEM_LIMIT),
-        name="forward_table",
-    )(u, v, cosine, sine)
-
-
-def back_table_body(depth, u_ref, v_ref, cos_ref, sin_ref, out_ref):
-    for place in range(u_ref.shape[0]):
-        out_ref[place * depth : (place + 1) * depth, :] = (
-            u_ref[place : place + 1, :] * cos_ref[...] + v_ref[place : place + 1, :] * sin_ref[...]
-        ).astype(BF16)
-
-
-def back_table(u, v, cosine, sine):
-    cells_y, modes = u.shape
-    depth = cosine.shape[0]
-    group = math.gcd(cells_y, 8)
-    narrow = pl.BlockSpec((group, modes), lambda i: (i, 0))
-    wide = pl.BlockSpec((depth, modes), lambda i: (0, 0))
-    return pl.pallas_call(
-        functools.partial(back_table_body, depth),
-        grid=(cells_y // group,),
-        in_specs=[narrow, narrow, wide, wide],
-        out_specs=pl.BlockSpec((group * depth, modes), lambda i: (i, 0)),
-        out_shape=jax.ShapeDtypeStruct((cells_y * depth, modes), BF16),
-        compiler_params=pltpu.CompilerParams(vmem_limit_bytes=VMEM_LIMIT),
-        name="back_table",
-    )(u, v, cosine, sine)
-
-
-def layer_body(table_ref, modes_ref, grid_ref, skip_ref, bias_ref, out_ref):
-    width = skip_ref.shape[0]
-    for start in range(0, out_ref.shape[1], width):
-        lanes = slice(start, start + width)
-        spectral = jnp.dot(table_ref[...], modes_ref[:, lanes], preferred_element_type=F32)
-        skipped = jnp.dot(grid_ref[:, lanes], skip_ref[...], preferred_element_type=F32)
-        value = spectral + skipped + bias_ref[...]
-        out_ref[:, lanes] = (
-            0.5 * value * (1.0 + lax.erf(value * math.sqrt(0.5)))
-        ).astype(BF16)
+        functools.partial(forward_body, groups),
+        grid=(lanes // width,),
+        in_specs=[
+            pl.BlockSpec(third.shape, lambda i: (0, 0)),
+            pl.BlockSpec(second.shape, lambda i: (0, 0)),
+            pl.BlockSpec((rows, width), lambda i: (0, i)),
+        ],
+        out_specs=pl.BlockSpec((groups * count_out, width), lambda i: (0, i)),
+        out_shape=jax.ShapeDtypeStruct((groups * count_out, lanes), BF16),
+        scratch_shapes=[pltpu.VMEM((groups * count_in, width), F32)],
+        compiler_params=pltpu.CompilerParams(vmem_limit_bytes=40 * 1024 * 1024),
+        cost_estimate=pl.CostEstimate(
+            flops=8 * groups * lanes * count_out * count_in,
+            bytes_accessed=2 * lanes * (rows + groups * count_out),
+            transcendentals=0,
+        ),
+        name="forward_modes",
+    )(third, second, grid)
+
+
+def layer_body(groups, second_ref, third_ref, modes_ref, grid_ref, skip_ref, bias_ref, out_ref, held_ref):
+    depth = third_ref.shape[0]
+    span = third_ref.shape[1] // groups
+    cells_y = grid_ref.shape[0] // depth
+    count_out, count_in = second_ref.shape
+    for at in range(groups):
+        held_ref[at * count_out : (at + 1) * count_out, :] = jnp.dot(
+            second_ref[...],
+            modes_ref[at * count_in : (at + 1) * count_in, :],
+            preferred_element_type=F32,
+        )
+
+    def some(turn, carry):
+        for way in range(2):
+            y = turn * 2 + way
+            pieces = []
+            for at in range(groups):
+                row = pl.multiple_of(at * count_out + y * span, span)
+                pieces.append(held_ref[pl.ds(row, span), :])
+            line = jnp.concatenate(pieces, axis=0).astype(BF16)
+            place = pl.ds(pl.multiple_of(y * depth, depth), depth)
+            spectral = jnp.dot(third_ref[...], line, preferred_element_type=F32)
+            skipped = jnp.dot(grid_ref[place, :], skip_ref[...], preferred_element_type=F32)
+            value = spectral + skipped + bias_ref[...]
+            out_ref[place, :] = (0.5 * value * (1.0 + lax.erf(value * math.sqrt(0.5)))).astype(BF16)
+        return carry
+
+    lax.fori_loop(0, cells_y // 2, some, 0)
 
 
 def skip_tables(skip, bias, width):
@@ -284,31 +299,32 @@
     return wide.reshape(width, width), jnp.tile(bias, copies).reshape(1, width)
 
 
-def layer_back(table, modes, grid, wide_skip, wide_bias):
+def layer_back(second, third, modes, grid, wide_skip, wide_bias, groups):
     rows, lanes = grid.shape
     depth = modes.shape[0]
-    block = math.gcd(rows, 512)
     width = wide_skip.shape[0]
     return pl.pallas_call(
-        layer_body,
-        grid=(rows // block,),
+        functools.partial(layer_body, groups),
+        grid=(lanes // width,),
         in_specs=[
-            pl.BlockSpec((block, depth), lambda i: (i, 0)),
-            pl.BlockSpec((depth, lanes), lambda i: (0, 0)),
-            pl.BlockSpec((block, lanes), lambda i: (i, 0)),
+            pl.BlockSpec(second.shape, lambda i: (0, 0)),
+            pl.BlockSpec(third.shape, lambda i: (0, 0)),
+            pl.BlockSpec((depth, width), lambda i: (0, i)),
+            pl.BlockSpec((rows, width), lambda i: (0, i)),
             pl.BlockSpec((width, width), lambda i: (0, 0)),
             pl.BlockSpec((1, width), lambda i: (0, 0)),
         ],
-        out_specs=pl.BlockSpec((block, lanes), lambda i: (i, 0)),
+        out_specs=pl.BlockSpec((rows, width), lambda i: (0, i)),
         out_shape=jax.ShapeDtypeStruct((rows, lanes), BF16),
+        scratch_shapes=[pltpu.VMEM((groups * second.shape[0], width), F32)],
         compiler_params=pltpu.CompilerParams(vmem_limit_bytes=40 * 1024 * 1024),
         cost_estimate=pl.CostEstimate(
-            flops=2 * rows * lanes * (depth + width),
+            flops=2 * rows * lanes * depth,
             bytes_accessed=2 * rows * (depth + 2 * lanes),
             transcendentals=rows * lanes,
         ),
         name="layer_back",
-    )(table, modes, grid, wide_skip, wide_bias)
+    )(second, third, modes, grid, wide_skip, wide_bias)
 
 
 def swap(values, distance, size):
@@ -317,7 +333,7 @@
 
 def reduced_modes(grid, forward, size):
     lanes = grid.shape[1]
-    held = jnp.dot(forward, grid, preferred_element_type=F32).astype(BF16)
+    held = forward_modes(*forward, grid, size)
     held = held.reshape(size, -1, lanes)
     distance = 1
     while distance < size:
@@ -437,25 +453,27 @@
     info = got_notes[:, 3, :13].astype(jnp.int32).reshape(-1)
 
     kz_dev = MODES // mesh_columns
-    me_x, me_y = lax.axis_index("px"), lax.axis_index("py")
-    index = jnp.arange(2 * MODES * MODES, dtype=jnp.int32)
-    part = index % 2
-    kz = index // 2 % kz_dev + kz_dev * jnp.bitwise_xor(index // (2 * kz_dev * MODES), me_y)
-    ky_at = index // (2 * kz_dev) % MODES
+    me_y = lax.axis_index("py")
+    index = jnp.arange(2 * MODES, dtype=jnp.int32)
+    group_at = jnp.bitwise_xor(index // (2 * kz_dev), me_y)
+    kz = index // 2 % kz_dev + kz_dev * group_at
+    angle_z = unit_angles(kz[:, None] * jnp.arange(NZ, dtype=jnp.int32)[None, :], NZ)
+    third = jnp.where((index % 2 == 0)[:, None], jnp.cos(angle_z), -jnp.sin(angle_z))
+    third = third / math.sqrt(NZ)
+    fold = jnp.where(kz == 0, 1.0, 2.0).astype(F32)[:, None]
+    third_back = (third * fold).T.astype(BF16)
+    span = 2 * kz_dev
+    row = jnp.arange(MODES * span, dtype=jnp.int32)[:, None]
+    column = jnp.arange(y_dev * span, dtype=jnp.int32)[None, :]
+    ky_at = row // span
     ky = jnp.where(ky_at < MODES // 2, ky_at, ky_at - MODES)
-    angle_y = unit_angles(
-        ky[:, None] * (me_y * y_dev + jnp.arange(y_dev, dtype=jnp.int32))[None, :], NY
-    )
-    angle_z = unit_angles(kz[:, None] * jnp.arange(NZ, dtype=jnp.int32)[None, :], NZ)
-    real_row = (part == 0)[:, None]
-    norm = 1.0 / math.sqrt(NY * NZ)
-    cos_y, sin_y = jnp.cos(angle_y) * norm, jnp.sin(angle_y) * norm
-    table_u = jnp.where(real_row, cos_y, -sin_y)
-    table_v = jnp.where(real_row, -sin_y, -cos_y)
-    cos_z, sin_z = jnp.cos(angle_z), jnp.sin(angle_z)
-    forward = forward_table(table_u, table_v, cos_z, sin_z)
-    fold = jnp.where(kz == 0, 1.0, 2.0).astype(F32)[:, None]
-    back = back_table(table_u.T, table_v.T, (cos_z * fold).T, (sin_z * fold).T)
+    angle_y = unit_angles(ky * (me_y * y_dev + column // span), NY)
+    row_part, column_part = row % 2, column % 2
+    sine = jnp.where(row_part == 0, jnp.sin(angle_y), -jnp.sin(angle_y))
+    second = jnp.where(row_part == column_part, jnp.cos(angle_y), sine) / math.sqrt(NY)
+    second = jnp.where(row % span // 2 == column % span // 2, second, 0.0).astype(BF16)
+    forward = (third.astype(BF16), second)
+    back = (second.T, third_back)
     first_matrix = forward_matrix(NX, wave_numbers(MODES))
     first_forward = first_matrix.reshape(mesh_rows, x_dev, 2, MODES, 2).astype(BF16)
     first_back = (
@@ -473,7 +491,8 @@
             grids, spectral_weights[depth_index], forward, first_forward, first_back, mesh_columns
         )
         grids = [
-            layer_back(back, mode, grid, *skips[depth_index]) for mode, grid in zip(modes, grids)
+            layer_back(*back, mode, grid, *skips[depth_index], mesh_columns)
+            for mode, grid in zip(modes, grids)
         ]
     reply = decode(info, grids, got_notes, channels, NZ)
     returned = route_back(reply)

time: 665 us -> 620 us (0.932)
  matrix products: 73.6 us -> 19.5 us
  waiting for transfers between devices: 269 us -> 306 us
  Pallas kernels: 157 us -> 129 us
  local copies, waits for them, and re-layouts: 29.3 us -> 38.7 us
  other arithmetic: 52.5 us -> 44.1 us
    dot_general x4 -> x0, matrix products: 54.1 us -> none  [reduced_modes(): held = jnp.dot(forward, grid, preferred_element_type=F32).astype(BF16)]
    all_to_all x3, waiting for transfers between devices: 138 us -> 177 us  [route_back(): lax.all_to_all(values, ('px', 'py'), split_axis=0, concat_axis=0, tiled=T...]
    pallas_call x6 -> x8, Pallas kernels: 85.2 us -> 61.4 us  [the longest x4 42.4 us: layer_back(): pl.pallas_call(functools.partial(layer_body, groups), grid=(lanes // widt...]
    convert_element_type x0 -> x3, other arithmetic: none -> 9.78 us  [the longest x1 9.28 us: per_device(): jnp.where(row % span // 2 == column % span // 2, second, 0.0).astype(BF16)]
    select_n x3 -> x1, other arithmetic: 8.3 us -> 0.01 us  [per_device(): row % span // 2 == column % span // 2]
    unnamed x33 -> x37, local copies, waits for them, and re-layouts: 9.9 us -> 14.6 us
  transfers between devices with their start and end apart: 26 -> 26, of which waited for: 20 -> 20; matrix products, arithmetic and copies ran while one was open for 13% -> 6% of each run, Pallas kernels for 9% -> 6%
where the time goes in v3:
time: 620 us; the launch traced here: 615 us
  waiting for transfers between devices  306 us (49%)
  Pallas kernels  129 us (21%)
  starting transfers between devices  58.6 us (9%)
  other arithmetic  44.1 us (7%)
  local copies, waits for them, and re-layouts  38.7 us (6%)
  matrix products  19.5 us (3%)
  blocking collectives  17.5 us (3%)
    all_to_all x3, waiting for transfers between devices, route_back(): lax.all_to_all(values, ('px', 'py'), split_axis=0, concat_axis=0, tiled=T...  177 us
    ppermute x16, waiting for transfers between devices, swap(): return lax.ppermute(values, 'py', [(i, i ^ distance) for i in range(size)])  76.6 us
    all_to_all x7, waiting for transfers between devices, exchange_x(): return lax.all_to_all(values, 'px', split_axis=0, concat_axis=0, tiled=True)  52.1 us
    pallas_call x4, Pallas kernels, layer_back(): pl.pallas_call(functools.partial(layer_body, groups), grid=(lanes // widt...  42.4 us
    pallas_call x1, Pallas kernels, encode(): pl.pallas_call(functools.partial(encode_body, group, depth, steps), grid_...  34.7 us
    pallas_call x1, Pallas kernels, decode(): pl.pallas_call(functools.partial(decode_body, group, depth), grid_spec=pl...  33.3 us
    all_to_all x7, starting transfers between devices, exchange_x(): return lax.all_to_all(values, 'px', split_axis=0, concat_axis=0, tiled=True)  31.7 us
    pallas_call x4, Pallas kernels, forward_modes(): pl.pallas_call(functools.partial(forward_body, groups), grid=(lanes // wi...  19 us
  transfers between devices with their start and end apart: 26, of which 20 were waited for; matrix products, arithmetic and copies ran while one was open for 6% of the time, Pallas kernels for 6%

profile of v3, /device:TPU:0, one launch (start us, length us, event | category | flops | bytes accessed | tf_op | source)
XLA Modules:
  0.0 614.6 jit_solution(13720343396788028602)
XLA Ops:
  6.4 2.1 select_select_fusion.1
  8.5 7.3 %all-to-all-start = ((bf16[256,4,128]{2,1,0:T(4,128)(2,1)}), bf16[256,4,128]{2,1,0:T(4,128)(2,1)S(1)}, u32[]{:S(2)}, u32[]{:S(2)}) async-start(bf16[256,4,128]{2,1,0:T(4,128)(2,1)} %select_select_fusion.1), calls=%async_computation | async-start | bytes 524288 | tf_op jit(solution)/shard_map/all_to_all | solution.py:418
  15.8 3.1 gather_fusion.1
  18.9 4.4 select_select_fusion
  23.3 3.1 all-to-all-done.offset_ref.refs_2_
  26.4 3.7 all-to-all-start.1
  32.4 9.3 %fusion.31 = (bf16[512,512]{1,0:T(8,128)(2,1)S(1)}, bf16[512,512]{1,0:T(8,128)(2,1)S(1)}) fusion(s32[512]{0:T(512)S(1)} %get-tuple-element.68, s32[512]{0:T(512)S(1)} %get-tuple-element.65, s32[512]{0:T(512)S(1)} %get-tuple-element.66, s32[512]{0:T(512)S(1)} %get-tuple-element.67, pred[512]{0:T(512)(128)(4,1)S(1)} %broadcast_compare_fusion), kind=kLoop, calls=%fused_computation.64 | loop fusion | flops 11534336 | bytes 1057280 | tf_op jit(solution)/shard_map/convert_element_type | solution.py:474
  43.0 81.0 %all-to-all-done.1.feature_ref = bf16[256,64,128]{2,1,0:T(8,128)(2,1)} async-done(((bf16[256,64,128]{2,1,0:T(8,128)(2,1)}), bf16[256,64,128]{2,1,0:T(8,128)(2,1)}, u32[]{:S(2)}, u32[]{:S(2)}) %all-to-all-start.1) | async-done | bytes 4194336 | tf_op jit(solution)/shard_map/all_to_all | solution.py:418
  124.0 34.7 %encode.1 = (bf16[4096,512]{1,0:T(8,128)(2,1)}, bf16[4096,512]{1,0:T(8,128)(2,1)}) custom-call(s32[3328]{0:T(1024)} %reshape.710.info_ref, bf16[256,64,128]{2,1,0:T(8,128)(2,1)} %all-to-all-done.1.feature_ref, bf16[256,4,128]{2,1,0:T(4,128)(2,1)} %copy-done.13), custom_call_target="tpu_custom_call" | custom-call | tf_op jit(solution)/shard_map/encode/pallas_call | solution.py:141
  158.8 2.2 copy-done.6
  160.9 4.7 forward_modes.5
  165.9 4.8 forward_modes.4
  173.8 11.7 %collective-permute-done.3 = bf16[1,512,512]{2,1,0:T(8,128)(2,1)S(1)} collective-permute-done((bf16[1,512,512]{2,1,0:T(8,128)(2,1)S(1)}, bf16[1,512,512]{2,1,0:T(8,128)(2,1)S(1)}, u32[]{:S(2)}, u32[]{:S(2)}) %collective-permute-start.3) | collective-permute-done | bytes 524320 | tf_op jit(solution)/shard_map/ppermute | solution.py:331
  186.4 3.6 all-to-all-start.3
  190.1 1.8 collective-permute-start.1
  191.9 11.3 %collective-permute-done.1 = bf16[1,512,512]{2,1,0:T(8,128)(2,1)S(1)} collective-permute-done((bf16[1,512,512]{2,1,0:T(8,128)(2,1)S(1)}, bf16[1,512,512]{2,1,0:T(8,128)(2,1)S(1)}, u32[]{:S(2)}, u32[]{:S(2)}) %collective-permute-start.1) | collective-permute-done | bytes 524320 | tf_op jit(solution)/shard_map/ppermute | solution.py:331
  205.0 5.8 all-to-all-start.2
  210.9 1.3 copy.111
  212.2 1.5 reshape.747
  213.7 9.8 %all-to-all-done.2 = bf16[8,64,512]{2,1,0:T(8,128)(2,1)S(1)} async-done(((bf16[8,64,512]{2,1,0:T(8,128)(2,1)}), bf16[8,64,512]{2,1,0:T(8,128)(2,1)S(1)}, u32[]{:S(2)}, u32[]{:S(2)}) %all-to-all-start.2) | async-done | bytes 524320 | tf_op jit(solution)/shard_map/all_to_all | solution.py:357
  226.0 8.0 %fusion.2 = f32[32,4,8,2,128]{4,3,2,1,0:T(2,128)S(1)} fusion(bf16[2,32,4,8,64,128]{5,4,3,2,1,0:T(8,128)(2,1)} %param.11, bf16[32,4,8,2,64]{4,0,2,1,3:T(8,128)(2,1)S(1)} %fusion.19), kind=kOutput, calls=%fused_computation.5 | convolution fusion | flops 33554432 | bytes 18087936 | tf_op jit(solution)/shard_map/mkzpc,mkzcr->mkzpr/dot_general | solution.py:376
  234.0 2.3 fusion.53
  236.4 1.4 maximum_bitcast_fusion
  238.4 1.4 reshape.698
  239.9 17.5 %all_to_all.55 = bf16[8,64,512]{2,1,0:T(8,128)(2,1)} all-to-all(bf16[8,64,512]{2,1,0:T(8,128)(2,1)} %reshape.698), channel_id=1, replica_groups=mesh['px'=8,'py'=4] {'px'}, dimensions={0} | all-to-all | bytes 1048576 | tf_op jit(solution)/shard_map/all_to_all | solution.py:357
  258.9 1.4 reshape.692
  260.4 4.1 all-to-all-start.4
  264.4 5.5 collective-permute-done.8
  270.0 2.3 fusion.47
  272.3 5.9 all-to-all-done.4
  279.3 11.1 %collective-permute-done.4 = bf16[1,512,512]{2,1,0:T(8,128)(2,1)S(1)} collective-permute-done((bf16[1,512,512]{2,1,0:T(8,128)(2,1)S(1)}, bf16[1,512,512]{2,1,0:T(8,128)(2,1)S(1)}, u32[]{:S(2)}, u32[]{:S(2)}) %collective-permute-start.4) | collective-permute-done | bytes 524320 | tf_op jit(solution)/shard_map/ppermute | solution.py:331
  290.6 1.6 pad_maximum_fusion.1
  293.1 10.6 %layer_back.5.grid_ref = bf16[4096,512]{1,0:T(8,128)(2,1)S(1)} custom-call(bf16[512,512]{1,0:T(8,128)(2,1)S(1)} %get-tuple-element.18.second_ref, bf16[128,64]{1,0:T(8,128)(2,1)S(1)} %multiply_convert_fusion.1.third_ref, bf16[2048,512]{1,0:T(8,128)(2,1)S(1)} %bitcast.302, bf16[4096,512]{1,0:T(8,128)(2,1)S(1)} %copy-done.7, ...), custom_call_target="tpu_custom_call" | custom-call | flops 8589934592 | bytes 25165824 | tf_op jit(solution)/shard_map/layer_back/pallas_call | solution.py:306
  303.7 4.8 forward_modes.7
  309.4 2.0 copy-done.5
  311.4 10.6 %layer_back.4.grid_ref = bf16[4096,512]{1,0:T(8,128)(2,1)S(1)} custom-call(bf16[512,512]{1,0:T(8,128)(2,1)S(1)} %get-tuple-element.18.second_ref, bf16[128,64]{1,0:T(8,128)(2,1)S(1)} %multiply_convert_fusion.1.third_ref, bf16[2048,512]{1,0:T(8,128)(2,1)S(1)} %bitcast.301, bf16[4096,512]{1,0:T(8,128)(2,1)S(1)} %copy-done.5, ...), custom_call_target="tpu_custom_call" | custom-call | flops 8589934592 | bytes 25165824 | tf_op jit(solution)/shard_map/layer_back/pallas_call | solution.py:306
  322.0 4.8 forward_modes.6
  329.8 11.8 %collective-permute-done.11 = bf16[1,512,512]{2,1,0:T(8,128)(2,1)S(1)} collective-permute-done((bf16[1,512,512]{2,1,0:T(8,128)(2,1)S(1)}, bf16[1,512,512]{2,1,0:T(8,128)(2,1)S(1)}, u32[]{:S(2)}, u32[]{:S(2)}) %collective-permute-start.11) | collective-permute-done | bytes 524320 | tf_op jit(solution)/shard_map/ppermute | solution.py:331
  342.6 4.7 all-to-all-start.7
  348.5 12.0 %collective-permute-done.7 = bf16[1,512,512]{2,1,0:T(8,128)(2,1)S(1)} collective-permute-done((bf16[1,512,512]{2,1,0:T(8,128)(2,1)S(1)}, bf16[1,512,512]{2,1,0:T(8,128)(2,1)S(1)}, u32[]{:S(2)}, u32[]{:S(2)}) %collective-permute-start.7) | collective-permute-done | bytes 524320 | tf_op jit(solution)/shard_map/ppermute | solution.py:331
  361.6 5.9 all-to-all-start.5
  368.3 12.0 %all-to-all-done.5 = bf16[8,64,512]{2,1,0:T(8,128)(2,1)S(1)} async-done(((bf16[8,64,512]{2,1,0:T(8,128)(2,1)}), bf16[8,64,512]{2,1,0:T(8,128)(2,1)S(1)}, u32[]{:S(2)}, u32[]{:S(2)}) %all-to-all-start.5) | async-done | bytes 524320 | tf_op jit(solution)/shard_map/all_to_all | solution.py:357
  381.3 1.6 reshape.752
  383.7 8.1 %fusion = f32[32,4,8,2,128]{4,3,2,1,0:T(2,128)S(1)} fusion(bf16[2,32,4,8,64,128]{5,4,3,2,1,0:T(8,128)(2,1)} %param.11, bf16[32,4,8,2,64]{4,0,2,1,3:T(8,128)(2,1)S(1)} %fusion.18), kind=kOutput, calls=%fused_computation.3 | convolution fusion | flops 33554432 | bytes 18087936 | tf_op jit(solution)/shard_map/mkzpc,mkzcr->mkzpr/dot_general | solution.py:376
  391.8 2.3 fusion.51
  394.1 1.4 maximum_bitcast_fusion.1
  396.2 1.4 reshape.707
  397.6 3.7 all-to-all-start.9
  402.0 1.4 reshape.704
  403.4 11.7 %all-to-all-done.9 = bf16[8,64,512]{2,1,0:T(8,128)(2,1)S(1)} async-done(((bf16[8,64,512]{2,1,0:T(8,128)(2,1)}), bf16[8,64,512]{2,1,0:T(8,128)(2,1)S(1)}, u32[]{:S(2)}, u32[]{:S(2)}) %all-to-all-start.9) | async-done | bytes 524320 | tf_op jit(solution)/shard_map/all_to_all | solution.py:357
  415.1 3.9 all-to-all-start.8
  420.2 12.5 %all-to-all-done.8 = bf16[8,64,512]{2,1,0:T(8,128)(2,1)S(1)} async-done(((bf16[8,64,512]{2,1,0:T(8,128)(2,1)}), bf16[8,64,512]{2,1,0:T(8,128)(2,1)S(1)}, u32[]{:S(2)}, u32[]{:S(2)}) %all-to-all-start.8) | async-done | bytes 524320 | tf_op jit(solution)/shard_map/all_to_all | solution.py:357
  435.9 9.0 %collective-permute-done.12 = bf16[1,512,512]{2,1,0:T(8,128)(2,1)S(1)} collective-permute-done((bf16[1,512,512]{2,1,0:T(8,128)(2,1)S(1)}, bf16[1,512,512]{2,1,0:T(8,128)(2,1)S(1)}, u32[]{:S(2)}, u32[]{:S(2)}) %collective-permute-start.12) | collective-permute-done | bytes 524320 | tf_op jit(solution)/shard_map/ppermute | solution.py:331
  445.4 2.4 collective-permute-done.13
  448.0 2.0 copy-done.9
  450.0 10.6 %layer_back.7.refs_1_ = bf16[4096,512]{1,0:T(8,128)(2,1)S(1)} custom-call(bf16[512,512]{1,0:T(8,128)(2,1)S(1)} %get-tuple-element.18.second_ref, bf16[128,64]{1,0:T(8,128)(2,1)S(1)} %multiply_convert_fusion.1.third_ref, bf16[2048,512]{1,0:T(8,128)(2,1)S(1)} %bitcast.299, bf16[4096,512]{1,0:T(8,128)(2,1)S(1)} %copy-done.9, ...), custom_call_target="tpu_custom_call" | custom-call | flops 8589934592 | bytes 25165824 | tf_op jit(solution)/shard_map/layer_back/pallas_call | solution.py:306
  460.6 2.0 copy-done.2
  462.6 10.6 %layer_back.6.refs_0_ = bf16[4096,512]{1,0:T(8,128)(2,1)S(1)} custom-call(bf16[512,512]{1,0:T(8,128)(2,1)S(1)} %get-tuple-element.18.second_ref, bf16[128,64]{1,0:T(8,128)(2,1)S(1)} %multiply_convert_fusion.1.third_ref, bf16[2048,512]{1,0:T(8,128)(2,1)S(1)} %bitcast.300, bf16[4096,512]{1,0:T(8,128)(2,1)S(1)} %copy-done.11, ...), custom_call_target="tpu_custom_call" | custom-call | flops 8589934592 | bytes 25165824 | tf_op jit(solution)/shard_map/layer_back/pallas_call | solution.py:306
  473.2 2.1 copy-done.3
  475.2 33.3 %decode.1 = bf16[256,64,128]{2,1,0:T(8,128)(2,1)} custom-call(s32[3328]{0:T(1024)} %reshape.710.info_ref, bf16[4096,512]{1,0:T(8,128)(2,1)} %copy-done.3, bf16[4096,512]{1,0:T(8,128)(2,1)} %copy-done.2, bf16[256,4,128]{2,1,0:T(4,128)(2,1)} %copy-done.13), custom_call_target="tpu_custom_call" | custom-call | tf_op jit(solution)/shard_map/decode/pallas_call | solution.py:200
  508.5 4.5 all-to-all-start.10
  513.7 93.0 %all-to-all-done.10 = bf16[256,64,128]{2,1,0:T(8,128)(2,1)} async-done(((bf16[256,64,128]{2,1,0:T(8,128)(2,1)}), bf16[256,64,128]{2,1,0:T(8,128)(2,1)}, u32[]{:S(2)}, u32[]{:S(2)}) %all-to-all-start.10) | async-done | bytes 4194336 | tf_op jit(solution)/shard_map/all_to_all | solution.py:418
  606.7 4.3 gather_fusion.2
  611.0 3.3 broadcast_select_fusion
  (145 shorter events, 39.5 us)
Async XLA Ops:
  0.0 15.8 %copy-start = (bf16[128,64,128]{2,1,0:T(8,128)(2,1)S(1)}, bf16[128,64,128]{2,1,0:T(8,128)(2,1)}, u32[]{:S(2)}) copy-start(bf16[128,64,128]{2,1,0:T(8,128)(2,1)} %param.7) | copy-start | bytes 6291460
  8.5 17.9 %all-to-all-start = ((bf16[256,4,128]{2,1,0:T(4,128)(2,1)}), bf16[256,4,128]{2,1,0:T(4,128)(2,1)S(1)}, u32[]{:S(2)}, u32[]{:S(2)}) async-start(bf16[256,4,128]{2,1,0:T(4,128)(2,1)} %select_select_fusion.1), calls=%async_computation | async-start | bytes 524288 | tf_op jit(solution)/shard_map/all_to_all | solution.py:418
  23.3 7.2 %copy-start.16 = (bf16[2,64,64]{2,1,0:T(8,128)(2,1)S(1)}, bf16[2,64,64]{2,1,0:T(8,128)(2,1)}, u32[]{:S(2)}) copy-start(bf16[2,64,64]{2,1,0:T(8,128)(2,1)} %param.12) | copy-start | bytes 49156
  23.3 7.9 %copy-start.17 = (f32[2,64]{1,0:T(2,128)S(1)}, f32[2,64]{1,0:T(2,128)}, u32[]{:S(2)}) copy-start(f32[2,64]{1,0:T(2,128)} %param.13) | copy-start | bytes 1540
  26.4 15.3 %copy-start.13 = (bf16[256,4,128]{2,1,0:T(4,128)(2,1)}, bf16[256,4,128]{2,1,0:T(4,128)(2,1)S(1)}, u32[]{:S(2)}) copy-start(bf16[256,4,128]{2,1,0:T(4,128)(2,1)S(1)} %all-to-all-done.offset_ref.refs_2_) | copy-start | bytes 786436
  26.4 97.6 %all-to-all-start.1 = ((bf16[256,64,128]{2,1,0:T(8,128)(2,1)}), bf16[256,64,128]{2,1,0:T(8,128)(2,1)}, u32[]{:S(2)}, u32[]{:S(2)}) async-start(bf16[256,64,128]{2,1,0:T(8,128)(2,1)} %select_select_fusion), calls=%async_computation.1 | async-start | bytes 8388608 | tf_op jit(solution)/shard_map/all_to_all | solution.py:418
  158.8 2.2 copy-start.6
  160.9 4.9 copy-start.4
  165.8 5.5 collective-permute-start.2
  170.7 2.8 collective-permute-start
  171.6 13.9 %collective-permute-start.3 = (bf16[1,512,512]{2,1,0:T(8,128)(2,1)S(1)}, bf16[1,512,512]{2,1,0:T(8,128)(2,1)S(1)}, u32[]{:S(2)}, u32[]{:S(2)}) collective-permute-start(bf16[1,512,512]{2,1,0:T(8,128)(2,1)S(1)} %slice_bitcast_fusion.12), channel_id=1, source_target_pairs={{0,2},{1,3},{2,0},{3,1},{4,6},{5,7},{6,4},{7,5},{8,10},{9,11},{10,... | collective-permute-start | bytes 1572872 | tf_op jit(solution)/shard_map/ppermute | solution.py:331
  186.4 17.8 %all-to-all-start.3 = ((bf16[8,64,512]{2,1,0:T(8,128)(2,1)}), bf16[8,64,512]{2,1,0:T(8,128)(2,1)S(1)}, u32[]{:S(2)}, u32[]{:S(2)}) async-start(bf16[8,64,512]{2,1,0:T(8,128)(2,1)} %bitcast.42), calls=%async_computation.3 | async-start | bytes 1048576 | tf_op jit(solution)/shard_map/all_to_all | solution.py:357
  190.1 13.1 %collective-permute-start.1 = (bf16[1,512,512]{2,1,0:T(8,128)(2,1)S(1)}, bf16[1,512,512]{2,1,0:T(8,128)(2,1)S(1)}, u32[]{:S(2)}, u32[]{:S(2)}) collective-permute-start(bf16[1,512,512]{2,1,0:T(8,128)(2,1)S(1)} %slice_bitcast_fusion.14), channel_id=1, source_target_pairs={{0,2},{1,3},{2,0},{3,1},{4,6},{5,7},{6,4},{7,5},{8,10},{9,11},{10,... | collective-permute-start | bytes 1572872 | tf_op jit(solution)/shard_map/ppermute | solution.py:331
  204.2 0.8 copy-start.14
  205.0 18.5 %all-to-all-start.2 = ((bf16[8,64,512]{2,1,0:T(8,128)(2,1)}), bf16[8,64,512]{2,1,0:T(8,128)(2,1)S(1)}, u32[]{:S(2)}, u32[]{:S(2)}) async-start(bf16[8,64,512]{2,1,0:T(8,128)(2,1)} %bitcast.31), calls=%async_computation.2 | async-start | bytes 1048576 | tf_op jit(solution)/shard_map/all_to_all | solution.py:357
  224.4 1.2 copy-start.12
  257.3 12.7 %collective-permute-start.8 = (bf16[1,512,512]{2,1,0:T(8,128)(2,1)}, bf16[1,512,512]{2,1,0:T(8,128)(2,1)}, u32[]{:S(2)}, u32[]{:S(2)}) collective-permute-start(bf16[1,512,512]{2,1,0:T(8,128)(2,1)} %bitcast.76), channel_id=1, source_target_pairs={{0,2},{1,3},{2,0},{3,1},{4,6},{5,7},{6,4},{7,5},{8,10},{9,11},{10,... | collective-permute-start | bytes 1572872 | tf_op jit(solution)/shard_map/ppermute | solution.py:331
  260.4 17.8 %all-to-all-start.4 = ((bf16[8,64,512]{2,1,0:T(8,128)(2,1)}), bf16[8,64,512]{2,1,0:T(8,128)(2,1)S(1)}, u32[]{:S(2)}, u32[]{:S(2)}) async-start(bf16[8,64,512]{2,1,0:T(8,128)(2,1)} %reshape.692), calls=%async_computation.4 | async-start | bytes 1048576 | tf_op jit(solution)/shard_map/all_to_all | solution.py:357
  272.3 18.3 %collective-permute-start.9 = (bf16[2,512,512]{2,1,0:T(8,128)(2,1)}, bf16[2,512,512]{2,1,0:T(8,128)(2,1)}, u32[]{:S(2)}, u32[]{:S(2)}) collective-permute-start(bf16[2,512,512]{2,1,0:T(8,128)(2,1)} %get-tuple-element.42), channel_id=1, source_target_pairs={{0,1},{1,0},{2,3},{3,2},{4,5},{5,4},{6,7},{7,6},{8,9},{9,8},{10,11... | collective-permute-start | bytes 3145736 | tf_op jit(solution)/shard_map/ppermute | solution.py:331
  278.2 12.2 %collective-permute-start.4 = (bf16[1,512,512]{2,1,0:T(8,128)(2,1)S(1)}, bf16[1,512,512]{2,1,0:T(8,128)(2,1)S(1)}, u32[]{:S(2)}, u32[]{:S(2)}) collective-permute-start(bf16[1,512,512]{2,1,0:T(8,128)(2,1)S(1)} %bitcast.307), channel_id=1, source_target_pairs={{0,2},{1,3},{2,0},{3,1},{4,6},{5,7},{6,4},{7,5},{8,10},{9,11},{10,... | collective-permute-start | bytes 1572872 | tf_op jit(solution)/shard_map/ppermute | solution.py:331
  290.5 18.6 %collective-permute-start.5 = (bf16[2,512,512]{2,1,0:T(8,128)(2,1)S(1)}, bf16[2,512,512]{2,1,0:T(8,128)(2,1)S(1)}, u32[]{:S(2)}, u32[]{:S(2)}) collective-permute-start(bf16[2,512,512]{2,1,0:T(8,128)(2,1)S(1)} %get-tuple-element.44), channel_id=1, source_target_pairs={{0,1},{1,0},{2,3},{3,2},{4,5},{5,4},{6,7},{7,6},{8,9},{9,8},{10,11... | collective-permute-start | bytes 3145736 | tf_op jit(solution)/shard_map/ppermute | solution.py:331
  290.6 2.5 copy-start.7
  303.7 4.8 copy-start.8
  308.6 18.3 %collective-permute-start.10 = (bf16[2,512,512]{2,1,0:T(8,128)(2,1)S(1)}, bf16[2,512,512]{2,1,0:T(8,128)(2,1)S(1)}, u32[]{:S(2)}, u32[]{:S(2)}) collective-permute-start(bf16[2,512,512]{2,1,0:T(8,128)(2,1)S(1)} %slice_bitcast_fusion), channel_id=1, source_target_pairs={{0,1},{1,0},{2,3},{3,2},{4,5},{5,4},{6,7},{7,6},{8,9},{9,8},{10,11... | collective-permute-start | bytes 3145736 | tf_op jit(solution)/shard_map/ppermute | solution.py:331
  309.2 2.2 copy-start.5
  322.0 4.8 copy-start.10
  326.8 2.7 collective-permute-start.6
  327.3 14.4 %collective-permute-start.11 = (bf16[1,512,512]{2,1,0:T(8,128)(2,1)S(1)}, bf16[1,512,512]{2,1,0:T(8,128)(2,1)S(1)}, u32[]{:S(2)}, u32[]{:S(2)}) collective-permute-start(bf16[1,512,512]{2,1,0:T(8,128)(2,1)S(1)} %slice_bitcast_fusion.8), channel_id=1, source_target_pairs={{0,2},{1,3},{2,0},{3,1},{4,6},{5,7},{6,4},{7,5},{8,10},{9,11},{10,... | collective-permute-start | bytes 1572872 | tf_op jit(solution)/shard_map/ppermute | solution.py:331
  342.6 19.0 %all-to-all-start.7 = ((bf16[8,64,512]{2,1,0:T(8,128)(2,1)}), bf16[8,64,512]{2,1,0:T(8,128)(2,1)S(1)}, u32[]{:S(2)}, u32[]{:S(2)}) async-start(bf16[8,64,512]{2,1,0:T(8,128)(2,1)} %bitcast.89), calls=%async_computation.7 | async-start | bytes 1048576 | tf_op jit(solution)/shard_map/all_to_all | solution.py:357
  347.3 13.2 %collective-permute-start.7 = (bf16[1,512,512]{2,1,0:T(8,128)(2,1)S(1)}, bf16[1,512,512]{2,1,0:T(8,128)(2,1)S(1)}, u32[]{:S(2)}, u32[]{:S(2)}) collective-permute-start(bf16[1,512,512]{2,1,0:T(8,128)(2,1)S(1)} %slice_bitcast_fusion.10), channel_id=1, source_target_pairs={{0,2},{1,3},{2,0},{3,1},{4,6},{5,7},{6,4},{7,5},{8,10},{9,11},{10,... | collective-permute-start | bytes 1572872 | tf_op jit(solution)/shard_map/ppermute | solution.py:331
  361.6 18.7 %all-to-all-start.5 = ((bf16[8,64,512]{2,1,0:T(8,128)(2,1)}), bf16[8,64,512]{2,1,0:T(8,128)(2,1)S(1)}, u32[]{:S(2)}, u32[]{:S(2)}) async-start(bf16[8,64,512]{2,1,0:T(8,128)(2,1)} %bitcast.65), calls=%async_computation.5 | async-start | bytes 1048576 | tf_op jit(solution)/shard_map/all_to_all | solution.py:357
  397.6 17.5 %all-to-all-start.9 = ((bf16[8,64,512]{2,1,0:T(8,128)(2,1)}), bf16[8,64,512]{2,1,0:T(8,128)(2,1)S(1)}, u32[]{:S(2)}, u32[]{:S(2)}) async-start(bf16[8,64,512]{2,1,0:T(8,128)(2,1)} %reshape.707), calls=%async_computation.9 | async-start | bytes 1048576 | tf_op jit(solution)/shard_map/all_to_all | solution.py:357
  415.1 17.6 %all-to-all-start.8 = ((bf16[8,64,512]{2,1,0:T(8,128)(2,1)}), bf16[8,64,512]{2,1,0:T(8,128)(2,1)S(1)}, u32[]{:S(2)}, u32[]{:S(2)}) async-start(bf16[8,64,512]{2,1,0:T(8,128)(2,1)} %reshape.704), calls=%async_computation.8 | async-start | bytes 1048576 | tf_op jit(solution)/shard_map/all_to_all | solution.py:357
  419.0 14.9 %collective-permute-start.14 = (bf16[1,512,512]{2,1,0:T(8,128)(2,1)S(1)}, bf16[1,512,512]{2,1,0:T(8,128)(2,1)S(1)}, u32[]{:S(2)}, u32[]{:S(2)}) collective-permute-start(bf16[1,512,512]{2,1,0:T(8,128)(2,1)S(1)} %bitcast.303), channel_id=1, source_target_pairs={{0,2},{1,3},{2,0},{3,1},{4,6},{5,7},{6,4},{7,5},{8,10},{9,11},{10,... | collective-permute-start | bytes 1572872 | tf_op jit(solution)/shard_map/ppermute | solution.py:331
  432.7 12.2 %collective-permute-start.12 = (bf16[1,512,512]{2,1,0:T(8,128)(2,1)S(1)}, bf16[1,512,512]{2,1,0:T(8,128)(2,1)S(1)}, u32[]{:S(2)}, u32[]{:S(2)}) collective-permute-start(bf16[1,512,512]{2,1,0:T(8,128)(2,1)S(1)} %bitcast.305), channel_id=1, source_target_pairs={{0,2},{1,3},{2,0},{3,1},{4,6},{5,7},{6,4},{7,5},{8,10},{9,11},{10,... | collective-permute-start | bytes 1572872 | tf_op jit(solution)/shard_map/ppermute | solution.py:331
  433.9 0.8 copy-start.15
  435.8 9.3 %collective-permute-start.15 = (bf16[2,512,512]{2,1,0:T(8,128)(2,1)S(1)}, bf16[2,512,512]{2,1,0:T(8,128)(2,1)S(1)}, u32[]{:S(2)}, u32[]{:S(2)}) collective-permute-start(bf16[2,512,512]{2,1,0:T(8,128)(2,1)S(1)} %get-tuple-element.36), channel_id=1, source_target_pairs={{0,1},{1,0},{2,3},{3,2},{4,5},{5,4},{6,7},{7,6},{8,9},{9,8},{10,11... | collective-permute-start | bytes 3145736 | tf_op jit(solution)/shard_map/ppermute | solution.py:331
  445.1 2.7 collective-permute-start.13
  447.8 2.2 copy-start.9
  450.0 12.6 %copy-start.11 = (bf16[4096,512]{1,0:T(8,128)(2,1)S(1)}, bf16[4096,512]{1,0:T(8,128)(2,1)}, u32[]{:S(2)}) copy-start(bf16[4096,512]{1,0:T(8,128)(2,1)} %copy-done.10) | copy-start | bytes 12582916
  460.6 2.0 copy-start.2
  473.2 2.1 copy-start.3
  508.5 98.2 %all-to-all-start.10 = ((bf16[256,64,128]{2,1,0:T(8,128)(2,1)}), bf16[256,64,128]{2,1,0:T(8,128)(2,1)}, u32[]{:S(2)}, u32[]{:S(2)}) async-start(bf16[256,64,128]{2,1,0:T(8,128)(2,1)} %decode.1), calls=%async_computation.10 | async-start | bytes 8388608 | tf_op jit(solution)/shard_map/all_to_all | solution.py:418
  611.0 3.3 copy-start.1

commit v4 on v3

--- a/solution.py
+++ b/solution.py
@@ -209,6 +209,11 @@
         ),
         out_shape=jax.ShapeDtypeStruct((slots, channels, points), BF16),
         compiler_params=pltpu.CompilerParams(vmem_limit_bytes=VMEM_LIMIT),
+        cost_estimate=pl.CostEstimate(
+            flops=4 * slots * channels * points * 512,
+            bytes_accessed=2 * rows * width * CHUNKS,
+            transcendentals=slots * points * 128,
+        ),
         name="decode",
     )(info, *grids, offsets)
 
@@ -409,7 +414,7 @@
 
 
 def pack_slots(values, present, sources, filler):
-    picked = jnp.take(values, sources, axis=0)
+    picked = jnp.take(values, sources, axis=0, mode="clip")
     masking = present.reshape((-1,) + (1,) * (values.ndim - 1))
     return jnp.where(masking, picked, jnp.asarray(filler, values.dtype))
 
@@ -494,9 +499,17 @@
             layer_back(*back, mode, grid, *skips[depth_index], mesh_columns)
             for mode, grid in zip(modes, grids)
         ]
-    reply = decode(info, grids, got_notes, channels, NZ)
-    returned = route_back(reply)
-    return jnp.take(returned, slot_index, axis=0)
+    half = capacity // 2
+    ranks = slot_index % capacity
+    at_half = slot_index // capacity * half + ranks % half
+    infos = info.reshape(device_total, 2, -1)
+    halved_notes = got_notes.reshape((device_total, 2, half) + got_notes.shape[1:])
+    picked = []
+    for side in range(2):
+        side_notes = halved_notes[:, side].reshape((-1,) + got_notes.shape[1:])
+        reply = decode(infos[:, side].reshape(-1), grids, side_notes, channels, NZ)
+        picked.append(jnp.take(route_back(reply), at_half, axis=0, mode="clip"))
+    return jnp.where((ranks < half)[:, None, None], picked[0], picked[1])
 
 
 def solution(mesh):

time: 620 us -> 616 us (level)
  waiting for transfers between devices: 306 us -> 285 us
    all_to_all x3 -> x4, waiting for transfers between devices: 177 us -> 159 us  [route_back(): lax.all_to_all(values, ('px', 'py'), split_axis=0, concat_axis=0, tiled=T...]
    pallas_call x1 -> x2, Pallas kernels: 33.3 us -> 38.9 us  [decode(): pl.pallas_call(functools.partial(decode_body, group, depth), grid_spec=pl...]
    all_to_all x3 -> x4, starting transfers between devices: 15.6 us -> 19.8 us  [route_back(): lax.all_to_all(values, ('px', 'py'), split_axis=0, concat_axis=0, tiled=T...]
    unnamed x37 -> x41, local copies, waits for them, and re-layouts: 14.6 us -> 13.5 us
  transfers between devices with their start and end apart: 26 -> 27, of which waited for: 20 -> 20; matrix products, arithmetic and copies ran while one was open for 6% -> 8% of each run, Pallas kernels for 6% -> 9%
where the time goes in v4:
time: 616 us; the launch traced here: 611 us
  waiting for transfers between devices  285 us (46%)
  Pallas kernels  135 us (22%)
  starting transfers between devices  62.8 us (10%)
  other arithmetic  49.1 us (8%)
  local copies, waits for them, and re-layouts  41.6 us (7%)
  matrix products  19.5 us (3%)
  blocking collectives  17.5 us (3%)
    all_to_all x4, waiting for transfers between devices, route_back(): lax.all_to_all(values, ('px', 'py'), split_axis=0, concat_axis=0, tiled=T...  159 us
    ppermute x16, waiting for transfers between devices, swap(): return lax.ppermute(values, 'py', [(i, i ^ distance) for i in range(size)])  73.2 us
    all_to_all x7, waiting for transfers between devices, exchange_x(): return lax.all_to_all(values, 'px', split_axis=0, concat_axis=0, tiled=True)  52.2 us
    pallas_call x4, Pallas kernels, layer_back(): pl.pallas_call(functools.partial(layer_body, groups), grid=(lanes // widt...  42.4 us
    pallas_call x2, Pallas kernels, decode(): pl.pallas_call(functools.partial(decode_body, group, depth), grid_spec=pl...  38.9 us
    pallas_call x1, Pallas kernels, encode(): pl.pallas_call(functools.partial(encode_body, group, depth, steps), grid_...  34.7 us
    all_to_all x7, starting transfers between devices, exchange_x(): return lax.all_to_all(values, 'px', split_axis=0, concat_axis=0, tiled=True)  31.8 us
    all_to_all x4, starting transfers between devices, route_back(): lax.all_to_all(values, ('px', 'py'), split_axis=0, concat_axis=0, tiled=T...  19.8 us
  transfers between devices with their start and end apart: 27, of which 20 were waited for; matrix products, arithmetic and copies ran while one was open for 8% of the time, Pallas kernels for 9%

profile of v4, /device:TPU:0, one launch (start us, length us, event | category | flops | bytes accessed | tf_op | source)
XLA Modules:
  0.0 611.0 jit_solution(8211527487348525642)
XLA Ops:
  7.4 7.3 %all-to-all-start = ((bf16[256,4,128]{2,1,0:T(4,128)(2,1)}), bf16[256,4,128]{2,1,0:T(4,128)(2,1)S(1)}, u32[]{:S(2)}, u32[]{:S(2)}) async-start(bf16[256,4,128]{2,1,0:T(4,128)(2,1)} %broadcast_select_fusion.2), calls=%async_computation | async-start | bytes 524288 | tf_op jit(solution)/shard_map/all_to_all | solution.py:423
  14.7 3.1 gather_fusion.1
  17.8 4.0 broadcast_select_fusion
  21.9 3.4 all-to-all-done.offset_ref
  25.3 3.8 all-to-all-start.1
  31.4 9.3 %fusion.31 = (bf16[512,512]{1,0:T(8,128)(2,1)S(1)}, bf16[512,512]{1,0:T(8,128)(2,1)S(1)}) fusion(s32[512]{0:T(512)S(1)} %get-tuple-element.72, s32[512]{0:T(512)S(1)} %get-tuple-element.69, s32[512]{0:T(512)S(1)} %get-tuple-element.70, s32[512]{0:T(512)S(1)} %get-tuple-element.71, pred[512]{0:T(512)(128)(4,1)S(1)} %broadcast_compare_fusion), kind=kLoop, calls=%fused_computation.65 | loop fusion | flops 11534336 | bytes 1057280 | tf_op jit(solution)/shard_map/convert_element_type | solution.py:479
  41.7 81.3 %all-to-all-done.1.feature_ref = bf16[256,64,128]{2,1,0:T(8,128)(2,1)} async-done(((bf16[256,64,128]{2,1,0:T(8,128)(2,1)}), bf16[256,64,128]{2,1,0:T(8,128)(2,1)}, u32[]{:S(2)}, u32[]{:S(2)}) %all-to-all-start.1) | async-done | bytes 4194336 | tf_op jit(solution)/shard_map/all_to_all | solution.py:423
  123.0 34.7 %encode.1 = (bf16[4096,512]{1,0:T(8,128)(2,1)}, bf16[4096,512]{1,0:T(8,128)(2,1)}) custom-call(s32[3328]{0:T(1024)} %reshape.739.info_ref, bf16[256,64,128]{2,1,0:T(8,128)(2,1)} %all-to-all-done.1.feature_ref, bf16[256,4,128]{2,1,0:T(4,128)(2,1)} %copy-done.12), custom_call_target="tpu_custom_call" | custom-call | tf_op jit(solution)/shard_map/encode/pallas_call | solution.py:141
  157.7 2.2 copy-done.6
  159.9 4.7 forward_modes.5
  164.8 4.8 forward_modes.4
  172.7 11.7 %collective-permute-done.3 = bf16[1,512,512]{2,1,0:T(8,128)(2,1)S(1)} collective-permute-done((bf16[1,512,512]{2,1,0:T(8,128)(2,1)S(1)}, bf16[1,512,512]{2,1,0:T(8,128)(2,1)S(1)}, u32[]{:S(2)}, u32[]{:S(2)}) %collective-permute-start.3) | collective-permute-done | bytes 524320 | tf_op jit(solution)/shard_map/ppermute | solution.py:336
  185.4 3.7 all-to-all-start.3
  189.1 1.8 collective-permute-start.1
  190.9 11.3 %collective-permute-done.1 = bf16[1,512,512]{2,1,0:T(8,128)(2,1)S(1)} collective-permute-done((bf16[1,512,512]{2,1,0:T(8,128)(2,1)S(1)}, bf16[1,512,512]{2,1,0:T(8,128)(2,1)S(1)}, u32[]{:S(2)}, u32[]{:S(2)}) %collective-permute-start.1) | collective-permute-done | bytes 524320 | tf_op jit(solution)/shard_map/ppermute | solution.py:336
  204.0 5.9 all-to-all-start.2
  211.2 1.5 reshape.786
  212.7 9.8 %all-to-all-done.2 = bf16[8,64,512]{2,1,0:T(8,128)(2,1)S(1)} async-done(((bf16[8,64,512]{2,1,0:T(8,128)(2,1)}), bf16[8,64,512]{2,1,0:T(8,128)(2,1)S(1)}, u32[]{:S(2)}, u32[]{:S(2)}) %all-to-all-start.2) | async-done | bytes 524320 | tf_op jit(solution)/shard_map/all_to_all | solution.py:362
  225.0 8.0 %fusion.2 = f32[32,4,8,2,128]{4,3,2,1,0:T(2,128)S(1)} fusion(bf16[2,32,4,8,64,128]{5,4,3,2,1,0:T(8,128)(2,1)} %param.11, bf16[32,4,8,2,64]{4,0,2,1,3:T(8,128)(2,1)S(1)} %fusion.19), kind=kOutput, calls=%fused_computation.6 | convolution fusion | flops 33554432 | bytes 18087936 | tf_op jit(solution)/shard_map/mkzpc,mkzcr->mkzpr/dot_general | solution.py:381
  233.0 2.3 fusion.53
  238.9 17.5 %all_to_all.60 = bf16[8,64,512]{2,1,0:T(8,128)(2,1)} all-to-all(bf16[8,64,512]{2,1,0:T(8,128)(2,1)} %reshape.725), channel_id=1, replica_groups=mesh['px'=8,'py'=4] {'px'}, dimensions={0} | all-to-all | bytes 1048576 | tf_op jit(solution)/shard_map/all_to_all | solution.py:362
  257.9 1.4 reshape.719
  259.4 4.1 all-to-all-start.4
  263.5 5.5 collective-permute-done.8
  269.0 2.3 fusion.47
  271.3 6.0 all-to-all-done.4
  278.4 11.1 %collective-permute-done.4 = bf16[1,512,512]{2,1,0:T(8,128)(2,1)S(1)} collective-permute-done((bf16[1,512,512]{2,1,0:T(8,128)(2,1)S(1)}, bf16[1,512,512]{2,1,0:T(8,128)(2,1)S(1)}, u32[]{:S(2)}, u32[]{:S(2)}) %collective-permute-start.4) | collective-permute-done | bytes 524320 | tf_op jit(solution)/shard_map/ppermute | solution.py:336
  289.7 1.6 pad_maximum_fusion.1
  292.2 10.6 %layer_back.5.grid_ref = bf16[4096,512]{1,0:T(8,128)(2,1)S(1)} custom-call(bf16[512,512]{1,0:T(8,128)(2,1)S(1)} %get-tuple-element.18.second_ref, bf16[128,64]{1,0:T(8,128)(2,1)S(1)} %multiply_convert_fusion.1.third_ref, bf16[2048,512]{1,0:T(8,128)(2,1)S(1)} %bitcast.308, bf16[4096,512]{1,0:T(8,128)(2,1)S(1)} %copy-done.7, ...), custom_call_target="tpu_custom_call" | custom-call | flops 8589934592 | bytes 25165824 | tf_op jit(solution)/shard_map/layer_back/pallas_call | solution.py:311
  302.8 4.8 forward_modes.7
  308.4 2.0 copy-done.5
  310.4 10.6 %layer_back.4.grid_ref = bf16[4096,512]{1,0:T(8,128)(2,1)S(1)} custom-call(bf16[512,512]{1,0:T(8,128)(2,1)S(1)} %get-tuple-element.18.second_ref, bf16[128,64]{1,0:T(8,128)(2,1)S(1)} %multiply_convert_fusion.1.third_ref, bf16[2048,512]{1,0:T(8,128)(2,1)S(1)} %bitcast.307, bf16[4096,512]{1,0:T(8,128)(2,1)S(1)} %copy-done.5, ...), custom_call_target="tpu_custom_call" | custom-call | flops 8589934592 | bytes 25165824 | tf_op jit(solution)/shard_map/layer_back/pallas_call | solution.py:311
  321.1 4.8 forward_modes.6
  328.9 11.8 %collective-permute-done.11 = bf16[1,512,512]{2,1,0:T(8,128)(2,1)S(1)} collective-permute-done((bf16[1,512,512]{2,1,0:T(8,128)(2,1)S(1)}, bf16[1,512,512]{2,1,0:T(8,128)(2,1)S(1)}, u32[]{:S(2)}, u32[]{:S(2)}) %collective-permute-start.11) | collective-permute-done | bytes 524320 | tf_op jit(solution)/shard_map/ppermute | solution.py:336
  341.6 4.7 all-to-all-start.7
  347.6 12.0 %collective-permute-done.7 = bf16[1,512,512]{2,1,0:T(8,128)(2,1)S(1)} collective-permute-done((bf16[1,512,512]{2,1,0:T(8,128)(2,1)S(1)}, bf16[1,512,512]{2,1,0:T(8,128)(2,1)S(1)}, u32[]{:S(2)}, u32[]{:S(2)}) %collective-permute-start.7) | collective-permute-done | bytes 524320 | tf_op jit(solution)/shard_map/ppermute | solution.py:336
  360.7 5.9 all-to-all-start.5
  367.4 12.0 %all-to-all-done.5 = bf16[8,64,512]{2,1,0:T(8,128)(2,1)S(1)} async-done(((bf16[8,64,512]{2,1,0:T(8,128)(2,1)}), bf16[8,64,512]{2,1,0:T(8,128)(2,1)S(1)}, u32[]{:S(2)}, u32[]{:S(2)}) %all-to-all-start.5) | async-done | bytes 524320 | tf_op jit(solution)/shard_map/all_to_all | solution.py:362
  380.4 1.6 reshape.791
  382.8 8.1 %fusion = f32[32,4,8,2,128]{4,3,2,1,0:T(2,128)S(1)} fusion(bf16[2,32,4,8,64,128]{5,4,3,2,1,0:T(8,128)(2,1)} %param.11, bf16[32,4,8,2,64]{4,0,2,1,3:T(8,128)(2,1)S(1)} %fusion.18), kind=kOutput, calls=%fused_computation.4 | convolution fusion | flops 33554432 | bytes 18087936 | tf_op jit(solution)/shard_map/mkzpc,mkzcr->mkzpr/dot_general | solution.py:381
  390.9 2.3 fusion.51
  396.7 3.7 all-to-all-start.9
  401.1 1.4 reshape.731
  402.5 11.7 %all-to-all-done.9 = bf16[8,64,512]{2,1,0:T(8,128)(2,1)S(1)} async-done(((bf16[8,64,512]{2,1,0:T(8,128)(2,1)}), bf16[8,64,512]{2,1,0:T(8,128)(2,1)S(1)}, u32[]{:S(2)}, u32[]{:S(2)}) %all-to-all-start.9) | async-done | bytes 524320 | tf_op jit(solution)/shard_map/all_to_all | solution.py:362
  414.2 3.9 all-to-all-start.8
  419.3 12.6 %all-to-all-done.8 = bf16[8,64,512]{2,1,0:T(8,128)(2,1)S(1)} async-done(((bf16[8,64,512]{2,1,0:T(8,128)(2,1)}), bf16[8,64,512]{2,1,0:T(8,128)(2,1)S(1)}, u32[]{:S(2)}, u32[]{:S(2)}) %all-to-all-start.8) | async-done | bytes 524320 | tf_op jit(solution)/shard_map/all_to_all | solution.py:362
  433.7 2.1 fusion.43
  435.9 8.1 %collective-permute-done.12 = bf16[1,512,512]{2,1,0:T(8,128)(2,1)S(1)} collective-permute-done((bf16[1,512,512]{2,1,0:T(8,128)(2,1)S(1)}, bf16[1,512,512]{2,1,0:T(8,128)(2,1)S(1)}, u32[]{:S(2)}, u32[]{:S(2)}) %collective-permute-start.12) | collective-permute-done | bytes 524320 | tf_op jit(solution)/shard_map/ppermute | solution.py:336
  444.0 2.1 fusion.45
  448.3 1.4 pad_maximum_fusion.3
  449.8 1.6 pad_maximum_fusion.2
  452.3 10.6 %layer_back.7.refs_1_ = bf16[4096,512]{1,0:T(8,128)(2,1)S(1)} custom-call(bf16[512,512]{1,0:T(8,128)(2,1)S(1)} %get-tuple-element.18.second_ref, bf16[128,64]{1,0:T(8,128)(2,1)S(1)} %multiply_convert_fusion.1.third_ref, bf16[2048,512]{1,0:T(8,128)(2,1)S(1)} %bitcast.305, bf16[4096,512]{1,0:T(8,128)(2,1)S(1)} %copy-done.9, ...), custom_call_target="tpu_custom_call" | custom-call | flops 8589934592 | bytes 25165824 | tf_op jit(solution)/shard_map/layer_back/pallas_call | solution.py:311
  462.9 2.0 copy-done.2
  464.9 10.6 %layer_back.6.refs_0_ = bf16[4096,512]{1,0:T(8,128)(2,1)S(1)} custom-call(bf16[512,512]{1,0:T(8,128)(2,1)S(1)} %get-tuple-element.18.second_ref, bf16[128,64]{1,0:T(8,128)(2,1)S(1)} %multiply_convert_fusion.1.third_ref, bf16[2048,512]{1,0:T(8,128)(2,1)S(1)} %bitcast.306, bf16[4096,512]{1,0:T(8,128)(2,1)S(1)} %copy-done.11, ...), custom_call_target="tpu_custom_call" | custom-call | flops 8589934592 | bytes 25165824 | tf_op jit(solution)/shard_map/layer_back/pallas_call | solution.py:311
  475.5 2.0 copy-done.3
  477.5 19.4 %decode.3 = bf16[128,64,128]{2,1,0:T(8,128)(2,1)} custom-call(s32[1664]{0:T(1024)} %reshape_squeeze.14.info_ref, bf16[4096,512]{1,0:T(8,128)(2,1)} %copy-done.3, bf16[4096,512]{1,0:T(8,128)(2,1)} %copy-done.2, bf16[128,4,128]{2,1,0:T(4,128)(2,1)} %bitcast.322), custom_call_target="tpu_custom_call" | custom-call | flops 2147483648 | bytes 8388608 | tf_op jit(solution)/shard_map/decode/pallas_call | solution.py:200
  496.9 4.5 all-to-all-start.11
  502.1 19.4 %decode.2 = bf16[128,64,128]{2,1,0:T(8,128)(2,1)} custom-call(s32[1664]{0:T(1024)} %reshape_squeeze.12.info_ref, bf16[4096,512]{1,0:T(8,128)(2,1)} %copy-done.3, bf16[4096,512]{1,0:T(8,128)(2,1)} %copy-done.2, bf16[128,4,128]{2,1,0:T(4,128)(2,1)} %bitcast.321), custom_call_target="tpu_custom_call" | custom-call | flops 2147483648 | bytes 8388608 | tf_op jit(solution)/shard_map/decode/pallas_call | solution.py:200
  521.5 28.6 %all-to-all-done.11 = bf16[128,64,128]{2,1,0:T(8,128)(2,1)S(1)} async-done(((bf16[128,64,128]{2,1,0:T(8,128)(2,1)}), bf16[128,64,128]{2,1,0:T(8,128)(2,1)S(1)}, u32[]{:S(2)}, u32[]{:S(2)}) %all-to-all-start.11) | async-done | bytes 2097184 | tf_op jit(solution)/shard_map/all_to_all | solution.py:423
  550.1 4.2 all-to-all-start.10
  555.1 2.2 gather_fusion.3
  557.2 45.8 %all-to-all-done.10 = bf16[128,64,128]{2,1,0:T(8,128)(2,1)} async-done(((bf16[128,64,128]{2,1,0:T(8,128)(2,1)}), bf16[128,64,128]{2,1,0:T(8,128)(2,1)}, u32[]{:S(2)}, u32[]{:S(2)}) %all-to-all-start.10) | async-done | bytes 2097184 | tf_op jit(solution)/shard_map/all_to_all | solution.py:423
  603.1 3.7 gather_fusion.2
  606.8 4.0 broadcast_select_fusion.1
  (157 shorter events, 49.1 us)
Async XLA Ops:
  0.0 14.7 %copy-start = (bf16[128,64,128]{2,1,0:T(8,128)(2,1)S(1)}, bf16[128,64,128]{2,1,0:T(8,128)(2,1)}, u32[]{:S(2)}) copy-start(bf16[128,64,128]{2,1,0:T(8,128)(2,1)} %param.7) | copy-start | bytes 6291460
  7.4 17.9 %all-to-all-start = ((bf16[256,4,128]{2,1,0:T(4,128)(2,1)}), bf16[256,4,128]{2,1,0:T(4,128)(2,1)S(1)}, u32[]{:S(2)}, u32[]{:S(2)}) async-start(bf16[256,4,128]{2,1,0:T(4,128)(2,1)} %broadcast_select_fusion.2), calls=%async_computation | async-start | bytes 524288 | tf_op jit(solution)/shard_map/all_to_all | solution.py:423
  21.9 7.6 %copy-start.18 = (bf16[2,64,64]{2,1,0:T(8,128)(2,1)S(1)}, bf16[2,64,64]{2,1,0:T(8,128)(2,1)}, u32[]{:S(2)}) copy-start(bf16[2,64,64]{2,1,0:T(8,128)(2,1)} %param.12) | copy-start | bytes 49156
  21.9 8.3 %copy-start.19 = (f32[2,64]{1,0:T(2,128)S(1)}, f32[2,64]{1,0:T(2,128)}, u32[]{:S(2)}) copy-start(f32[2,64]{1,0:T(2,128)} %param.13) | copy-start | bytes 1540
  25.3 15.4 %copy-start.12 = (bf16[256,4,128]{2,1,0:T(4,128)(2,1)}, bf16[256,4,128]{2,1,0:T(4,128)(2,1)S(1)}, u32[]{:S(2)}) copy-start(bf16[256,4,128]{2,1,0:T(4,128)(2,1)S(1)} %all-to-all-done.offset_ref) | copy-start | bytes 786436
  25.3 97.7 %all-to-all-start.1 = ((bf16[256,64,128]{2,1,0:T(8,128)(2,1)}), bf16[256,64,128]{2,1,0:T(8,128)(2,1)}, u32[]{:S(2)}, u32[]{:S(2)}) async-start(bf16[256,64,128]{2,1,0:T(8,128)(2,1)} %broadcast_select_fusion), calls=%async_computation.1 | async-start | bytes 8388608 | tf_op jit(solution)/shard_map/all_to_all | solution.py:423
  157.7 2.2 copy-start.6
  159.9 4.9 copy-start.4
  164.7 5.5 collective-permute-start.2
  169.6 2.8 collective-permute-start
  170.5 13.9 %collective-permute-start.3 = (bf16[1,512,512]{2,1,0:T(8,128)(2,1)S(1)}, bf16[1,512,512]{2,1,0:T(8,128)(2,1)S(1)}, u32[]{:S(2)}, u32[]{:S(2)}) collective-permute-start(bf16[1,512,512]{2,1,0:T(8,128)(2,1)S(1)} %slice_bitcast_fusion.12), channel_id=1, source_target_pairs={{0,2},{1,3},{2,0},{3,1},{4,6},{5,7},{6,4},{7,5},{8,10},{9,11},{10,... | collective-permute-start | bytes 1572872 | tf_op jit(solution)/shard_map/ppermute | solution.py:336
  185.4 17.8 %all-to-all-start.3 = ((bf16[8,64,512]{2,1,0:T(8,128)(2,1)}), bf16[8,64,512]{2,1,0:T(8,128)(2,1)S(1)}, u32[]{:S(2)}, u32[]{:S(2)}) async-start(bf16[8,64,512]{2,1,0:T(8,128)(2,1)} %bitcast.38), calls=%async_computation.3 | async-start | bytes 1048576 | tf_op jit(solution)/shard_map/all_to_all | solution.py:362
  189.1 13.1 %collective-permute-start.1 = (bf16[1,512,512]{2,1,0:T(8,128)(2,1)S(1)}, bf16[1,512,512]{2,1,0:T(8,128)(2,1)S(1)}, u32[]{:S(2)}, u32[]{:S(2)}) collective-permute-start(bf16[1,512,512]{2,1,0:T(8,128)(2,1)S(1)} %slice_bitcast_fusion.14), channel_id=1, source_target_pairs={{0,2},{1,3},{2,0},{3,1},{4,6},{5,7},{6,4},{7,5},{8,10},{9,11},{10,... | collective-permute-start | bytes 1572872 | tf_op jit(solution)/shard_map/ppermute | solution.py:336
  203.2 0.8 copy-start.15
  204.0 18.6 %all-to-all-start.2 = ((bf16[8,64,512]{2,1,0:T(8,128)(2,1)}), bf16[8,64,512]{2,1,0:T(8,128)(2,1)S(1)}, u32[]{:S(2)}, u32[]{:S(2)}) async-start(bf16[8,64,512]{2,1,0:T(8,128)(2,1)} %bitcast.27), calls=%async_computation.2 | async-start | bytes 1048576 | tf_op jit(solution)/shard_map/all_to_all | solution.py:362
  223.4 1.2 copy-start.14
  256.3 12.7 %collective-permute-start.8 = (bf16[1,512,512]{2,1,0:T(8,128)(2,1)}, bf16[1,512,512]{2,1,0:T(8,128)(2,1)}, u32[]{:S(2)}, u32[]{:S(2)}) collective-permute-start(bf16[1,512,512]{2,1,0:T(8,128)(2,1)} %bitcast.72), channel_id=1, source_target_pairs={{0,2},{1,3},{2,0},{3,1},{4,6},{5,7},{6,4},{7,5},{8,10},{9,11},{10,... | collective-permute-start | bytes 1572872 | tf_op jit(solution)/shard_map/ppermute | solution.py:336
  259.4 17.9 %all-to-all-start.4 = ((bf16[8,64,512]{2,1,0:T(8,128)(2,1)}), bf16[8,64,512]{2,1,0:T(8,128)(2,1)S(1)}, u32[]{:S(2)}, u32[]{:S(2)}) async-start(bf16[8,64,512]{2,1,0:T(8,128)(2,1)} %reshape.719), calls=%async_computation.4 | async-start | bytes 1048576 | tf_op jit(solution)/shard_map/all_to_all | solution.py:362
  271.3 18.4 %collective-permute-start.9 = (bf16[2,512,512]{2,1,0:T(8,128)(2,1)}, bf16[2,512,512]{2,1,0:T(8,128)(2,1)}, u32[]{:S(2)}, u32[]{:S(2)}) collective-permute-start(bf16[2,512,512]{2,1,0:T(8,128)(2,1)} %get-tuple-element.44), channel_id=1, source_target_pairs={{0,1},{1,0},{2,3},{3,2},{4,5},{5,4},{6,7},{7,6},{8,9},{9,8},{10,11... | collective-permute-start | bytes 3145736 | tf_op jit(solution)/shard_map/ppermute | solution.py:336
  277.3 12.2 %collective-permute-start.4 = (bf16[1,512,512]{2,1,0:T(8,128)(2,1)S(1)}, bf16[1,512,512]{2,1,0:T(8,128)(2,1)S(1)}, u32[]{:S(2)}, u32[]{:S(2)}) collective-permute-start(bf16[1,512,512]{2,1,0:T(8,128)(2,1)S(1)} %bitcast.314), channel_id=1, source_target_pairs={{0,2},{1,3},{2,0},{3,1},{4,6},{5,7},{6,4},{7,5},{8,10},{9,11},{10,... | collective-permute-start | bytes 1572872 | tf_op jit(solution)/shard_map/ppermute | solution.py:336
  289.6 18.6 %collective-permute-start.5 = (bf16[2,512,512]{2,1,0:T(8,128)(2,1)S(1)}, bf16[2,512,512]{2,1,0:T(8,128)(2,1)S(1)}, u32[]{:S(2)}, u32[]{:S(2)}) collective-permute-start(bf16[2,512,512]{2,1,0:T(8,128)(2,1)S(1)} %get-tuple-element.46), channel_id=1, source_target_pairs={{0,1},{1,0},{2,3},{3,2},{4,5},{5,4},{6,7},{7,6},{8,9},{9,8},{10,11... | collective-permute-start | bytes 3145736 | tf_op jit(solution)/shard_map/ppermute | solution.py:336
  289.7 2.5 copy-start.7
  302.8 4.8 copy-start.8
  307.7 18.3 %collective-permute-start.10 = (bf16[2,512,512]{2,1,0:T(8,128)(2,1)S(1)}, bf16[2,512,512]{2,1,0:T(8,128)(2,1)S(1)}, u32[]{:S(2)}, u32[]{:S(2)}) collective-permute-start(bf16[2,512,512]{2,1,0:T(8,128)(2,1)S(1)} %slice_bitcast_fusion), channel_id=1, source_target_pairs={{0,1},{1,0},{2,3},{3,2},{4,5},{5,4},{6,7},{7,6},{8,9},{9,8},{10,11... | collective-permute-start | bytes 3145736 | tf_op jit(solution)/shard_map/ppermute | solution.py:336
  308.2 2.2 copy-start.5
  321.0 4.8 copy-start.10
  325.9 2.7 collective-permute-start.6
  326.3 14.4 %collective-permute-start.11 = (bf16[1,512,512]{2,1,0:T(8,128)(2,1)S(1)}, bf16[1,512,512]{2,1,0:T(8,128)(2,1)S(1)}, u32[]{:S(2)}, u32[]{:S(2)}) collective-permute-start(bf16[1,512,512]{2,1,0:T(8,128)(2,1)S(1)} %slice_bitcast_fusion.8), channel_id=1, source_target_pairs={{0,2},{1,3},{2,0},{3,1},{4,6},{5,7},{6,4},{7,5},{8,10},{9,11},{10,... | collective-permute-start | bytes 1572872 | tf_op jit(solution)/shard_map/ppermute | solution.py:336
  341.6 19.0 %all-to-all-start.7 = ((bf16[8,64,512]{2,1,0:T(8,128)(2,1)}), bf16[8,64,512]{2,1,0:T(8,128)(2,1)S(1)}, u32[]{:S(2)}, u32[]{:S(2)}) async-start(bf16[8,64,512]{2,1,0:T(8,128)(2,1)} %bitcast.85), calls=%async_computation.7 | async-start | bytes 1048576 | tf_op jit(solution)/shard_map/all_to_all | solution.py:362
  346.4 13.2 %collective-permute-start.7 = (bf16[1,512,512]{2,1,0:T(8,128)(2,1)S(1)}, bf16[1,512,512]{2,1,0:T(8,128)(2,1)S(1)}, u32[]{:S(2)}, u32[]{:S(2)}) collective-permute-start(bf16[1,512,512]{2,1,0:T(8,128)(2,1)S(1)} %slice_bitcast_fusion.10), channel_id=1, source_target_pairs={{0,2},{1,3},{2,0},{3,1},{4,6},{5,7},{6,4},{7,5},{8,10},{9,11},{10,... | collective-permute-start | bytes 1572872 | tf_op jit(solution)/shard_map/ppermute | solution.py:336
  360.7 18.7 %all-to-all-start.5 = ((bf16[8,64,512]{2,1,0:T(8,128)(2,1)}), bf16[8,64,512]{2,1,0:T(8,128)(2,1)S(1)}, u32[]{:S(2)}, u32[]{:S(2)}) async-start(bf16[8,64,512]{2,1,0:T(8,128)(2,1)} %bitcast.61), calls=%async_computation.5 | async-start | bytes 1048576 | tf_op jit(solution)/shard_map/all_to_all | solution.py:362
  396.7 17.5 %all-to-all-start.9 = ((bf16[8,64,512]{2,1,0:T(8,128)(2,1)}), bf16[8,64,512]{2,1,0:T(8,128)(2,1)S(1)}, u32[]{:S(2)}, u32[]{:S(2)}) async-start(bf16[8,64,512]{2,1,0:T(8,128)(2,1)} %reshape.734), calls=%async_computation.9 | async-start | bytes 1048576 | tf_op jit(solution)/shard_map/all_to_all | solution.py:362
  414.2 17.6 %all-to-all-start.8 = ((bf16[8,64,512]{2,1,0:T(8,128)(2,1)}), bf16[8,64,512]{2,1,0:T(8,128)(2,1)S(1)}, u32[]{:S(2)}, u32[]{:S(2)}) async-start(bf16[8,64,512]{2,1,0:T(8,128)(2,1)} %reshape.731), calls=%async_computation.8 | async-start | bytes 1048576 | tf_op jit(solution)/shard_map/all_to_all | solution.py:362
  418.1 14.9 %collective-permute-start.14 = (bf16[1,512,512]{2,1,0:T(8,128)(2,1)S(1)}, bf16[1,512,512]{2,1,0:T(8,128)(2,1)S(1)}, u32[]{:S(2)}, u32[]{:S(2)}) collective-permute-start(bf16[1,512,512]{2,1,0:T(8,128)(2,1)S(1)} %bitcast.310), channel_id=1, source_target_pairs={{0,2},{1,3},{2,0},{3,1},{4,6},{5,7},{6,4},{7,5},{8,10},{9,11},{10,... | collective-permute-start | bytes 1572872 | tf_op jit(solution)/shard_map/ppermute | solution.py:336
  431.8 12.2 %copy-start.16 = (bf16[8,64,512]{2,1,0:T(8,128)(2,1)}, bf16[8,64,512]{2,1,0:T(8,128)(2,1)S(1)}, u32[]{:S(2)}) copy-start(bf16[8,64,512]{2,1,0:T(8,128)(2,1)S(1)} %all-to-all-done.8) | copy-start | bytes 1572868
  431.8 12.2 %collective-permute-start.12 = (bf16[1,512,512]{2,1,0:T(8,128)(2,1)S(1)}, bf16[1,512,512]{2,1,0:T(8,128)(2,1)S(1)}, u32[]{:S(2)}, u32[]{:S(2)}) collective-permute-start(bf16[1,512,512]{2,1,0:T(8,128)(2,1)S(1)} %bitcast.312), channel_id=1, source_target_pairs={{0,2},{1,3},{2,0},{3,1},{4,6},{5,7},{6,4},{7,5},{8,10},{9,11},{10,... | collective-permute-start | bytes 1572872 | tf_op jit(solution)/shard_map/ppermute | solution.py:336
  432.9 0.8 copy-start.17
  435.9 10.3 %copy-start.13 = (bf16[256,4,128]{2,1,0:T(4,128)(2,1)S(1)}, bf16[256,4,128]{2,1,0:T(4,128)(2,1)}, u32[]{:S(2)}) copy-start(bf16[256,4,128]{2,1,0:T(4,128)(2,1)} %copy-done.12) | copy-start | bytes 786436
  435.9 12.5 %collective-permute-start.15 = (bf16[2,512,512]{2,1,0:T(8,128)(2,1)}, bf16[2,512,512]{2,1,0:T(8,128)(2,1)}, u32[]{:S(2)}, u32[]{:S(2)}) collective-permute-start(bf16[2,512,512]{2,1,0:T(8,128)(2,1)} %get-tuple-element.38), channel_id=1, source_target_pairs={{0,1},{1,0},{2,3},{3,2},{4,5},{5,4},{6,7},{7,6},{8,9},{9,8},{10,11... | collective-permute-start | bytes 3145736 | tf_op jit(solution)/shard_map/ppermute | solution.py:336
  446.2 3.6 collective-permute-start.13
  449.8 2.5 copy-start.9
  452.3 12.6 %copy-start.11 = (bf16[4096,512]{1,0:T(8,128)(2,1)S(1)}, bf16[4096,512]{1,0:T(8,128)(2,1)}, u32[]{:S(2)}) copy-start(bf16[4096,512]{1,0:T(8,128)(2,1)} %copy-done.10) | copy-start | bytes 12582916
  462.9 2.0 copy-start.2
  475.5 2.0 copy-start.3
  496.9 53.2 %all-to-all-start.11 = ((bf16[128,64,128]{2,1,0:T(8,128)(2,1)}), bf16[128,64,128]{2,1,0:T(8,128)(2,1)S(1)}, u32[]{:S(2)}, u32[]{:S(2)}) async-start(bf16[128,64,128]{2,1,0:T(8,128)(2,1)} %decode.3), calls=%async_computation.11 | async-start | bytes 4194304 | tf_op jit(solution)/shard_map/all_to_all | solution.py:423
  550.1 52.9 %all-to-all-start.10 = ((bf16[128,64,128]{2,1,0:T(8,128)(2,1)}), bf16[128,64,128]{2,1,0:T(8,128)(2,1)}, u32[]{:S(2)}, u32[]{:S(2)}) async-start(bf16[128,64,128]{2,1,0:T(8,128)(2,1)} %decode.2), calls=%async_computation.10 | async-start | bytes 4194304 | tf_op jit(solution)/shard_map/all_to_all | solution.py:423
  606.8 4.0 copy-start.1
